TPU v7x, 128 devices: a whole 4x4x4 slice. The times are simulated.
128 devices in a mesh: span: 16 (over y, x_hi, core), tok: 8 (over x_lo, z).
Axes of the slice: x: 4 (x_hi: 2, x_lo: 2; x = x_hi * 2 + x_lo), y: 4, z: 4, core: 2. Of those that a mesh axis runs over, the one named last changes fastest.
Arguments:
- queries: bfloat16 [16, 512, 3072], P('span', 'tok'), may hold values from -9 to 9
- keys: bfloat16 [16, 512, 3072], P('span', 'tok'), may hold values from -9 to 9
- values: bfloat16 [16, 512, 3072], P('span', 'tok'), may hold values from -6 to 6
- levels: int32 [16], P('span'), may hold values from 0 to 15
- retiring: int32 [1], replicated, may hold values from 0 to 15
- block_mask: int32 [16, 16], P('span'), may hold values 0 or 1
- gates: float32 [16, 3072], replicated, may hold values from 0.5 to 2
Outputs:
- attended: bfloat16 [16, 512, 3072], P('span', 'tok')
All inputs are finite; a program needn't handle non-finite values. No bound on the sum of `block_mask` on one device may be relied on, other than what follows from the above.
Results may differ from a plain program's by a relative error of at most 0.0085.
Values may be sent and summed in bfloat16 or wider, within the bound.
No kernel may reach another device: no remote copies, remote signals or barrier semaphores. Data moves between devices by JAX's collectives and lax.ppermute only.
A program may use at most 128 MiB of HBM per device.

v0:
```python
import functools

import jax
import jax.numpy as jnp
from jax import lax
from jax.experimental import pallas as pl
from jax.experimental.pallas import tpu as pltpu
from jax.sharding import PartitionSpec as P


HEAD_DIM = 128
SPANS = 16
ROWS = 64
GROUP = 8
HEADS_DEV = 3
WIDTH = HEADS_DEV * HEAD_DIM
RING = 4
SET = GROUP * ROWS
META = 32
PARTS = ((0, 1), (2,))
TILE = 2 * ROWS
TILES = 16
STEP = 4
SUB = 2
LOG2E = 1.4426950408889634


BOTH = ("span", "tok")
VMEM = pl.BlockSpec(memory_space=pltpu.VMEM)
SMEM = pl.BlockSpec(memory_space=pltpu.SMEM)


def device_at(x, y, z, core):
    return (y * 4 + (x // 2) * 2 + core) * 8 + (x % 2) * 4 + z


def moved(array, dx=0, dy=0, dz=0, core=0, swap=0):
    pairs = []
    for x in range(4):
        for y in range(4):
            for z in range(4):
                for c in range(2):
                    mx, mz = (dz, dx) if swap and c else (dx, dz)
                    there = device_at((x + mx) % 4, (y + dy) % 4, (z + mz) % 4, c ^ core)
                    pairs.append((device_at(x, y, z, c), there))
    return lax.ppermute(array, BOTH, pairs)


def call(kernel, shapes, specs, scratch=()):
    return pl.pallas_call(
        kernel,
        out_shape=shapes,
        in_specs=specs,
        out_specs=jax.tree.map(lambda unused: VMEM, shapes),
        scratch_shapes=scratch,
    )


def shape(rows, columns, dtype=jnp.bfloat16):
    return jax.ShapeDtypeStruct((rows, columns), dtype)


def pack_kernel(at_ref, q_ref, k_ref, v_ref, meta_ref, *out_refs):
    for j in range(GROUP):
        columns = pl.ds(pl.multiple_of(at_ref[j] * WIDTH, HEAD_DIM), WIDTH)
        for i, ref in enumerate((q_ref, k_ref, v_ref)):
            out_refs[j][i * ROWS : (i + 1) * ROWS, :] = ref[:, columns]
        out_refs[j][3 * ROWS :, :] = meta_ref[...]


def spread_kernel(*refs):
    in_refs, out_refs = refs[:GROUP], refs[GROUP:]
    for j in range(GROUP):
        ref = in_refs[j]
        for p, part in enumerate(PARTS):
            q_ref, kv_ref = out_refs[2 * p], out_refs[2 * p + 1]
            for i, h in enumerate(part):
                columns = slice(h * HEAD_DIM, (h + 1) * HEAD_DIM)
                q_ref[i * SET + j * ROWS : i * SET + (j + 1) * ROWS, :] = ref[0:ROWS, columns]
                for t in range(2):
                    base = (2 * i + t) * SET + j * ROWS
                    kv_ref[base : base + ROWS, :] = ref[(t + 1) * ROWS : (t + 2) * ROWS, columns]
        row = ref[3 * ROWS : 3 * ROWS + 16, 0:HEAD_DIM].astype(jnp.float32)
        out_refs[-1][j : j + 1, :] = row[0:1]


def together_in(count):
    return 2 if count == 1 else 1


def attend_kernel(count, table_ref, *refs):
    together = together_in(count)
    q_refs, kv_refs = refs[:RING], refs[RING : 2 * RING]
    out_refs = refs[2 * RING : 3 * RING]
    q_all, k_all, v_all, o_all, v_turned, score_ref, lse_ref, sems = refs[3 * RING :]
    factor = jnp.float32(HEAD_DIM ** (-0.5) * LOG2E)

    def rows_of(ref, h, i):
        return ref[h, i // 2, pl.ds(i % 2 * 2, 2)].reshape(TILE, HEAD_DIM)

    limits = TILES * TILES
    q_place = [table_ref[limits + TILES + d] for d in range(RING)]
    k_place = [table_ref[limits + TILES + RING + d] for d in range(RING)]
    copies = []
    for h in range(count):
        for d in range(RING):
            for n, (source, target, place) in enumerate(
                (
                    (q_refs[d].at[h], q_all, q_place[d]),
                    (kv_refs[d].at[h, 0], k_all, k_place[d]),
                    (kv_refs[d].at[h, 1], v_all, k_place[d]),
                )
            ):
                copy = pltpu.make_async_copy(
                    source, target.at[h, :, place], sems.at[(h * RING + d) * 3 + n]
                )
                copy.start()
                copies.append(copy)
    for copy in copies:
        copy.wait()
    for h in range(count):
        for i in range(TILES):
            rows = slice(i * TILE, (i + 1) * TILE)
            v_turned[h, :, rows] = rows_of(v_all, h, i).T

    chains = [(t, h) for t in range(together) for h in range(count)]

    def trips_of(first):
        seen = [table_ref[limits + first * together + t] for t in range(together)]
        return jnp.maximum((functools.reduce(jnp.maximum, seen) + STEP - 1) // STEP, 1)

    def fill(first, g):
        for c, (t, h) in enumerate(chains):
            pick = first * together + t
            at = pick * TILES + g * STEP
            rows = [rows_of(k_all, h, table_ref[at + u]) for u in range(STEP)]
            score_ref[c] = lax.dot_general(
                jnp.concatenate(rows, axis=0),
                rows_of(q_all, h, pick),
                (((1,), (1,)), ((), ())),
                preferred_element_type=jnp.float32,
            )

    def tiles(first, unused):
        picks = [first * together + t for t in range(together)]
        seen = [table_ref[limits + i] for i in picks]
        trips = trips_of(first)
        starts = [pl.multiple_of(i * TILE, TILE) for i in picks]

        def place(t, g, u):
            return table_ref[picks[t] * TILES + g * STEP + u]

        def step(g, carry):
            parts = [range(at, at + SUB) for at in range(0, STEP, SUB)]
            scores = [score_ref[c] for c in range(len(chains))]
            last = (g + 1 >= trips).astype(jnp.int32)
            fill(jnp.minimum(first + last, TILES // together - 1), (1 - last) * (g + 1))
            result = list(carry)
            for part in parts:
                for c, (t, h) in enumerate(chains):
                    top, total, acc = result[c]
                    score = scores[c][part[0] * TILE : (part[-1] + 1) * TILE]
                    blocks = []
                    for n, u in enumerate(part):
                        block = score[n * TILE : (n + 1) * TILE]
                        blocks.append(jnp.where(g * STEP + u < seen[t], block, -1e30))
                    largest = functools.reduce(jnp.maximum, blocks)
                    new_top = jnp.maximum(top, jnp.max(largest, axis=0, keepdims=True))
                    shrink = jnp.exp2((top - new_top) * factor)
                    weights = [jnp.exp2((block - new_top) * factor) for block in blocks]
                    added = functools.reduce(jnp.add, weights).reshape(TILE // 8, 8, TILE)
                    total = total * shrink + jnp.sum(added, axis=0)
                    weight = jnp.concatenate([w.astype(jnp.bfloat16) for w in weights], axis=0)
                    ats = [pl.multiple_of(place(t, g, u) * TILE, TILE) for u in part]
                    columns = [v_turned[h, :, pl.ds(at, TILE)] for at in ats]
                    acc = acc * shrink + jnp.dot(
                        jnp.concatenate(columns, axis=1),
                        weight,
                        preferred_element_type=jnp.float32,
                    )
                    result[c] = (new_top, total, acc)
            return result

        empty = (
            jnp.full((1, TILE), -1e30, jnp.float32),
            jnp.zeros((8, TILE), jnp.float32),
            jnp.zeros((HEAD_DIM, TILE), jnp.float32),
        )
        final = lax.fori_loop(0, trips, step, [empty] * len(chains))
        for (t, h), (top, total, acc) in zip(chains, final):
            total = jnp.sum(total, axis=0, keepdims=True)
            total = jnp.where(total > 0.0, total, 1.0)
            o_all[h, pl.ds(starts[t], TILE), :] = (acc * (1.0 / total)).T.astype(jnp.bfloat16)
            lse_ref[h, picks[t] % 2, pl.ds(picks[t] // 2, 1), :] = top * factor + jnp.log2(total)
        return unused

    fill(0, 0)
    lax.fori_loop(0, TILES // together, tiles, 0)
    for h in range(count):
        for d in range(RING):
            base = h * (SET + META)
            for j in range(GROUP):
                at = pl.multiple_of(j * RING * ROWS + q_place[d] * ROWS, ROWS)
                out_refs[d][base + j * ROWS : base + (j + 1) * ROWS, :] = o_all[
                    h, pl.ds(at, ROWS), :
                ]
            value = lse_ref[h, q_place[d] // 2]
            high = value.astype(jnp.bfloat16).astype(jnp.float32)
            middle = (value - high).astype(jnp.bfloat16).astype(jnp.float32)
            low = value - high - middle
            out_refs[d][base + SET : base + SET + META, :] = jnp.concatenate(
                [high, middle, low, jnp.zeros_like(low)], axis=0
            ).astype(jnp.bfloat16)


def attend(count, table, q, kv):
    q = [piece.reshape(count, GROUP, ROWS, HEAD_DIM) for piece in q]
    kv = [piece.reshape(count, 2, GROUP, ROWS, HEAD_DIM) for piece in kv]
    pieces = pltpu.VMEM((count, GROUP, RING, ROWS, HEAD_DIM), jnp.bfloat16)
    return call(
        functools.partial(attend_kernel, count),
        [shape(count * (SET + META), HEAD_DIM)] * RING,
        [SMEM] + [pl.BlockSpec(memory_space=pl.ANY)] * (2 * RING),
        [pieces] * 3
        + [
            pltpu.VMEM((count, RING * SET, HEAD_DIM), jnp.bfloat16),
            pltpu.VMEM((count, HEAD_DIM, RING * SET), jnp.bfloat16),
            pltpu.VMEM((count * together_in(count), STEP * TILE, TILE), jnp.float32),
            pltpu.VMEM((count, 2, GROUP, HEAD_DIM), jnp.float32),
            pltpu.SemaphoreType.DMA((count * RING * 3,)),
        ],
    )(table, *q, *kv)


def combine_kernel(table_ref, *refs):
    out_refs = refs[-GROUP:]
    shift = table_ref[TILES * TILES + TILES] % 2 * ROWS
    lanes = lax.broadcasted_iota(jnp.int32, (ROWS, HEAD_DIM), 1)
    eye = lanes == lax.broadcasted_iota(jnp.int32, (ROWS, HEAD_DIM), 0) + shift
    for p, part in enumerate(PARTS):
        pieces = refs[p * RING : (p + 1) * RING]
        for i, h in enumerate(part):
            base = i * (SET + META)
            lse = []
            for ref in pieces:
                coded = ref[base + SET : base + SET + META, :].astype(jnp.float32)
                lse.append(coded[0:8] + coded[8:16] + coded[16:24])
            top = functools.reduce(jnp.maximum, lse)
            shares = [jnp.exp2(value - top) for value in lse]
            total = functools.reduce(jnp.add, shares)
            shares = [value / total for value in shares]
            for j in range(GROUP):
                mixed = jnp.zeros((ROWS, HEAD_DIM), jnp.float32)
                for ref, share in zip(pieces, shares):
                    column = jnp.sum(jnp.where(eye, share[j : j + 1], 0.0), axis=1, keepdims=True)
                    rows = ref[base + j * ROWS : base + (j + 1) * ROWS, :]
                    mixed = mixed + column * rows.astype(jnp.float32)
                out_refs[j][:, h * HEAD_DIM : (h + 1) * HEAD_DIM] = mixed.astype(jnp.bfloat16)


def finish_kernel(at_ref, level_ref, gates_ref, *refs):
    out_ref = refs[-1]
    for j in range(GROUP):
        columns = pl.ds(pl.multiple_of(at_ref[j] * WIDTH, HEAD_DIM), WIDTH)
        gate = gates_ref[pl.ds(level_ref[0], 1), columns]
        out_ref[:, columns] = (refs[j][...].astype(jnp.float32) * gate).astype(jnp.bfloat16)


def see_table(q_slots, k_slots, retiring, mask, places):
    names = jnp.arange(TILES, dtype=jnp.int32)
    q_order = (q_slots - retiring[0]) % SPANS
    k_order = (k_slots - retiring[0]) % SPANS
    slots = jnp.arange(SPANS, dtype=jnp.int32)
    picked = (k_slots[:, None] == slots[None, :]).astype(jnp.float32)
    masked = jnp.sum(mask[:, None, :SPANS] * picked[None], axis=-1) > 0.5
    older = k_order[None, :] < q_order[:, None]
    same = k_slots[None, :] == q_slots[:, None]
    sees = same | masked & older
    before = names[None, :] < names[:, None]
    rank = jnp.sum((sees[:, None, :] & before[None]).astype(jnp.int32), axis=-1)
    chosen = sees[:, None, :] & (rank[:, None, :] == names[None, :, None])
    listed = jnp.sum(jnp.where(chosen, names[None, None, :], 0), axis=-1)
    counts = jnp.sum(sees.astype(jnp.int32), axis=-1)
    return jnp.concatenate([listed.reshape(-1), counts, places])


def local(queries, keys, values, levels, retiring, block_mask, gates):
    span = lax.axis_index("span").astype(jnp.int32)
    token = lax.axis_index("tok").astype(jnp.int32)
    y, half, core = span // 4, span // 2 % 2, span % 2
    x, z = half * 2 + token // RING, token % RING
    hop = jnp.arange(GROUP, dtype=jnp.int32)
    target = (y + hop // 2) % 4 * 2 + (core ^ hop % 2)
    hops = [dict(dy=j // 2, core=j % 2) for j in range(GROUP)]
    backs = [dict(dy=-(j // 2), core=j % 2) for j in range(GROUP)]

    meta = jnp.pad(block_mask.astype(jnp.bfloat16), ((0, 15), (0, WIDTH - SPANS)))
    packed = call(
        pack_kernel,
        [shape(3 * ROWS + 16, WIDTH)] * GROUP,
        [SMEM, VMEM, VMEM, VMEM, VMEM],
    )(target, queries[0], keys[0], values[0], meta)
    shared = [packed[0]] + [moved(packed[j], **hops[j]) for j in range(1, GROUP)]

    shapes = []
    for part in PARTS:
        shapes += [shape(len(part) * SET, HEAD_DIM), shape(len(part) * 2 * SET, HEAD_DIM)]
    spread = call(
        spread_kernel, shapes + [shape(GROUP, HEAD_DIM, jnp.float32)], [VMEM] * GROUP
    )(*shared)

    tile = jnp.arange(TILES, dtype=jnp.int32)
    base = (y - tile // 4) % 4 * 4 + (core ^ tile // 2 % 2)
    wide_slots, near_slots = base + 2 * (tile % 2), base + 2 * half
    near_mask = jnp.repeat(spread[-1], 2, axis=0)
    far_mask = jnp.repeat(moved(spread[-1], dx=2), 2, axis=0)
    wide_mask = jnp.where((tile % 2 == half)[:, None], near_mask, far_mask)
    first = core == 0
    ring = jnp.arange(RING, dtype=jnp.int32)
    table = see_table(
        jnp.where(first, wide_slots, near_slots),
        jnp.where(first, near_slots, wide_slots),
        retiring,
        jnp.where(first, wide_mask, near_mask),
        jnp.concatenate(
            [(jnp.where(first, x, z) - ring) % RING, (jnp.where(first, z, x) - ring) % RING]
        ),
    )

    pieces = []
    for p, part in enumerate(PARTS):
        own_q, own_kv = spread[2 * p], spread[2 * p + 1]
        if p > 0:
            own_q, own_kv, table = lax.optimization_barrier((own_q, own_kv, table))
        q, kv = [own_q], [own_kv]
        for d in range(1, RING):
            kv.append(moved(own_kv, dz=d, swap=1))
        for d in range(1, RING):
            q.append(moved(own_q, dx=d, swap=1))
        parts = attend(len(part), table, q, kv)
        pieces.append(parts[0])
        for d in range(1, RING):
            pieces.append(moved(parts[d], dx=-d, swap=1))

    mixed = call(
        combine_kernel, [shape(ROWS, WIDTH)] * GROUP, [SMEM] + [VMEM] * len(pieces)
    )(table, *pieces)
    returned = [mixed[0]] + [moved(mixed[j], **backs[j]) for j in range(1, GROUP)]
    result = call(finish_kernel, shape(ROWS, GROUP * WIDTH), [SMEM, SMEM] + [VMEM] * (GROUP + 1))(
        target, levels, gates, *returned
    )
    return result[None]


def solution(mesh):
    return jax.shard_map(
        local,
        mesh=mesh,
        in_specs=(
            P("span", "tok", None),
            P("span", "tok", None),
            P("span", "tok", None),
            P("span"),
            P(),
            P("span", None),
            P(),
        ),
        out_specs=P("span", "tok", None),
        check_vma=False,
    )
```

profile of v0, /device:TPU:33, one launch (start us, length us, event | category | flops | bytes accessed | tf_op | source)
XLA Modules:
  0.0 132.3 jit_solution(15900515895141059410)
XLA Ops:
  1.9 2.4 %shard_map.73 = (bf16[208,384]{1,0:T(8,128)(2,1)}, bf16[208,384]{1,0:T(8,128)(2,1)}, bf16[208,384]{1,0:T(8,128)(2,1)}, bf16[208,384]{1,0:T(8,128)(2,1)}, bf16[20...) custom-call(s32[8]{0:T(128)} %fusion.3.at_ref, ...), custom_call_target="tpu_custom_call" | custom-call | tf_op jit(solution)/shard_map/pallas_call | solution.py:298
  6.2 1.5 %collective-permute-start.2 = (bf16[208,384]{1,0:T(8,128)(2,1)}, bf16[208,384]{1,0:T(8,128)(2,1)S(1)}, u32[]{:S(2)}, u32[]{:S(2)}) collective-permute-start(bf16[208,384]{1,0:T(8,128)(2,1)} %get-tuple-element.40), channel_id=1, source_target_pairs={{0,40},{8,32},{1,41},{9,33},{2,42},{10,34},{3,43},{11,35},{32,72},... | collective-permute-start | bytes 479240 | tf_op jit(solution)/shard_map/ppermute | solution.py:46
  9.0 2.0 %collective-permute-start.4 = (bf16[208,384]{1,0:T(8,128)(2,1)}, bf16[208,384]{1,0:T(8,128)(2,1)S(1)}, u32[]{:S(2)}, u32[]{:S(2)}) collective-permute-start(bf16[208,384]{1,0:T(8,128)(2,1)} %get-tuple-element.42), channel_id=1, source_target_pairs={{0,72},{8,64},{1,73},{9,65},{2,74},{10,66},{3,75},{11,67},{32,104}... | collective-permute-start | bytes 479240 | tf_op jit(solution)/shard_map/ppermute | solution.py:46
  11.8 1.4 %collective-permute-start.5 = (bf16[208,384]{1,0:T(8,128)(2,1)}, bf16[208,384]{1,0:T(8,128)(2,1)S(1)}, u32[]{:S(2)}, u32[]{:S(2)}) collective-permute-start(bf16[208,384]{1,0:T(8,128)(2,1)} %get-tuple-element.43), channel_id=1, source_target_pairs={{0,96},{8,104},{1,97},{9,105},{2,98},{10,106},{3,99},{11,107},{32,... | collective-permute-start | bytes 479240 | tf_op jit(solution)/shard_map/ppermute | solution.py:46
  13.3 1.5 %collective-permute-start.6 = (bf16[208,384]{1,0:T(8,128)(2,1)}, bf16[208,384]{1,0:T(8,128)(2,1)S(1)}, u32[]{:S(2)}, u32[]{:S(2)}) collective-permute-start(bf16[208,384]{1,0:T(8,128)(2,1)} %get-tuple-element.44), channel_id=1, source_target_pairs={{0,104},{8,96},{1,105},{9,97},{2,106},{10,98},{3,107},{11,99},{32,... | collective-permute-start | bytes 479240 | tf_op jit(solution)/shard_map/ppermute | solution.py:46
  15.7 4.4 %collective-permute-done.3.refs_4_ = bf16[208,384]{1,0:T(8,128)(2,1)S(1)} collective-permute-done((bf16[208,384]{1,0:T(8,128)(2,1)}, bf16[208,384]{1,0:T(8,128)(2,1)S(1)}, u32[]{:S(2)}, u32[]{:S(2)}) %collective-permute-start.3) | collective-permute-done | bytes 159776 | tf_op jit(solution)/shard_map/ppermute | solution.py:46
  20.1 3.6 %collective-permute-done.4.refs_5_ = bf16[208,384]{1,0:T(8,128)(2,1)S(1)} collective-permute-done((bf16[208,384]{1,0:T(8,128)(2,1)}, bf16[208,384]{1,0:T(8,128)(2,1)S(1)}, u32[]{:S(2)}, u32[]{:S(2)}) %collective-permute-start.4) | collective-permute-done | bytes 159776 | tf_op jit(solution)/shard_map/ppermute | solution.py:46
  25.3 2.6 %shard_map.74 = (bf16[1024,128]{1,0:T(8,128)(2,1)}, bf16[2048,128]{1,0:T(8,128)(2,1)}, bf16[512,128]{1,0:T(8,128)(2,1)}, bf16[1024,128]{1,0:T(8,128)(2,1)}, f32[8,128]{1,0:T(8,128)}) custom-call(bf16[208,384]{1,0:T(8,128)(2,1)} %get-tuple-element.37.refs_0_, bf16[208,384]{1,0:T(8,128)(2,1)} %copy-done.12, bf16[208,384]{1,0:T(8,128)(2,1)} %copy-done.13, ...), custom_call_target="tpu_custom_call" | custom-call | tf_op jit(solution)/shard_map/pallas_call | solution.py:308
  27.8 2.8 %collective-permute-start.7 = (f32[8,128]{1,0:T(8,128)}, f32[8,128]{1,0:T(8,128)S(1)}, u32[]{:S(2)}, u32[]{:S(2)}) collective-permute-start(f32[8,128]{1,0:T(8,128)} %get-tuple-element.47), channel_id=1, source_target_pairs={{0,16},{8,24},{1,17},{9,25},{2,18},{10,26},{3,19},{11,27},{32,48},... | collective-permute-start | bytes 12296 | tf_op jit(solution)/shard_map/ppermute | solution.py:46
  30.7 1.6 %collective-permute-start.8 = (bf16[1024,128]{1,0:T(8,128)(2,1)}, bf16[1024,128]{1,0:T(8,128)(2,1)S(1)}, u32[]{:S(2)}, u32[]{:S(2)}) collective-permute-start(bf16[1024,128]{1,0:T(8,128)(2,1)} %get-tuple-element.49), channel_id=1, source_target_pairs={{0,4},{8,9},{1,5},{9,10},{2,6},{10,11},{3,7},{11,8},{32,36},{40,41... | collective-permute-start | bytes 786440 | tf_op jit(solution)/shard_map/ppermute | solution.py:46
  35.8 1.6 %collective-permute-start.17 = (bf16[512,128]{1,0:T(8,128)(2,1)S(1)}, bf16[512,128]{1,0:T(8,128)(2,1)S(1)}, u32[]{:S(2)}, u32[]{:S(2)}) collective-permute-start(bf16[512,128]{1,0:T(8,128)(2,1)S(1)} %copy-done.22), channel_id=1, source_target_pairs={{0,4},{8,9},{1,5},{9,10},{2,6},{10,11},{3,7},{11,8},{32,36},{40,41... | collective-permute-start | bytes 393224 | tf_op jit(solution)/shard_map/ppermute | solution.py:46
  38.5 2.1 %collective-permute-start.19 = (bf16[512,128]{1,0:T(8,128)(2,1)S(1)}, bf16[512,128]{1,0:T(8,128)(2,1)S(1)}, u32[]{:S(2)}, u32[]{:S(2)}) collective-permute-start(bf16[512,128]{1,0:T(8,128)(2,1)S(1)} %copy-done.22), channel_id=1, source_target_pairs={{0,20},{8,11},{1,21},{9,8},{2,22},{10,9},{3,23},{11,10},{32,52},{4... | collective-permute-start | bytes 393224 | tf_op jit(solution)/shard_map/ppermute | solution.py:46
  40.7 2.4 %collective-permute-start.21 = (bf16[1024,128]{1,0:T(8,128)(2,1)}, bf16[1024,128]{1,0:T(8,128)(2,1)S(1)}, u32[]{:S(2)}, u32[]{:S(2)}) collective-permute-start(bf16[1024,128]{1,0:T(8,128)(2,1)} %get-tuple-element.56), channel_id=1, source_target_pairs={{0,2},{8,24},{1,3},{9,25},{2,0},{10,26},{3,1},{11,27},{32,34},{40,... | collective-permute-start | bytes 786440 | tf_op jit(solution)/shard_map/ppermute | solution.py:46
  44.2 1.6 %collective-permute-start.22 = (bf16[1024,128]{1,0:T(8,128)(2,1)}, bf16[1024,128]{1,0:T(8,128)(2,1)S(1)}, u32[]{:S(2)}, u32[]{:S(2)}) collective-permute-start(bf16[1024,128]{1,0:T(8,128)(2,1)} %get-tuple-element.56), channel_id=1, source_target_pairs={{0,3},{8,28},{1,0},{9,29},{2,1},{10,30},{3,2},{11,31},{32,35},{40,... | collective-permute-start | bytes 786440 | tf_op jit(solution)/shard_map/ppermute | solution.py:46
  48.5 2.1 %collective-permute-start.9 = (bf16[1024,128]{1,0:T(8,128)(2,1)}, bf16[1024,128]{1,0:T(8,128)(2,1)S(1)}, u32[]{:S(2)}, u32[]{:S(2)}) collective-permute-start(bf16[1024,128]{1,0:T(8,128)(2,1)} %get-tuple-element.49), channel_id=1, source_target_pairs={{0,16},{8,10},{1,17},{9,11},{2,18},{10,8},{3,19},{11,9},{32,48},{4... | collective-permute-start | bytes 786440 | tf_op jit(solution)/shard_map/ppermute | solution.py:46
  51.4 2.3 %collective-permute-start.10 = (bf16[1024,128]{1,0:T(8,128)(2,1)}, bf16[1024,128]{1,0:T(8,128)(2,1)S(1)}, u32[]{:S(2)}, u32[]{:S(2)}) collective-permute-start(bf16[1024,128]{1,0:T(8,128)(2,1)} %get-tuple-element.49), channel_id=1, source_target_pairs={{0,20},{8,11},{1,21},{9,8},{2,22},{10,9},{3,23},{11,10},{32,52},{4... | collective-permute-start | bytes 786440 | tf_op jit(solution)/shard_map/ppermute | solution.py:46
  53.7 10.2 %shard_map.76 = (bf16[544,128]{1,0:T(8,128)(2,1)}, bf16[544,128]{1,0:T(8,128)(2,1)}, bf16[544,128]{1,0:T(8,128)(2,1)}, bf16[544,128]{1,0:T(8,128)(2,1)}) custom-call(s32[280]{0:T(512)} %pad_add_fusion.table_ref, bf16[1,8,64,128]{3,2,1,0:T(8,128)(2,1)} %bitcast.39, bf16[1,8,64,128]{3,2,1,0:T(8,128)(2,1)} %bitcast.40, bf16[1,8,64,128]{3,2,1,0:T(8,128)(2,1)} %bitcast.41, ...), custom_call_target="tpu_custom_call" | custom-call | tf_op jit(solution)/shard_map/pallas_call | solution.py:220
  64.7 3.1 %collective-permute-done.10 = bf16[1024,128]{1,0:T(8,128)(2,1)S(1)} collective-permute-done((bf16[1024,128]{1,0:T(8,128)(2,1)}, bf16[1024,128]{1,0:T(8,128)(2,1)S(1)}, u32[]{:S(2)}, u32[]{:S(2)}) %collective-permute-start.10) | collective-permute-done | bytes 262176 | tf_op jit(solution)/shard_map/ppermute | solution.py:46
  69.0 18.2 %shard_map.75 = (bf16[1088,128]{1,0:T(8,128)(2,1)}, bf16[1088,128]{1,0:T(8,128)(2,1)}, bf16[1088,128]{1,0:T(8,128)(2,1)}, bf16[1088,128]{1,0:T(8,128)(2,1)}) custom-call(s32[280]{0:T(512)} %pad_add_fusion.table_ref, bf16[2,8,64,128]{3,2,1,0:T(8,128)(2,1)} %bitcast.35, bf16[2,8,64,128]{3,2,1,0:T(8,128)(2,1)} %bitcast.36, bf16[2,8,64,128]{3,2,1,0:T(8,128)(2,1)} %bitcast.37, ...), custom_call_target="tpu_custom_call" | custom-call | tf_op jit(solution)/shard_map/pallas_call | solution.py:220
  87.2 2.4 %collective-permute-start.14 = (bf16[1088,128]{1,0:T(8,128)(2,1)}, bf16[1088,128]{1,0:T(8,128)(2,1)S(1)}, u32[]{:S(2)}, u32[]{:S(2)}) collective-permute-start(bf16[1088,128]{1,0:T(8,128)(2,1)} %get-tuple-element.52), channel_id=1, source_target_pairs={{0,20},{8,11},{1,21},{9,8},{2,22},{10,9},{3,23},{11,10},{32,52},{4... | collective-permute-start | bytes 835592 | tf_op jit(solution)/shard_map/ppermute | solution.py:46
  89.9 1.8 %collective-permute-start.16 = (bf16[1088,128]{1,0:T(8,128)(2,1)}, bf16[1088,128]{1,0:T(8,128)(2,1)S(1)}, u32[]{:S(2)}, u32[]{:S(2)}) collective-permute-start(bf16[1088,128]{1,0:T(8,128)(2,1)} %get-tuple-element.54), channel_id=1, source_target_pairs={{0,4},{8,9},{1,5},{9,10},{2,6},{10,11},{3,7},{11,8},{32,36},{40,41... | collective-permute-start | bytes 835592 | tf_op jit(solution)/shard_map/ppermute | solution.py:46
  93.2 5.3 %collective-permute-done.24.refs_6_ = bf16[544,128]{1,0:T(8,128)(2,1)S(1)} collective-permute-done((bf16[544,128]{1,0:T(8,128)(2,1)S(1)}, bf16[544,128]{1,0:T(8,128)(2,1)S(1)}, u32[]{:S(2)}, u32[]{:S(2)}) %collective-permute-start.24) | collective-permute-done | bytes 139296 | tf_op jit(solution)/shard_map/ppermute | solution.py:46
  98.5 2.2 %collective-permute-done.25.refs_7_ = bf16[544,128]{1,0:T(8,128)(2,1)S(1)} collective-permute-done((bf16[544,128]{1,0:T(8,128)(2,1)S(1)}, bf16[544,128]{1,0:T(8,128)(2,1)S(1)}, u32[]{:S(2)}, u32[]{:S(2)}) %collective-permute-start.25) | collective-permute-done | bytes 139296 | tf_op jit(solution)/shard_map/ppermute | solution.py:46
  101.7 2.9 %shard_map.77 = (bf16[64,384]{1,0:T(8,128)(2,1)}, bf16[64,384]{1,0:T(8,128)(2,1)}, bf16[64,384]{1,0:T(8,128)(2,1)}, bf16[64,384]{1,0:T(8,128)(2,1)}, bf16[64,384...) custom-call(s32[280]{0:T(512)} %pad_add_fusion.table_ref, ...), custom_call_target="tpu_custom_call" | custom-call | tf_op jit(solution)/shard_map/pallas_call | solution.py:345
  104.7 11.3 %collective-permute-start.26 = (bf16[64,384]{1,0:T(8,128)(2,1)}, bf16[64,384]{1,0:T(8,128)(2,1)S(1)}, u32[]{:S(2)}, u32[]{:S(2)}) collective-permute-start(bf16[64,384]{1,0:T(8,128)(2,1)} %get-tuple-element.62), channel_id=1, source_target_pairs={{0,8},{8,0},{1,9},{9,1},{2,10},{10,2},{3,11},{11,3},{32,40},{40,32... | collective-permute-start | bytes 147464 | tf_op jit(solution)/shard_map/ppermute | solution.py:46
  116.0 3.7 %collective-permute-start.27 = (bf16[64,384]{1,0:T(8,128)(2,1)}, bf16[64,384]{1,0:T(8,128)(2,1)S(1)}, u32[]{:S(2)}, u32[]{:S(2)}) collective-permute-start(bf16[64,384]{1,0:T(8,128)(2,1)} %get-tuple-element.63), channel_id=1, source_target_pairs={{0,96},{8,104},{1,97},{9,105},{2,98},{10,106},{3,99},{11,107},{32,... | collective-permute-start | bytes 147464 | tf_op jit(solution)/shard_map/ppermute | solution.py:46
  119.7 1.4 %collective-permute-start.29 = (bf16[64,384]{1,0:T(8,128)(2,1)}, bf16[64,384]{1,0:T(8,128)(2,1)S(1)}, u32[]{:S(2)}, u32[]{:S(2)}) collective-permute-start(bf16[64,384]{1,0:T(8,128)(2,1)} %get-tuple-element.65), channel_id=1, source_target_pairs={{0,64},{8,72},{1,65},{9,73},{2,66},{10,74},{3,67},{11,75},{32,96},... | collective-permute-start | bytes 147464 | tf_op jit(solution)/shard_map/ppermute | solution.py:46
  121.1 2.1 %collective-permute-start.30 = (bf16[64,384]{1,0:T(8,128)(2,1)}, bf16[64,384]{1,0:T(8,128)(2,1)S(1)}, u32[]{:S(2)}, u32[]{:S(2)}) collective-permute-start(bf16[64,384]{1,0:T(8,128)(2,1)} %get-tuple-element.66), channel_id=1, source_target_pairs={{0,72},{8,64},{1,73},{9,65},{2,74},{10,66},{3,75},{11,67},{32,104}... | collective-permute-start | bytes 147464 | tf_op jit(solution)/shard_map/ppermute | solution.py:46
  123.2 1.5 %collective-permute-start.31 = (bf16[64,384]{1,0:T(8,128)(2,1)}, bf16[64,384]{1,0:T(8,128)(2,1)S(1)}, u32[]{:S(2)}, u32[]{:S(2)}) collective-permute-start(bf16[64,384]{1,0:T(8,128)(2,1)} %get-tuple-element.67), channel_id=1, source_target_pairs={{0,32},{8,40},{1,33},{9,41},{2,34},{10,42},{3,35},{11,43},{32,64},... | collective-permute-start | bytes 147464 | tf_op jit(solution)/shard_map/ppermute | solution.py:46
  125.4 1.6 %collective-permute-done.30.refs_5_ = bf16[64,384]{1,0:T(8,128)(2,1)S(1)} collective-permute-done((bf16[64,384]{1,0:T(8,128)(2,1)}, bf16[64,384]{1,0:T(8,128)(2,1)S(1)}, u32[]{:S(2)}, u32[]{:S(2)}) %collective-permute-start.30) | collective-permute-done | bytes 49184 | tf_op jit(solution)/shard_map/ppermute | solution.py:46
  128.1 1.7 %collective-permute-done.32.refs_7_ = bf16[64,384]{1,0:T(8,128)(2,1)S(1)} collective-permute-done((bf16[64,384]{1,0:T(8,128)(2,1)}, bf16[64,384]{1,0:T(8,128)(2,1)S(1)}, u32[]{:S(2)}, u32[]{:S(2)}) %collective-permute-start.32) | collective-permute-done | bytes 49184 | tf_op jit(solution)/shard_map/ppermute | solution.py:46
  130.4 1.9 %shard_map.78 = bf16[64,3072]{1,0:T(8,128)(2,1)} custom-call(s32[8]{0:T(128)} %fusion.3.at_ref, s32[1]{0:T(128)S(6)} %copy.8.level_ref, f32[16,3072]{1,0:T(8,128)} %gates_ref.1, bf16[64,384]{1,0:T(8,128)(2,1)} %get-tuple-element.61.refs_0_, bf16[64,384]{1,0:T(8,128)(2,1)} %copy-done.26, bf16[64,384]{1,0:T(8,128)(2,1)} %copy-done.27, ...), custom_call_target="tpu_custom_call" | custom-call | tf_op jit(solution)/shard_map/pallas_call | solution.py:349
  (129 shorter events, 23.3 us)
Async XLA Ops:
  4.3 7.6 %collective-permute-start = (bf16[208,384]{1,0:T(8,128)(2,1)}, bf16[208,384]{1,0:T(8,128)(2,1)S(1)}, u32[]{:S(2)}, u32[]{:S(2)}) collective-permute-start(bf16[208,384]{1,0:T(8,128)(2,1)} %get-tuple-element.38), channel_id=1, source_target_pairs={{0,8},{8,0},{1,9},{9,1},{2,10},{10,2},{3,11},{11,3},{32,40},{40,32... | collective-permute-start | bytes 479240 | tf_op jit(solution)/shard_map/ppermute | solution.py:46
  4.9 8.3 %collective-permute-start.1 = (bf16[208,384]{1,0:T(8,128)(2,1)}, bf16[208,384]{1,0:T(8,128)(2,1)S(1)}, u32[]{:S(2)}, u32[]{:S(2)}) collective-permute-start(bf16[208,384]{1,0:T(8,128)(2,1)} %get-tuple-element.39), channel_id=1, source_target_pairs={{0,32},{8,40},{1,33},{9,41},{2,34},{10,42},{3,35},{11,43},{32,64},... | collective-permute-start | bytes 479240 | tf_op jit(solution)/shard_map/ppermute | solution.py:46
  6.2 9.4 %collective-permute-start.2 = (bf16[208,384]{1,0:T(8,128)(2,1)}, bf16[208,384]{1,0:T(8,128)(2,1)S(1)}, u32[]{:S(2)}, u32[]{:S(2)}) collective-permute-start(bf16[208,384]{1,0:T(8,128)(2,1)} %get-tuple-element.40), channel_id=1, source_target_pairs={{0,40},{8,32},{1,41},{9,33},{2,42},{10,34},{3,43},{11,35},{32,72},... | collective-permute-start | bytes 479240 | tf_op jit(solution)/shard_map/ppermute | solution.py:46
  7.7 12.3 %collective-permute-start.3 = (bf16[208,384]{1,0:T(8,128)(2,1)}, bf16[208,384]{1,0:T(8,128)(2,1)S(1)}, u32[]{:S(2)}, u32[]{:S(2)}) collective-permute-start(bf16[208,384]{1,0:T(8,128)(2,1)} %get-tuple-element.41), channel_id=1, source_target_pairs={{0,64},{8,72},{1,65},{9,73},{2,66},{10,74},{3,67},{11,75},{32,96},... | collective-permute-start | bytes 479240 | tf_op jit(solution)/shard_map/ppermute | solution.py:46
  9.0 14.7 %collective-permute-start.4 = (bf16[208,384]{1,0:T(8,128)(2,1)}, bf16[208,384]{1,0:T(8,128)(2,1)S(1)}, u32[]{:S(2)}, u32[]{:S(2)}) collective-permute-start(bf16[208,384]{1,0:T(8,128)(2,1)} %get-tuple-element.42), channel_id=1, source_target_pairs={{0,72},{8,64},{1,73},{9,65},{2,74},{10,66},{3,75},{11,67},{32,104}... | collective-permute-start | bytes 479240 | tf_op jit(solution)/shard_map/ppermute | solution.py:46
  11.8 11.9 %collective-permute-start.5 = (bf16[208,384]{1,0:T(8,128)(2,1)}, bf16[208,384]{1,0:T(8,128)(2,1)S(1)}, u32[]{:S(2)}, u32[]{:S(2)}) collective-permute-start(bf16[208,384]{1,0:T(8,128)(2,1)} %get-tuple-element.43), channel_id=1, source_target_pairs={{0,96},{8,104},{1,97},{9,105},{2,98},{10,106},{3,99},{11,107},{32,... | collective-permute-start | bytes 479240 | tf_op jit(solution)/shard_map/ppermute | solution.py:46
  13.3 11.3 %collective-permute-start.6 = (bf16[208,384]{1,0:T(8,128)(2,1)}, bf16[208,384]{1,0:T(8,128)(2,1)S(1)}, u32[]{:S(2)}, u32[]{:S(2)}) collective-permute-start(bf16[208,384]{1,0:T(8,128)(2,1)} %get-tuple-element.44), channel_id=1, source_target_pairs={{0,104},{8,96},{1,105},{9,97},{2,106},{10,98},{3,107},{11,99},{32,... | collective-permute-start | bytes 479240 | tf_op jit(solution)/shard_map/ppermute | solution.py:46
  30.7 15.2 %collective-permute-start.8 = (bf16[1024,128]{1,0:T(8,128)(2,1)}, bf16[1024,128]{1,0:T(8,128)(2,1)S(1)}, u32[]{:S(2)}, u32[]{:S(2)}) collective-permute-start(bf16[1024,128]{1,0:T(8,128)(2,1)} %get-tuple-element.49), channel_id=1, source_target_pairs={{0,4},{8,9},{1,5},{9,10},{2,6},{10,11},{3,7},{11,8},{32,36},{40,41... | collective-permute-start | bytes 786440 | tf_op jit(solution)/shard_map/ppermute | solution.py:46
  34.8 12.3 %collective-permute-start.20 = (bf16[1024,128]{1,0:T(8,128)(2,1)}, bf16[1024,128]{1,0:T(8,128)(2,1)S(1)}, u32[]{:S(2)}, u32[]{:S(2)}) collective-permute-start(bf16[1024,128]{1,0:T(8,128)(2,1)} %get-tuple-element.56), channel_id=1, source_target_pairs={{0,1},{8,12},{1,2},{9,13},{2,3},{10,14},{3,0},{11,15},{32,33},{40,... | collective-permute-start | bytes 786440 | tf_op jit(solution)/shard_map/ppermute | solution.py:46
  35.8 4.9 %collective-permute-start.17 = (bf16[512,128]{1,0:T(8,128)(2,1)S(1)}, bf16[512,128]{1,0:T(8,128)(2,1)S(1)}, u32[]{:S(2)}, u32[]{:S(2)}) collective-permute-start(bf16[512,128]{1,0:T(8,128)(2,1)S(1)} %copy-done.22), channel_id=1, source_target_pairs={{0,4},{8,9},{1,5},{9,10},{2,6},{10,11},{3,7},{11,8},{32,36},{40,41... | collective-permute-start | bytes 393224 | tf_op jit(solution)/shard_map/ppermute | solution.py:46
  37.5 5.7 %collective-permute-start.18 = (bf16[512,128]{1,0:T(8,128)(2,1)S(1)}, bf16[512,128]{1,0:T(8,128)(2,1)S(1)}, u32[]{:S(2)}, u32[]{:S(2)}) collective-permute-start(bf16[512,128]{1,0:T(8,128)(2,1)S(1)} %copy-done.22), channel_id=1, source_target_pairs={{0,16},{8,10},{1,17},{9,11},{2,18},{10,8},{3,19},{11,9},{32,48},{4... | collective-permute-start | bytes 393224 | tf_op jit(solution)/shard_map/ppermute | solution.py:46
  38.5 5.7 %collective-permute-start.19 = (bf16[512,128]{1,0:T(8,128)(2,1)S(1)}, bf16[512,128]{1,0:T(8,128)(2,1)S(1)}, u32[]{:S(2)}, u32[]{:S(2)}) collective-permute-start(bf16[512,128]{1,0:T(8,128)(2,1)S(1)} %copy-done.22), channel_id=1, source_target_pairs={{0,20},{8,11},{1,21},{9,8},{2,22},{10,9},{3,23},{11,10},{32,52},{4... | collective-permute-start | bytes 393224 | tf_op jit(solution)/shard_map/ppermute | solution.py:46
  40.7 7.8 %collective-permute-start.21 = (bf16[1024,128]{1,0:T(8,128)(2,1)}, bf16[1024,128]{1,0:T(8,128)(2,1)S(1)}, u32[]{:S(2)}, u32[]{:S(2)}) collective-permute-start(bf16[1024,128]{1,0:T(8,128)(2,1)} %get-tuple-element.56), channel_id=1, source_target_pairs={{0,2},{8,24},{1,3},{9,25},{2,0},{10,26},{3,1},{11,27},{32,34},{40,... | collective-permute-start | bytes 786440 | tf_op jit(solution)/shard_map/ppermute | solution.py:46
  43.1 24.6 %collective-permute-start.11 = (bf16[2048,128]{1,0:T(8,128)(2,1)}, bf16[2048,128]{1,0:T(8,128)(2,1)S(1)}, u32[]{:S(2)}, u32[]{:S(2)}) collective-permute-start(bf16[2048,128]{1,0:T(8,128)(2,1)} %get-tuple-element.50), channel_id=1, source_target_pairs={{0,1},{8,12},{1,2},{9,13},{2,3},{10,14},{3,0},{11,15},{32,33},{40,... | collective-permute-start | bytes 1572872 | tf_op jit(solution)/shard_map/ppermute | solution.py:46
  44.2 7.2 %collective-permute-start.22 = (bf16[1024,128]{1,0:T(8,128)(2,1)}, bf16[1024,128]{1,0:T(8,128)(2,1)S(1)}, u32[]{:S(2)}, u32[]{:S(2)}) collective-permute-start(bf16[1024,128]{1,0:T(8,128)(2,1)} %get-tuple-element.56), channel_id=1, source_target_pairs={{0,3},{8,28},{1,0},{9,29},{2,1},{10,30},{3,2},{11,31},{32,35},{40,... | collective-permute-start | bytes 786440 | tf_op jit(solution)/shard_map/ppermute | solution.py:46
  45.8 22.0 %collective-permute-start.12 = (bf16[2048,128]{1,0:T(8,128)(2,1)}, bf16[2048,128]{1,0:T(8,128)(2,1)S(1)}, u32[]{:S(2)}, u32[]{:S(2)}) collective-permute-start(bf16[2048,128]{1,0:T(8,128)(2,1)} %get-tuple-element.50), channel_id=1, source_target_pairs={{0,2},{8,24},{1,3},{9,25},{2,0},{10,26},{3,1},{11,27},{32,34},{40,... | collective-permute-start | bytes 1572872 | tf_op jit(solution)/shard_map/ppermute | solution.py:46
  47.2 20.6 %collective-permute-start.13 = (bf16[2048,128]{1,0:T(8,128)(2,1)}, bf16[2048,128]{1,0:T(8,128)(2,1)S(1)}, u32[]{:S(2)}, u32[]{:S(2)}) collective-permute-start(bf16[2048,128]{1,0:T(8,128)(2,1)} %get-tuple-element.50), channel_id=1, source_target_pairs={{0,3},{8,28},{1,0},{9,29},{2,1},{10,30},{3,2},{11,31},{32,35},{40,... | collective-permute-start | bytes 1572872 | tf_op jit(solution)/shard_map/ppermute | solution.py:46
  48.5 15.4 %collective-permute-start.9 = (bf16[1024,128]{1,0:T(8,128)(2,1)}, bf16[1024,128]{1,0:T(8,128)(2,1)S(1)}, u32[]{:S(2)}, u32[]{:S(2)}) collective-permute-start(bf16[1024,128]{1,0:T(8,128)(2,1)} %get-tuple-element.49), channel_id=1, source_target_pairs={{0,16},{8,10},{1,17},{9,11},{2,18},{10,8},{3,19},{11,9},{32,48},{4... | collective-permute-start | bytes 786440 | tf_op jit(solution)/shard_map/ppermute | solution.py:46
  51.4 16.4 %collective-permute-start.10 = (bf16[1024,128]{1,0:T(8,128)(2,1)}, bf16[1024,128]{1,0:T(8,128)(2,1)S(1)}, u32[]{:S(2)}, u32[]{:S(2)}) collective-permute-start(bf16[1024,128]{1,0:T(8,128)(2,1)} %get-tuple-element.49), channel_id=1, source_target_pairs={{0,20},{8,11},{1,21},{9,8},{2,22},{10,9},{3,23},{11,10},{32,52},{4... | collective-permute-start | bytes 786440 | tf_op jit(solution)/shard_map/ppermute | solution.py:46
  63.9 28.7 %collective-permute-start.23 = (bf16[544,128]{1,0:T(8,128)(2,1)}, bf16[544,128]{1,0:T(8,128)(2,1)S(1)}, u32[]{:S(2)}, u32[]{:S(2)}) collective-permute-start(bf16[544,128]{1,0:T(8,128)(2,1)} %get-tuple-element.58), channel_id=1, source_target_pairs={{0,20},{8,11},{1,21},{9,8},{2,22},{10,9},{3,23},{11,10},{32,52},{4... | collective-permute-start | bytes 417800 | tf_op jit(solution)/shard_map/ppermute | solution.py:46
  87.2 13.5 %collective-permute-start.14 = (bf16[1088,128]{1,0:T(8,128)(2,1)}, bf16[1088,128]{1,0:T(8,128)(2,1)S(1)}, u32[]{:S(2)}, u32[]{:S(2)}) collective-permute-start(bf16[1088,128]{1,0:T(8,128)(2,1)} %get-tuple-element.52), channel_id=1, source_target_pairs={{0,20},{8,11},{1,21},{9,8},{2,22},{10,9},{3,23},{11,10},{32,52},{4... | collective-permute-start | bytes 835592 | tf_op jit(solution)/shard_map/ppermute | solution.py:46
  89.6 11.1 %collective-permute-start.15 = (bf16[1088,128]{1,0:T(8,128)(2,1)}, bf16[1088,128]{1,0:T(8,128)(2,1)S(1)}, u32[]{:S(2)}, u32[]{:S(2)}) collective-permute-start(bf16[1088,128]{1,0:T(8,128)(2,1)} %get-tuple-element.53), channel_id=1, source_target_pairs={{0,16},{8,10},{1,17},{9,11},{2,18},{10,8},{3,19},{11,9},{32,48},{4... | collective-permute-start | bytes 835592 | tf_op jit(solution)/shard_map/ppermute | solution.py:46
  89.9 10.9 %collective-permute-start.16 = (bf16[1088,128]{1,0:T(8,128)(2,1)}, bf16[1088,128]{1,0:T(8,128)(2,1)S(1)}, u32[]{:S(2)}, u32[]{:S(2)}) collective-permute-start(bf16[1088,128]{1,0:T(8,128)(2,1)} %get-tuple-element.54), channel_id=1, source_target_pairs={{0,4},{8,9},{1,5},{9,10},{2,6},{10,11},{3,7},{11,8},{32,36},{40,41... | collective-permute-start | bytes 835592 | tf_op jit(solution)/shard_map/ppermute | solution.py:46
  91.7 6.8 %collective-permute-start.24 = (bf16[544,128]{1,0:T(8,128)(2,1)S(1)}, bf16[544,128]{1,0:T(8,128)(2,1)S(1)}, u32[]{:S(2)}, u32[]{:S(2)}) collective-permute-start(bf16[544,128]{1,0:T(8,128)(2,1)S(1)} %copy-done.34), channel_id=1, source_target_pairs={{0,16},{8,10},{1,17},{9,11},{2,18},{10,8},{3,19},{11,9},{32,48},{4... | collective-permute-start | bytes 417800 | tf_op jit(solution)/shard_map/ppermute | solution.py:46
  92.6 8.1 %collective-permute-start.25 = (bf16[544,128]{1,0:T(8,128)(2,1)S(1)}, bf16[544,128]{1,0:T(8,128)(2,1)S(1)}, u32[]{:S(2)}, u32[]{:S(2)}) collective-permute-start(bf16[544,128]{1,0:T(8,128)(2,1)S(1)} %copy-done.33), channel_id=1, source_target_pairs={{0,4},{8,9},{1,5},{9,10},{2,6},{10,11},{3,7},{11,8},{32,36},{40,41... | collective-permute-start | bytes 417800 | tf_op jit(solution)/shard_map/ppermute | solution.py:46
  104.7 18.6 %collective-permute-start.26 = (bf16[64,384]{1,0:T(8,128)(2,1)}, bf16[64,384]{1,0:T(8,128)(2,1)S(1)}, u32[]{:S(2)}, u32[]{:S(2)}) collective-permute-start(bf16[64,384]{1,0:T(8,128)(2,1)} %get-tuple-element.62), channel_id=1, source_target_pairs={{0,8},{8,0},{1,9},{9,1},{2,10},{10,2},{3,11},{11,3},{32,40},{40,32... | collective-permute-start | bytes 147464 | tf_op jit(solution)/shard_map/ppermute | solution.py:46
  116.0 8.7 %collective-permute-start.27 = (bf16[64,384]{1,0:T(8,128)(2,1)}, bf16[64,384]{1,0:T(8,128)(2,1)S(1)}, u32[]{:S(2)}, u32[]{:S(2)}) collective-permute-start(bf16[64,384]{1,0:T(8,128)(2,1)} %get-tuple-element.63), channel_id=1, source_target_pairs={{0,96},{8,104},{1,97},{9,105},{2,98},{10,106},{3,99},{11,107},{32,... | collective-permute-start | bytes 147464 | tf_op jit(solution)/shard_map/ppermute | solution.py:46
  119.7 5.7 %collective-permute-start.28 = (bf16[64,384]{1,0:T(8,128)(2,1)}, bf16[64,384]{1,0:T(8,128)(2,1)S(1)}, u32[]{:S(2)}, u32[]{:S(2)}) collective-permute-start(bf16[64,384]{1,0:T(8,128)(2,1)} %get-tuple-element.64), channel_id=1, source_target_pairs={{0,104},{8,96},{1,105},{9,97},{2,106},{10,98},{3,107},{11,99},{32,... | collective-permute-start | bytes 147464 | tf_op jit(solution)/shard_map/ppermute | solution.py:46
  119.7 5.7 %collective-permute-start.29 = (bf16[64,384]{1,0:T(8,128)(2,1)}, bf16[64,384]{1,0:T(8,128)(2,1)S(1)}, u32[]{:S(2)}, u32[]{:S(2)}) collective-permute-start(bf16[64,384]{1,0:T(8,128)(2,1)} %get-tuple-element.65), channel_id=1, source_target_pairs={{0,64},{8,72},{1,65},{9,73},{2,66},{10,74},{3,67},{11,75},{32,96},... | collective-permute-start | bytes 147464 | tf_op jit(solution)/shard_map/ppermute | solution.py:46
  121.1 5.9 %collective-permute-start.30 = (bf16[64,384]{1,0:T(8,128)(2,1)}, bf16[64,384]{1,0:T(8,128)(2,1)S(1)}, u32[]{:S(2)}, u32[]{:S(2)}) collective-permute-start(bf16[64,384]{1,0:T(8,128)(2,1)} %get-tuple-element.66), channel_id=1, source_target_pairs={{0,72},{8,64},{1,73},{9,65},{2,74},{10,66},{3,75},{11,67},{32,104}... | collective-permute-start | bytes 147464 | tf_op jit(solution)/shard_map/ppermute | solution.py:46
  123.2 4.8 %collective-permute-start.31 = (bf16[64,384]{1,0:T(8,128)(2,1)}, bf16[64,384]{1,0:T(8,128)(2,1)S(1)}, u32[]{:S(2)}, u32[]{:S(2)}) collective-permute-start(bf16[64,384]{1,0:T(8,128)(2,1)} %get-tuple-element.67), channel_id=1, source_target_pairs={{0,32},{8,40},{1,33},{9,41},{2,34},{10,42},{3,35},{11,43},{32,64},... | collective-permute-start | bytes 147464 | tf_op jit(solution)/shard_map/ppermute | solution.py:46
  124.7 5.1 %collective-permute-start.32 = (bf16[64,384]{1,0:T(8,128)(2,1)}, bf16[64,384]{1,0:T(8,128)(2,1)S(1)}, u32[]{:S(2)}, u32[]{:S(2)}) collective-permute-start(bf16[64,384]{1,0:T(8,128)(2,1)} %get-tuple-element.68), channel_id=1, source_target_pairs={{0,40},{8,32},{1,41},{9,33},{2,42},{10,34},{3,43},{11,35},{32,72},... | collective-permute-start | bytes 147464 | tf_op jit(solution)/shard_map/ppermute | solution.py:46
  (37 other events, 209.5 us)
where the time goes:
time: 133 us; the launch traced here: 132 us
  starting transfers between devices  58.4 us (44%)
  Pallas kernels  38.2 us (29%)
  waiting for transfers between devices  26.2 us (20%)
  local copies, waits for them, and re-layouts  5.44 us (4%)
  other arithmetic  2.47 us (2%)
  between operations  1.61 us (1%)
    ppermute x33, starting transfers between devices, moved(): return lax.ppermute(array, BOTH, pairs)  58.4 us
    pallas_call x2, Pallas kernels, attend(): call(functools.partial(attend_kernel, count), [shape(count * (SET + META)...  28.4 us
    ppermute x33, waiting for transfers between devices, moved(): return lax.ppermute(array, BOTH, pairs)  26.2 us
    unnamed x72, local copies, waits for them, and re-layouts  4.07 us
    pallas_call x1, Pallas kernels, local(): call(combine_kernel, [shape(ROWS, WIDTH)] * GROUP, [SMEM] + [VMEM] * len(...  2.93 us
  transfers between devices with their start and end apart: 33, of which 14 were waited for; matrix products, arithmetic and copies ran while one was open for 2% of the time, Pallas kernels for 21%

commit v1 on v0

--- a/solution.py
+++ b/solution.py
@@ -300,7 +300,9 @@
         [shape(3 * ROWS + 16, WIDTH)] * GROUP,
         [SMEM, VMEM, VMEM, VMEM, VMEM],
     )(target, queries[0], keys[0], values[0], meta)
-    shared = [packed[0]] + [moved(packed[j], **hops[j]) for j in range(1, GROUP)]
+    shared = [packed[0]]
+    for j in range(1, GROUP):
+        shared.append(moved(packed[j], **hops[j]))
 
     shapes = []
     for part in PARTS:
@@ -345,7 +347,9 @@
     mixed = call(
         combine_kernel, [shape(ROWS, WIDTH)] * GROUP, [SMEM] + [VMEM] * len(pieces)
     )(table, *pieces)
-    returned = [mixed[0]] + [moved(mixed[j], **backs[j]) for j in range(1, GROUP)]
+    returned = [mixed[0]]
+    for j in range(1, GROUP):
+        returned.append(moved(mixed[j], **backs[j]))
     result = call(finish_kernel, shape(ROWS, GROUP * WIDTH), [SMEM, SMEM] + [VMEM] * (GROUP + 1))(
         target, levels, gates, *returned
     )

time: 133 us -> 133 us (level)
  no operation moved by 1% of the time
where the time goes in v1:
time: 133 us; the launch traced here: 132 us
  starting transfers between devices  58.4 us (44%)
  Pallas kernels  38.2 us (29%)
  waiting for transfers between devices  26.2 us (20%)
  local copies, waits for them, and re-layouts  5.44 us (4%)
  other arithmetic  2.47 us (2%)
  between operations  1.61 us (1%)
    ppermute x33, starting transfers between devices, moved(): return lax.ppermute(array, BOTH, pairs)  58.4 us
    pallas_call x2, Pallas kernels, attend(): call(functools.partial(attend_kernel, count), [shape(count * (SET + META)...  28.4 us
    ppermute x33, waiting for transfers between devices, moved(): return lax.ppermute(array, BOTH, pairs)  26.2 us
    unnamed x72, local copies, waits for them, and re-layouts  4.07 us
    pallas_call x1, Pallas kernels, local(): call(combine_kernel, [shape(ROWS, WIDTH)] * GROUP, [SMEM] + [VMEM] * len(...  2.93 us
  transfers between devices with their start and end apart: 33, of which 14 were waited for; matrix products, arithmetic and copies ran while one was open for 2% of the time, Pallas kernels for 21%

profile of v1, /device:TPU:33, one launch (start us, length us, event | category | flops | bytes accessed | tf_op | source)
XLA Modules:
  0.0 132.3 jit_solution(15900515895141059410)
XLA Ops:
  1.9 2.4 %shard_map.73 = (bf16[208,384]{1,0:T(8,128)(2,1)}, bf16[208,384]{1,0:T(8,128)(2,1)}, bf16[208,384]{1,0:T(8,128)(2,1)}, bf16[208,384]{1,0:T(8,128)(2,1)}, bf16[20...) custom-call(s32[8]{0:T(128)} %fusion.3.at_ref, ...), custom_call_target="tpu_custom_call" | custom-call | tf_op jit(solution)/shard_map/pallas_call | solution.py:298
  6.2 1.5 %collective-permute-start.2 = (bf16[208,384]{1,0:T(8,128)(2,1)}, bf16[208,384]{1,0:T(8,128)(2,1)S(1)}, u32[]{:S(2)}, u32[]{:S(2)}) collective-permute-start(bf16[208,384]{1,0:T(8,128)(2,1)} %get-tuple-element.40), channel_id=1, source_target_pairs={{0,40},{8,32},{1,41},{9,33},{2,42},{10,34},{3,43},{11,35},{32,72},... | collective-permute-start | bytes 479240 | tf_op jit(solution)/shard_map/ppermute | solution.py:46
  9.0 2.0 %collective-permute-start.4 = (bf16[208,384]{1,0:T(8,128)(2,1)}, bf16[208,384]{1,0:T(8,128)(2,1)S(1)}, u32[]{:S(2)}, u32[]{:S(2)}) collective-permute-start(bf16[208,384]{1,0:T(8,128)(2,1)} %get-tuple-element.42), channel_id=1, source_target_pairs={{0,72},{8,64},{1,73},{9,65},{2,74},{10,66},{3,75},{11,67},{32,104}... | collective-permute-start | bytes 479240 | tf_op jit(solution)/shard_map/ppermute | solution.py:46
  11.8 1.4 %collective-permute-start.5 = (bf16[208,384]{1,0:T(8,128)(2,1)}, bf16[208,384]{1,0:T(8,128)(2,1)S(1)}, u32[]{:S(2)}, u32[]{:S(2)}) collective-permute-start(bf16[208,384]{1,0:T(8,128)(2,1)} %get-tuple-element.43), channel_id=1, source_target_pairs={{0,96},{8,104},{1,97},{9,105},{2,98},{10,106},{3,99},{11,107},{32,... | collective-permute-start | bytes 479240 | tf_op jit(solution)/shard_map/ppermute | solution.py:46
  13.3 1.5 %collective-permute-start.6 = (bf16[208,384]{1,0:T(8,128)(2,1)}, bf16[208,384]{1,0:T(8,128)(2,1)S(1)}, u32[]{:S(2)}, u32[]{:S(2)}) collective-permute-start(bf16[208,384]{1,0:T(8,128)(2,1)} %get-tuple-element.44), channel_id=1, source_target_pairs={{0,104},{8,96},{1,105},{9,97},{2,106},{10,98},{3,107},{11,99},{32,... | collective-permute-start | bytes 479240 | tf_op jit(solution)/shard_map/ppermute | solution.py:46
  15.7 4.4 %collective-permute-done.3.refs_4_ = bf16[208,384]{1,0:T(8,128)(2,1)S(1)} collective-permute-done((bf16[208,384]{1,0:T(8,128)(2,1)}, bf16[208,384]{1,0:T(8,128)(2,1)S(1)}, u32[]{:S(2)}, u32[]{:S(2)}) %collective-permute-start.3) | collective-permute-done | bytes 159776 | tf_op jit(solution)/shard_map/ppermute | solution.py:46
  20.1 3.6 %collective-permute-done.4.refs_5_ = bf16[208,384]{1,0:T(8,128)(2,1)S(1)} collective-permute-done((bf16[208,384]{1,0:T(8,128)(2,1)}, bf16[208,384]{1,0:T(8,128)(2,1)S(1)}, u32[]{:S(2)}, u32[]{:S(2)}) %collective-permute-start.4) | collective-permute-done | bytes 159776 | tf_op jit(solution)/shard_map/ppermute | solution.py:46
  25.3 2.6 %shard_map.74 = (bf16[1024,128]{1,0:T(8,128)(2,1)}, bf16[2048,128]{1,0:T(8,128)(2,1)}, bf16[512,128]{1,0:T(8,128)(2,1)}, bf16[1024,128]{1,0:T(8,128)(2,1)}, f32[8,128]{1,0:T(8,128)}) custom-call(bf16[208,384]{1,0:T(8,128)(2,1)} %get-tuple-element.37.refs_0_, bf16[208,384]{1,0:T(8,128)(2,1)} %copy-done.12, bf16[208,384]{1,0:T(8,128)(2,1)} %copy-done.13, ...), custom_call_target="tpu_custom_call" | custom-call | tf_op jit(solution)/shard_map/pallas_call | solution.py:310
  27.8 2.8 %collective-permute-start.7 = (f32[8,128]{1,0:T(8,128)}, f32[8,128]{1,0:T(8,128)S(1)}, u32[]{:S(2)}, u32[]{:S(2)}) collective-permute-start(f32[8,128]{1,0:T(8,128)} %get-tuple-element.47), channel_id=1, source_target_pairs={{0,16},{8,24},{1,17},{9,25},{2,18},{10,26},{3,19},{11,27},{32,48},... | collective-permute-start | bytes 12296 | tf_op jit(solution)/shard_map/ppermute | solution.py:46
  30.7 1.6 %collective-permute-start.8 = (bf16[1024,128]{1,0:T(8,128)(2,1)}, bf16[1024,128]{1,0:T(8,128)(2,1)S(1)}, u32[]{:S(2)}, u32[]{:S(2)}) collective-permute-start(bf16[1024,128]{1,0:T(8,128)(2,1)} %get-tuple-element.49), channel_id=1, source_target_pairs={{0,4},{8,9},{1,5},{9,10},{2,6},{10,11},{3,7},{11,8},{32,36},{40,41... | collective-permute-start | bytes 786440 | tf_op jit(solution)/shard_map/ppermute | solution.py:46
  35.8 1.6 %collective-permute-start.17 = (bf16[512,128]{1,0:T(8,128)(2,1)S(1)}, bf16[512,128]{1,0:T(8,128)(2,1)S(1)}, u32[]{:S(2)}, u32[]{:S(2)}) collective-permute-start(bf16[512,128]{1,0:T(8,128)(2,1)S(1)} %copy-done.22), channel_id=1, source_target_pairs={{0,4},{8,9},{1,5},{9,10},{2,6},{10,11},{3,7},{11,8},{32,36},{40,41... | collective-permute-start | bytes 393224 | tf_op jit(solution)/shard_map/ppermute | solution.py:46
  38.5 2.1 %collective-permute-start.19 = (bf16[512,128]{1,0:T(8,128)(2,1)S(1)}, bf16[512,128]{1,0:T(8,128)(2,1)S(1)}, u32[]{:S(2)}, u32[]{:S(2)}) collective-permute-start(bf16[512,128]{1,0:T(8,128)(2,1)S(1)} %copy-done.22), channel_id=1, source_target_pairs={{0,20},{8,11},{1,21},{9,8},{2,22},{10,9},{3,23},{11,10},{32,52},{4... | collective-permute-start | bytes 393224 | tf_op jit(solution)/shard_map/ppermute | solution.py:46
  40.7 2.4 %collective-permute-start.21 = (bf16[1024,128]{1,0:T(8,128)(2,1)}, bf16[1024,128]{1,0:T(8,128)(2,1)S(1)}, u32[]{:S(2)}, u32[]{:S(2)}) collective-permute-start(bf16[1024,128]{1,0:T(8,128)(2,1)} %get-tuple-element.56), channel_id=1, source_target_pairs={{0,2},{8,24},{1,3},{9,25},{2,0},{10,26},{3,1},{11,27},{32,34},{40,... | collective-permute-start | bytes 786440 | tf_op jit(solution)/shard_map/ppermute | solution.py:46
  44.2 1.6 %collective-permute-start.22 = (bf16[1024,128]{1,0:T(8,128)(2,1)}, bf16[1024,128]{1,0:T(8,128)(2,1)S(1)}, u32[]{:S(2)}, u32[]{:S(2)}) collective-permute-start(bf16[1024,128]{1,0:T(8,128)(2,1)} %get-tuple-element.56), channel_id=1, source_target_pairs={{0,3},{8,28},{1,0},{9,29},{2,1},{10,30},{3,2},{11,31},{32,35},{40,... | collective-permute-start | bytes 786440 | tf_op jit(solution)/shard_map/ppermute | solution.py:46
  48.5 2.1 %collective-permute-start.9 = (bf16[1024,128]{1,0:T(8,128)(2,1)}, bf16[1024,128]{1,0:T(8,128)(2,1)S(1)}, u32[]{:S(2)}, u32[]{:S(2)}) collective-permute-start(bf16[1024,128]{1,0:T(8,128)(2,1)} %get-tuple-element.49), channel_id=1, source_target_pairs={{0,16},{8,10},{1,17},{9,11},{2,18},{10,8},{3,19},{11,9},{32,48},{4... | collective-permute-start | bytes 786440 | tf_op jit(solution)/shard_map/ppermute | solution.py:46
  51.4 2.3 %collective-permute-start.10 = (bf16[1024,128]{1,0:T(8,128)(2,1)}, bf16[1024,128]{1,0:T(8,128)(2,1)S(1)}, u32[]{:S(2)}, u32[]{:S(2)}) collective-permute-start(bf16[1024,128]{1,0:T(8,128)(2,1)} %get-tuple-element.49), channel_id=1, source_target_pairs={{0,20},{8,11},{1,21},{9,8},{2,22},{10,9},{3,23},{11,10},{32,52},{4... | collective-permute-start | bytes 786440 | tf_op jit(solution)/shard_map/ppermute | solution.py:46
  53.7 10.2 %shard_map.76 = (bf16[544,128]{1,0:T(8,128)(2,1)}, bf16[544,128]{1,0:T(8,128)(2,1)}, bf16[544,128]{1,0:T(8,128)(2,1)}, bf16[544,128]{1,0:T(8,128)(2,1)}) custom-call(s32[280]{0:T(512)} %pad_add_fusion.table_ref, bf16[1,8,64,128]{3,2,1,0:T(8,128)(2,1)} %bitcast.39, bf16[1,8,64,128]{3,2,1,0:T(8,128)(2,1)} %bitcast.40, bf16[1,8,64,128]{3,2,1,0:T(8,128)(2,1)} %bitcast.41, ...), custom_call_target="tpu_custom_call" | custom-call | tf_op jit(solution)/shard_map/pallas_call | solution.py:220
  64.7 3.1 %collective-permute-done.10 = bf16[1024,128]{1,0:T(8,128)(2,1)S(1)} collective-permute-done((bf16[1024,128]{1,0:T(8,128)(2,1)}, bf16[1024,128]{1,0:T(8,128)(2,1)S(1)}, u32[]{:S(2)}, u32[]{:S(2)}) %collective-permute-start.10) | collective-permute-done | bytes 262176 | tf_op jit(solution)/shard_map/ppermute | solution.py:46
  69.0 18.2 %shard_map.75 = (bf16[1088,128]{1,0:T(8,128)(2,1)}, bf16[1088,128]{1,0:T(8,128)(2,1)}, bf16[1088,128]{1,0:T(8,128)(2,1)}, bf16[1088,128]{1,0:T(8,128)(2,1)}) custom-call(s32[280]{0:T(512)} %pad_add_fusion.table_ref, bf16[2,8,64,128]{3,2,1,0:T(8,128)(2,1)} %bitcast.35, bf16[2,8,64,128]{3,2,1,0:T(8,128)(2,1)} %bitcast.36, bf16[2,8,64,128]{3,2,1,0:T(8,128)(2,1)} %bitcast.37, ...), custom_call_target="tpu_custom_call" | custom-call | tf_op jit(solution)/shard_map/pallas_call | solution.py:220
  87.2 2.4 %collective-permute-start.14 = (bf16[1088,128]{1,0:T(8,128)(2,1)}, bf16[1088,128]{1,0:T(8,128)(2,1)S(1)}, u32[]{:S(2)}, u32[]{:S(2)}) collective-permute-start(bf16[1088,128]{1,0:T(8,128)(2,1)} %get-tuple-element.52), channel_id=1, source_target_pairs={{0,20},{8,11},{1,21},{9,8},{2,22},{10,9},{3,23},{11,10},{32,52},{4... | collective-permute-start | bytes 835592 | tf_op jit(solution)/shard_map/ppermute | solution.py:46
  89.9 1.8 %collective-permute-start.16 = (bf16[1088,128]{1,0:T(8,128)(2,1)}, bf16[1088,128]{1,0:T(8,128)(2,1)S(1)}, u32[]{:S(2)}, u32[]{:S(2)}) collective-permute-start(bf16[1088,128]{1,0:T(8,128)(2,1)} %get-tuple-element.54), channel_id=1, source_target_pairs={{0,4},{8,9},{1,5},{9,10},{2,6},{10,11},{3,7},{11,8},{32,36},{40,41... | collective-permute-start | bytes 835592 | tf_op jit(solution)/shard_map/ppermute | solution.py:46
  93.2 5.3 %collective-permute-done.24.refs_6_ = bf16[544,128]{1,0:T(8,128)(2,1)S(1)} collective-permute-done((bf16[544,128]{1,0:T(8,128)(2,1)S(1)}, bf16[544,128]{1,0:T(8,128)(2,1)S(1)}, u32[]{:S(2)}, u32[]{:S(2)}) %collective-permute-start.24) | collective-permute-done | bytes 139296 | tf_op jit(solution)/shard_map/ppermute | solution.py:46
  98.5 2.2 %collective-permute-done.25.refs_7_ = bf16[544,128]{1,0:T(8,128)(2,1)S(1)} collective-permute-done((bf16[544,128]{1,0:T(8,128)(2,1)S(1)}, bf16[544,128]{1,0:T(8,128)(2,1)S(1)}, u32[]{:S(2)}, u32[]{:S(2)}) %collective-permute-start.25) | collective-permute-done | bytes 139296 | tf_op jit(solution)/shard_map/ppermute | solution.py:46
  101.7 2.9 %shard_map.77 = (bf16[64,384]{1,0:T(8,128)(2,1)}, bf16[64,384]{1,0:T(8,128)(2,1)}, bf16[64,384]{1,0:T(8,128)(2,1)}, bf16[64,384]{1,0:T(8,128)(2,1)}, bf16[64,384...) custom-call(s32[280]{0:T(512)} %pad_add_fusion.table_ref, ...), custom_call_target="tpu_custom_call" | custom-call | tf_op jit(solution)/shard_map/pallas_call | solution.py:347
  104.7 11.3 %collective-permute-start.26 = (bf16[64,384]{1,0:T(8,128)(2,1)}, bf16[64,384]{1,0:T(8,128)(2,1)S(1)}, u32[]{:S(2)}, u32[]{:S(2)}) collective-permute-start(bf16[64,384]{1,0:T(8,128)(2,1)} %get-tuple-element.62), channel_id=1, source_target_pairs={{0,8},{8,0},{1,9},{9,1},{2,10},{10,2},{3,11},{11,3},{32,40},{40,32... | collective-permute-start | bytes 147464 | tf_op jit(solution)/shard_map/ppermute | solution.py:46
  116.0 3.7 %collective-permute-start.27 = (bf16[64,384]{1,0:T(8,128)(2,1)}, bf16[64,384]{1,0:T(8,128)(2,1)S(1)}, u32[]{:S(2)}, u32[]{:S(2)}) collective-permute-start(bf16[64,384]{1,0:T(8,128)(2,1)} %get-tuple-element.63), channel_id=1, source_target_pairs={{0,96},{8,104},{1,97},{9,105},{2,98},{10,106},{3,99},{11,107},{32,... | collective-permute-start | bytes 147464 | tf_op jit(solution)/shard_map/ppermute | solution.py:46
  119.7 1.4 %collective-permute-start.29 = (bf16[64,384]{1,0:T(8,128)(2,1)}, bf16[64,384]{1,0:T(8,128)(2,1)S(1)}, u32[]{:S(2)}, u32[]{:S(2)}) collective-permute-start(bf16[64,384]{1,0:T(8,128)(2,1)} %get-tuple-element.65), channel_id=1, source_target_pairs={{0,64},{8,72},{1,65},{9,73},{2,66},{10,74},{3,67},{11,75},{32,96},... | collective-permute-start | bytes 147464 | tf_op jit(solution)/shard_map/ppermute | solution.py:46
  121.1 2.1 %collective-permute-start.30 = (bf16[64,384]{1,0:T(8,128)(2,1)}, bf16[64,384]{1,0:T(8,128)(2,1)S(1)}, u32[]{:S(2)}, u32[]{:S(2)}) collective-permute-start(bf16[64,384]{1,0:T(8,128)(2,1)} %get-tuple-element.66), channel_id=1, source_target_pairs={{0,72},{8,64},{1,73},{9,65},{2,74},{10,66},{3,75},{11,67},{32,104}... | collective-permute-start | bytes 147464 | tf_op jit(solution)/shard_map/ppermute | solution.py:46
  123.2 1.5 %collective-permute-start.31 = (bf16[64,384]{1,0:T(8,128)(2,1)}, bf16[64,384]{1,0:T(8,128)(2,1)S(1)}, u32[]{:S(2)}, u32[]{:S(2)}) collective-permute-start(bf16[64,384]{1,0:T(8,128)(2,1)} %get-tuple-element.67), channel_id=1, source_target_pairs={{0,32},{8,40},{1,33},{9,41},{2,34},{10,42},{3,35},{11,43},{32,64},... | collective-permute-start | bytes 147464 | tf_op jit(solution)/shard_map/ppermute | solution.py:46
  125.4 1.6 %collective-permute-done.30.refs_5_ = bf16[64,384]{1,0:T(8,128)(2,1)S(1)} collective-permute-done((bf16[64,384]{1,0:T(8,128)(2,1)}, bf16[64,384]{1,0:T(8,128)(2,1)S(1)}, u32[]{:S(2)}, u32[]{:S(2)}) %collective-permute-start.30) | collective-permute-done | bytes 49184 | tf_op jit(solution)/shard_map/ppermute | solution.py:46
  128.1 1.7 %collective-permute-done.32.refs_7_ = bf16[64,384]{1,0:T(8,128)(2,1)S(1)} collective-permute-done((bf16[64,384]{1,0:T(8,128)(2,1)}, bf16[64,384]{1,0:T(8,128)(2,1)S(1)}, u32[]{:S(2)}, u32[]{:S(2)}) %collective-permute-start.32) | collective-permute-done | bytes 49184 | tf_op jit(solution)/shard_map/ppermute | solution.py:46
  130.4 1.9 %shard_map.78 = bf16[64,3072]{1,0:T(8,128)(2,1)} custom-call(s32[8]{0:T(128)} %fusion.3.at_ref, s32[1]{0:T(128)S(6)} %copy.8.level_ref, f32[16,3072]{1,0:T(8,128)} %gates_ref.1, bf16[64,384]{1,0:T(8,128)(2,1)} %get-tuple-element.61.refs_0_, bf16[64,384]{1,0:T(8,128)(2,1)} %copy-done.26, bf16[64,384]{1,0:T(8,128)(2,1)} %copy-done.27, ...), custom_call_target="tpu_custom_call" | custom-call | tf_op jit(solution)/shard_map/pallas_call | solution.py:353
  (129 shorter events, 23.3 us)
Async XLA Ops:
  4.3 7.6 %collective-permute-start = (bf16[208,384]{1,0:T(8,128)(2,1)}, bf16[208,384]{1,0:T(8,128)(2,1)S(1)}, u32[]{:S(2)}, u32[]{:S(2)}) collective-permute-start(bf16[208,384]{1,0:T(8,128)(2,1)} %get-tuple-element.38), channel_id=1, source_target_pairs={{0,8},{8,0},{1,9},{9,1},{2,10},{10,2},{3,11},{11,3},{32,40},{40,32... | collective-permute-start | bytes 479240 | tf_op jit(solution)/shard_map/ppermute | solution.py:46
  4.9 8.3 %collective-permute-start.1 = (bf16[208,384]{1,0:T(8,128)(2,1)}, bf16[208,384]{1,0:T(8,128)(2,1)S(1)}, u32[]{:S(2)}, u32[]{:S(2)}) collective-permute-start(bf16[208,384]{1,0:T(8,128)(2,1)} %get-tuple-element.39), channel_id=1, source_target_pairs={{0,32},{8,40},{1,33},{9,41},{2,34},{10,42},{3,35},{11,43},{32,64},... | collective-permute-start | bytes 479240 | tf_op jit(solution)/shard_map/ppermute | solution.py:46
  6.2 9.4 %collective-permute-start.2 = (bf16[208,384]{1,0:T(8,128)(2,1)}, bf16[208,384]{1,0:T(8,128)(2,1)S(1)}, u32[]{:S(2)}, u32[]{:S(2)}) collective-permute-start(bf16[208,384]{1,0:T(8,128)(2,1)} %get-tuple-element.40), channel_id=1, source_target_pairs={{0,40},{8,32},{1,41},{9,33},{2,42},{10,34},{3,43},{11,35},{32,72},... | collective-permute-start | bytes 479240 | tf_op jit(solution)/shard_map/ppermute | solution.py:46
  7.7 12.3 %collective-permute-start.3 = (bf16[208,384]{1,0:T(8,128)(2,1)}, bf16[208,384]{1,0:T(8,128)(2,1)S(1)}, u32[]{:S(2)}, u32[]{:S(2)}) collective-permute-start(bf16[208,384]{1,0:T(8,128)(2,1)} %get-tuple-element.41), channel_id=1, source_target_pairs={{0,64},{8,72},{1,65},{9,73},{2,66},{10,74},{3,67},{11,75},{32,96},... | collective-permute-start | bytes 479240 | tf_op jit(solution)/shard_map/ppermute | solution.py:46
  9.0 14.7 %collective-permute-start.4 = (bf16[208,384]{1,0:T(8,128)(2,1)}, bf16[208,384]{1,0:T(8,128)(2,1)S(1)}, u32[]{:S(2)}, u32[]{:S(2)}) collective-permute-start(bf16[208,384]{1,0:T(8,128)(2,1)} %get-tuple-element.42), channel_id=1, source_target_pairs={{0,72},{8,64},{1,73},{9,65},{2,74},{10,66},{3,75},{11,67},{32,104}... | collective-permute-start | bytes 479240 | tf_op jit(solution)/shard_map/ppermute | solution.py:46
  11.8 11.9 %collective-permute-start.5 = (bf16[208,384]{1,0:T(8,128)(2,1)}, bf16[208,384]{1,0:T(8,128)(2,1)S(1)}, u32[]{:S(2)}, u32[]{:S(2)}) collective-permute-start(bf16[208,384]{1,0:T(8,128)(2,1)} %get-tuple-element.43), channel_id=1, source_target_pairs={{0,96},{8,104},{1,97},{9,105},{2,98},{10,106},{3,99},{11,107},{32,... | collective-permute-start | bytes 479240 | tf_op jit(solution)/shard_map/ppermute | solution.py:46
  13.3 11.3 %collective-permute-start.6 = (bf16[208,384]{1,0:T(8,128)(2,1)}, bf16[208,384]{1,0:T(8,128)(2,1)S(1)}, u32[]{:S(2)}, u32[]{:S(2)}) collective-permute-start(bf16[208,384]{1,0:T(8,128)(2,1)} %get-tuple-element.44), channel_id=1, source_target_pairs={{0,104},{8,96},{1,105},{9,97},{2,106},{10,98},{3,107},{11,99},{32,... | collective-permute-start | bytes 479240 | tf_op jit(solution)/shard_map/ppermute | solution.py:46
  30.7 15.2 %collective-permute-start.8 = (bf16[1024,128]{1,0:T(8,128)(2,1)}, bf16[1024,128]{1,0:T(8,128)(2,1)S(1)}, u32[]{:S(2)}, u32[]{:S(2)}) collective-permute-start(bf16[1024,128]{1,0:T(8,128)(2,1)} %get-tuple-element.49), channel_id=1, source_target_pairs={{0,4},{8,9},{1,5},{9,10},{2,6},{10,11},{3,7},{11,8},{32,36},{40,41... | collective-permute-start | bytes 786440 | tf_op jit(solution)/shard_map/ppermute | solution.py:46
  34.8 12.3 %collective-permute-start.20 = (bf16[1024,128]{1,0:T(8,128)(2,1)}, bf16[1024,128]{1,0:T(8,128)(2,1)S(1)}, u32[]{:S(2)}, u32[]{:S(2)}) collective-permute-start(bf16[1024,128]{1,0:T(8,128)(2,1)} %get-tuple-element.56), channel_id=1, source_target_pairs={{0,1},{8,12},{1,2},{9,13},{2,3},{10,14},{3,0},{11,15},{32,33},{40,... | collective-permute-start | bytes 786440 | tf_op jit(solution)/shard_map/ppermute | solution.py:46
  35.8 4.9 %collective-permute-start.17 = (bf16[512,128]{1,0:T(8,128)(2,1)S(1)}, bf16[512,128]{1,0:T(8,128)(2,1)S(1)}, u32[]{:S(2)}, u32[]{:S(2)}) collective-permute-start(bf16[512,128]{1,0:T(8,128)(2,1)S(1)} %copy-done.22), channel_id=1, source_target_pairs={{0,4},{8,9},{1,5},{9,10},{2,6},{10,11},{3,7},{11,8},{32,36},{40,41... | collective-permute-start | bytes 393224 | tf_op jit(solution)/shard_map/ppermute | solution.py:46
  37.5 5.7 %collective-permute-start.18 = (bf16[512,128]{1,0:T(8,128)(2,1)S(1)}, bf16[512,128]{1,0:T(8,128)(2,1)S(1)}, u32[]{:S(2)}, u32[]{:S(2)}) collective-permute-start(bf16[512,128]{1,0:T(8,128)(2,1)S(1)} %copy-done.22), channel_id=1, source_target_pairs={{0,16},{8,10},{1,17},{9,11},{2,18},{10,8},{3,19},{11,9},{32,48},{4... | collective-permute-start | bytes 393224 | tf_op jit(solution)/shard_map/ppermute | solution.py:46
  38.5 5.7 %collective-permute-start.19 = (bf16[512,128]{1,0:T(8,128)(2,1)S(1)}, bf16[512,128]{1,0:T(8,128)(2,1)S(1)}, u32[]{:S(2)}, u32[]{:S(2)}) collective-permute-start(bf16[512,128]{1,0:T(8,128)(2,1)S(1)} %copy-done.22), channel_id=1, source_target_pairs={{0,20},{8,11},{1,21},{9,8},{2,22},{10,9},{3,23},{11,10},{32,52},{4... | collective-permute-start | bytes 393224 | tf_op jit(solution)/shard_map/ppermute | solution.py:46
  40.7 7.8 %collective-permute-start.21 = (bf16[1024,128]{1,0:T(8,128)(2,1)}, bf16[1024,128]{1,0:T(8,128)(2,1)S(1)}, u32[]{:S(2)}, u32[]{:S(2)}) collective-permute-start(bf16[1024,128]{1,0:T(8,128)(2,1)} %get-tuple-element.56), channel_id=1, source_target_pairs={{0,2},{8,24},{1,3},{9,25},{2,0},{10,26},{3,1},{11,27},{32,34},{40,... | collective-permute-start | bytes 786440 | tf_op jit(solution)/shard_map/ppermute | solution.py:46
  43.1 24.6 %collective-permute-start.11 = (bf16[2048,128]{1,0:T(8,128)(2,1)}, bf16[2048,128]{1,0:T(8,128)(2,1)S(1)}, u32[]{:S(2)}, u32[]{:S(2)}) collective-permute-start(bf16[2048,128]{1,0:T(8,128)(2,1)} %get-tuple-element.50), channel_id=1, source_target_pairs={{0,1},{8,12},{1,2},{9,13},{2,3},{10,14},{3,0},{11,15},{32,33},{40,... | collective-permute-start | bytes 1572872 | tf_op jit(solution)/shard_map/ppermute | solution.py:46
  44.2 7.2 %collective-permute-start.22 = (bf16[1024,128]{1,0:T(8,128)(2,1)}, bf16[1024,128]{1,0:T(8,128)(2,1)S(1)}, u32[]{:S(2)}, u32[]{:S(2)}) collective-permute-start(bf16[1024,128]{1,0:T(8,128)(2,1)} %get-tuple-element.56), channel_id=1, source_target_pairs={{0,3},{8,28},{1,0},{9,29},{2,1},{10,30},{3,2},{11,31},{32,35},{40,... | collective-permute-start | bytes 786440 | tf_op jit(solution)/shard_map/ppermute | solution.py:46
  45.8 22.0 %collective-permute-start.12 = (bf16[2048,128]{1,0:T(8,128)(2,1)}, bf16[2048,128]{1,0:T(8,128)(2,1)S(1)}, u32[]{:S(2)}, u32[]{:S(2)}) collective-permute-start(bf16[2048,128]{1,0:T(8,128)(2,1)} %get-tuple-element.50), channel_id=1, source_target_pairs={{0,2},{8,24},{1,3},{9,25},{2,0},{10,26},{3,1},{11,27},{32,34},{40,... | collective-permute-start | bytes 1572872 | tf_op jit(solution)/shard_map/ppermute | solution.py:46
  47.2 20.6 %collective-permute-start.13 = (bf16[2048,128]{1,0:T(8,128)(2,1)}, bf16[2048,128]{1,0:T(8,128)(2,1)S(1)}, u32[]{:S(2)}, u32[]{:S(2)}) collective-permute-start(bf16[2048,128]{1,0:T(8,128)(2,1)} %get-tuple-element.50), channel_id=1, source_target_pairs={{0,3},{8,28},{1,0},{9,29},{2,1},{10,30},{3,2},{11,31},{32,35},{40,... | collective-permute-start | bytes 1572872 | tf_op jit(solution)/shard_map/ppermute | solution.py:46
  48.5 15.4 %collective-permute-start.9 = (bf16[1024,128]{1,0:T(8,128)(2,1)}, bf16[1024,128]{1,0:T(8,128)(2,1)S(1)}, u32[]{:S(2)}, u32[]{:S(2)}) collective-permute-start(bf16[1024,128]{1,0:T(8,128)(2,1)} %get-tuple-element.49), channel_id=1, source_target_pairs={{0,16},{8,10},{1,17},{9,11},{2,18},{10,8},{3,19},{11,9},{32,48},{4... | collective-permute-start | bytes 786440 | tf_op jit(solution)/shard_map/ppermute | solution.py:46
  51.4 16.4 %collective-permute-start.10 = (bf16[1024,128]{1,0:T(8,128)(2,1)}, bf16[1024,128]{1,0:T(8,128)(2,1)S(1)}, u32[]{:S(2)}, u32[]{:S(2)}) collective-permute-start(bf16[1024,128]{1,0:T(8,128)(2,1)} %get-tuple-element.49), channel_id=1, source_target_pairs={{0,20},{8,11},{1,21},{9,8},{2,22},{10,9},{3,23},{11,10},{32,52},{4... | collective-permute-start | bytes 786440 | tf_op jit(solution)/shard_map/ppermute | solution.py:46
  63.9 28.7 %collective-permute-start.23 = (bf16[544,128]{1,0:T(8,128)(2,1)}, bf16[544,128]{1,0:T(8,128)(2,1)S(1)}, u32[]{:S(2)}, u32[]{:S(2)}) collective-permute-start(bf16[544,128]{1,0:T(8,128)(2,1)} %get-tuple-element.58), channel_id=1, source_target_pairs={{0,20},{8,11},{1,21},{9,8},{2,22},{10,9},{3,23},{11,10},{32,52},{4... | collective-permute-start | bytes 417800 | tf_op jit(solution)/shard_map/ppermute | solution.py:46
  87.2 13.5 %collective-permute-start.14 = (bf16[1088,128]{1,0:T(8,128)(2,1)}, bf16[1088,128]{1,0:T(8,128)(2,1)S(1)}, u32[]{:S(2)}, u32[]{:S(2)}) collective-permute-start(bf16[1088,128]{1,0:T(8,128)(2,1)} %get-tuple-element.52), channel_id=1, source_target_pairs={{0,20},{8,11},{1,21},{9,8},{2,22},{10,9},{3,23},{11,10},{32,52},{4... | collective-permute-start | bytes 835592 | tf_op jit(solution)/shard_map/ppermute | solution.py:46
  89.6 11.1 %collective-permute-start.15 = (bf16[1088,128]{1,0:T(8,128)(2,1)}, bf16[1088,128]{1,0:T(8,128)(2,1)S(1)}, u32[]{:S(2)}, u32[]{:S(2)}) collective-permute-start(bf16[1088,128]{1,0:T(8,128)(2,1)} %get-tuple-element.53), channel_id=1, source_target_pairs={{0,16},{8,10},{1,17},{9,11},{2,18},{10,8},{3,19},{11,9},{32,48},{4... | collective-permute-start | bytes 835592 | tf_op jit(solution)/shard_map/ppermute | solution.py:46
  89.9 10.9 %collective-permute-start.16 = (bf16[1088,128]{1,0:T(8,128)(2,1)}, bf16[1088,128]{1,0:T(8,128)(2,1)S(1)}, u32[]{:S(2)}, u32[]{:S(2)}) collective-permute-start(bf16[1088,128]{1,0:T(8,128)(2,1)} %get-tuple-element.54), channel_id=1, source_target_pairs={{0,4},{8,9},{1,5},{9,10},{2,6},{10,11},{3,7},{11,8},{32,36},{40,41... | collective-permute-start | bytes 835592 | tf_op jit(solution)/shard_map/ppermute | solution.py:46
  91.7 6.8 %collective-permute-start.24 = (bf16[544,128]{1,0:T(8,128)(2,1)S(1)}, bf16[544,128]{1,0:T(8,128)(2,1)S(1)}, u32[]{:S(2)}, u32[]{:S(2)}) collective-permute-start(bf16[544,128]{1,0:T(8,128)(2,1)S(1)} %copy-done.34), channel_id=1, source_target_pairs={{0,16},{8,10},{1,17},{9,11},{2,18},{10,8},{3,19},{11,9},{32,48},{4... | collective-permute-start | bytes 417800 | tf_op jit(solution)/shard_map/ppermute | solution.py:46
  92.6 8.1 %collective-permute-start.25 = (bf16[544,128]{1,0:T(8,128)(2,1)S(1)}, bf16[544,128]{1,0:T(8,128)(2,1)S(1)}, u32[]{:S(2)}, u32[]{:S(2)}) collective-permute-start(bf16[544,128]{1,0:T(8,128)(2,1)S(1)} %copy-done.33), channel_id=1, source_target_pairs={{0,4},{8,9},{1,5},{9,10},{2,6},{10,11},{3,7},{11,8},{32,36},{40,41... | collective-permute-start | bytes 417800 | tf_op jit(solution)/shard_map/ppermute | solution.py:46
  104.7 18.6 %collective-permute-start.26 = (bf16[64,384]{1,0:T(8,128)(2,1)}, bf16[64,384]{1,0:T(8,128)(2,1)S(1)}, u32[]{:S(2)}, u32[]{:S(2)}) collective-permute-start(bf16[64,384]{1,0:T(8,128)(2,1)} %get-tuple-element.62), channel_id=1, source_target_pairs={{0,8},{8,0},{1,9},{9,1},{2,10},{10,2},{3,11},{11,3},{32,40},{40,32... | collective-permute-start | bytes 147464 | tf_op jit(solution)/shard_map/ppermute | solution.py:46
  116.0 8.7 %collective-permute-start.27 = (bf16[64,384]{1,0:T(8,128)(2,1)}, bf16[64,384]{1,0:T(8,128)(2,1)S(1)}, u32[]{:S(2)}, u32[]{:S(2)}) collective-permute-start(bf16[64,384]{1,0:T(8,128)(2,1)} %get-tuple-element.63), channel_id=1, source_target_pairs={{0,96},{8,104},{1,97},{9,105},{2,98},{10,106},{3,99},{11,107},{32,... | collective-permute-start | bytes 147464 | tf_op jit(solution)/shard_map/ppermute | solution.py:46
  119.7 5.7 %collective-permute-start.28 = (bf16[64,384]{1,0:T(8,128)(2,1)}, bf16[64,384]{1,0:T(8,128)(2,1)S(1)}, u32[]{:S(2)}, u32[]{:S(2)}) collective-permute-start(bf16[64,384]{1,0:T(8,128)(2,1)} %get-tuple-element.64), channel_id=1, source_target_pairs={{0,104},{8,96},{1,105},{9,97},{2,106},{10,98},{3,107},{11,99},{32,... | collective-permute-start | bytes 147464 | tf_op jit(solution)/shard_map/ppermute | solution.py:46
  119.7 5.7 %collective-permute-start.29 = (bf16[64,384]{1,0:T(8,128)(2,1)}, bf16[64,384]{1,0:T(8,128)(2,1)S(1)}, u32[]{:S(2)}, u32[]{:S(2)}) collective-permute-start(bf16[64,384]{1,0:T(8,128)(2,1)} %get-tuple-element.65), channel_id=1, source_target_pairs={{0,64},{8,72},{1,65},{9,73},{2,66},{10,74},{3,67},{11,75},{32,96},... | collective-permute-start | bytes 147464 | tf_op jit(solution)/shard_map/ppermute | solution.py:46
  121.1 5.9 %collective-permute-start.30 = (bf16[64,384]{1,0:T(8,128)(2,1)}, bf16[64,384]{1,0:T(8,128)(2,1)S(1)}, u32[]{:S(2)}, u32[]{:S(2)}) collective-permute-start(bf16[64,384]{1,0:T(8,128)(2,1)} %get-tuple-element.66), channel_id=1, source_target_pairs={{0,72},{8,64},{1,73},{9,65},{2,74},{10,66},{3,75},{11,67},{32,104}... | collective-permute-start | bytes 147464 | tf_op jit(solution)/shard_map/ppermute | solution.py:46
  123.2 4.8 %collective-permute-start.31 = (bf16[64,384]{1,0:T(8,128)(2,1)}, bf16[64,384]{1,0:T(8,128)(2,1)S(1)}, u32[]{:S(2)}, u32[]{:S(2)}) collective-permute-start(bf16[64,384]{1,0:T(8,128)(2,1)} %get-tuple-element.67), channel_id=1, source_target_pairs={{0,32},{8,40},{1,33},{9,41},{2,34},{10,42},{3,35},{11,43},{32,64},... | collective-permute-start | bytes 147464 | tf_op jit(solution)/shard_map/ppermute | solution.py:46
  124.7 5.1 %collective-permute-start.32 = (bf16[64,384]{1,0:T(8,128)(2,1)}, bf16[64,384]{1,0:T(8,128)(2,1)S(1)}, u32[]{:S(2)}, u32[]{:S(2)}) collective-permute-start(bf16[64,384]{1,0:T(8,128)(2,1)} %get-tuple-element.68), channel_id=1, source_target_pairs={{0,40},{8,32},{1,41},{9,33},{2,42},{10,34},{3,43},{11,35},{32,72},... | collective-permute-start | bytes 147464 | tf_op jit(solution)/shard_map/ppermute | solution.py:46
  (37 other events, 209.5 us)

commit v2 on v1

--- a/solution.py
+++ b/solution.py
@@ -17,7 +17,7 @@
 RING = 4
 SET = GROUP * ROWS
 META = 32
-PARTS = ((0, 1), (2,))
+PARTS = ((0, 1, 2),)
 TILE = 2 * ROWS
 TILES = 16
 STEP = 4
@@ -60,12 +60,17 @@
     return jax.ShapeDtypeStruct((rows, columns), dtype)
 
 
-def pack_kernel(at_ref, q_ref, k_ref, v_ref, meta_ref, *out_refs):
+def pack_kernel(at_ref, mask_ref, q_ref, k_ref, v_ref, *out_refs):
+    lanes = lax.broadcasted_iota(jnp.int32, (16, WIDTH), 1)
+    meta = jnp.zeros((16, WIDTH), jnp.int32)
+    for t in range(SPANS):
+        meta = jnp.where(lanes == t, mask_ref[0, t], meta)
+    meta = meta.astype(jnp.float32).astype(jnp.bfloat16)
     for j in range(GROUP):
         columns = pl.ds(pl.multiple_of(at_ref[j] * WIDTH, HEAD_DIM), WIDTH)
         for i, ref in enumerate((q_ref, k_ref, v_ref)):
             out_refs[j][i * ROWS : (i + 1) * ROWS, :] = ref[:, columns]
-        out_refs[j][3 * ROWS :, :] = meta_ref[...]
+        out_refs[j][3 * ROWS :, :] = meta
 
 
 def spread_kernel(*refs):
@@ -294,12 +299,11 @@
     hops = [dict(dy=j // 2, core=j % 2) for j in range(GROUP)]
     backs = [dict(dy=-(j // 2), core=j % 2) for j in range(GROUP)]
 
-    meta = jnp.pad(block_mask.astype(jnp.bfloat16), ((0, 15), (0, WIDTH - SPANS)))
     packed = call(
         pack_kernel,
         [shape(3 * ROWS + 16, WIDTH)] * GROUP,
-        [SMEM, VMEM, VMEM, VMEM, VMEM],
-    )(target, queries[0], keys[0], values[0], meta)
+        [SMEM, SMEM, VMEM, VMEM, VMEM],
+    )(target, block_mask, queries[0], keys[0], values[0])
     shared = [packed[0]]
     for j in range(1, GROUP):
         shared.append(moved(packed[j], **hops[j]))

time: 133 us -> 122 us (0.917)
  the two profiles are of different devices: /device:TPU:33 before, /device:TPU:1 now
where the time goes in v2:
time: 122 us
  waiting for transfers between devices  44.5 us (36%)
  starting transfers between devices  35.6 us (29%)
  Pallas kernels  31.9 us (26%)
  local copies, waits for them, and re-layouts  4.21 us (3%)
  other arithmetic  3.95 us (3%)
  between operations  1.52 us (1%)
    ppermute x24, waiting for transfers between devices, moved(): return lax.ppermute(array, BOTH, pairs)  44.5 us
    ppermute x24, starting transfers between devices, moved(): return lax.ppermute(array, BOTH, pairs)  35.6 us
    pallas_call x1, Pallas kernels, attend(): call(functools.partial(attend_kernel, count), [shape(count * (SET + META)...  22.1 us
    unnamed x56, local copies, waits for them, and re-layouts  4.12 us
    pallas_call x1, Pallas kernels, local(): call(combine_kernel, [shape(ROWS, WIDTH)] * GROUP, [SMEM] + [VMEM] * len(...  2.93 us
    pallas_call x1, Pallas kernels, local(): call(spread_kernel, shapes + [shape(GROUP, HEAD_DIM, jnp.float32)], [VMEM...  2.59 us
  transfers between devices with their start and end apart: 24, of which 13 were waited for; matrix products, arithmetic and copies ran while one was open for 3% of the time, Pallas kernels for 0%

profile of v2, /device:TPU:1, one launch (start us, length us, event | category | flops | bytes accessed | tf_op | source)
XLA Modules:
  0.0 121.6 jit_solution(15897801414520730907)
XLA Ops:
  0.5 2.4 %shard_map.73 = (bf16[208,384]{1,0:T(8,128)(2,1)}, bf16[208,384]{1,0:T(8,128)(2,1)}, bf16[208,384]{1,0:T(8,128)(2,1)}, bf16[208,384]{1,0:T(8,128)(2,1)}, bf16[20...) custom-call(s32[8]{0:T(128)} %fusion.3.at_ref, ...), custom_call_target="tpu_custom_call" | custom-call | tf_op jit(solution)/shard_map/pallas_call | solution.py:302
  2.9 1.4 %collective-permute-start = (bf16[208,384]{1,0:T(8,128)(2,1)}, bf16[208,384]{1,0:T(8,128)(2,1)S(1)}, u32[]{:S(2)}, u32[]{:S(2)}) collective-permute-start(bf16[208,384]{1,0:T(8,128)(2,1)} %get-tuple-element.29), channel_id=1, source_target_pairs={{0,8},{8,0},{1,9},{9,1},{2,10},{10,2},{3,11},{11,3},{32,40},{40,32... | collective-permute-start | bytes 479240 | tf_op jit(solution)/shard_map/ppermute | solution.py:46
  4.3 1.4 %collective-permute-start.1 = (bf16[208,384]{1,0:T(8,128)(2,1)}, bf16[208,384]{1,0:T(8,128)(2,1)S(1)}, u32[]{:S(2)}, u32[]{:S(2)}) collective-permute-start(bf16[208,384]{1,0:T(8,128)(2,1)} %get-tuple-element.30), channel_id=1, source_target_pairs={{0,32},{8,40},{1,33},{9,41},{2,34},{10,42},{3,35},{11,43},{32,64},... | collective-permute-start | bytes 479240 | tf_op jit(solution)/shard_map/ppermute | solution.py:46
  5.7 1.5 %collective-permute-start.2 = (bf16[208,384]{1,0:T(8,128)(2,1)}, bf16[208,384]{1,0:T(8,128)(2,1)S(1)}, u32[]{:S(2)}, u32[]{:S(2)}) collective-permute-start(bf16[208,384]{1,0:T(8,128)(2,1)} %get-tuple-element.31), channel_id=1, source_target_pairs={{0,40},{8,32},{1,41},{9,33},{2,42},{10,34},{3,43},{11,35},{32,72},... | collective-permute-start | bytes 479240 | tf_op jit(solution)/shard_map/ppermute | solution.py:46
  7.2 1.2 collective-permute-start.3
  8.4 2.2 %collective-permute-start.4 = (bf16[208,384]{1,0:T(8,128)(2,1)}, bf16[208,384]{1,0:T(8,128)(2,1)S(1)}, u32[]{:S(2)}, u32[]{:S(2)}) collective-permute-start(bf16[208,384]{1,0:T(8,128)(2,1)} %get-tuple-element.33), channel_id=1, source_target_pairs={{0,72},{8,64},{1,73},{9,65},{2,74},{10,66},{3,75},{11,67},{32,104}... | collective-permute-start | bytes 479240 | tf_op jit(solution)/shard_map/ppermute | solution.py:46
  11.8 1.4 %collective-permute-start.5 = (bf16[208,384]{1,0:T(8,128)(2,1)}, bf16[208,384]{1,0:T(8,128)(2,1)S(1)}, u32[]{:S(2)}, u32[]{:S(2)}) collective-permute-start(bf16[208,384]{1,0:T(8,128)(2,1)} %get-tuple-element.34), channel_id=1, source_target_pairs={{0,96},{8,104},{1,97},{9,105},{2,98},{10,106},{3,99},{11,107},{32,... | collective-permute-start | bytes 479240 | tf_op jit(solution)/shard_map/ppermute | solution.py:46
  13.3 1.0 collective-permute-start.6
  15.2 4.4 %collective-permute-done.3.refs_4_ = bf16[208,384]{1,0:T(8,128)(2,1)S(1)} collective-permute-done((bf16[208,384]{1,0:T(8,128)(2,1)}, bf16[208,384]{1,0:T(8,128)(2,1)S(1)}, u32[]{:S(2)}, u32[]{:S(2)}) %collective-permute-start.3) | collective-permute-done | bytes 159776 | tf_op jit(solution)/shard_map/ppermute | solution.py:46
  19.5 3.6 %collective-permute-done.4.refs_5_ = bf16[208,384]{1,0:T(8,128)(2,1)S(1)} collective-permute-done((bf16[208,384]{1,0:T(8,128)(2,1)}, bf16[208,384]{1,0:T(8,128)(2,1)S(1)}, u32[]{:S(2)}, u32[]{:S(2)}) %collective-permute-start.4) | collective-permute-done | bytes 159776 | tf_op jit(solution)/shard_map/ppermute | solution.py:46
  24.7 2.6 %shard_map.74 = (bf16[1536,128]{1,0:T(8,128)(2,1)}, bf16[3072,128]{1,0:T(8,128)(2,1)}, f32[8,128]{1,0:T(8,128)}) custom-call(bf16[208,384]{1,0:T(8,128)(2,1)} %get-tuple-element.28.refs_0_, bf16[208,384]{1,0:T(8,128)(2,1)} %copy-done.9, bf16[208,384]{1,0:T(8,128)(2,1)} %copy-done.10, bf16[208,384]{1,0:T(8,128)(2,1)} %copy-done.11, ...), custom_call_target="tpu_custom_call" | custom-call | tf_op jit(solution)/shard_map/pallas_call | solution.py:314
  27.3 1.6 %collective-permute-start.8 = (bf16[1536,128]{1,0:T(8,128)(2,1)}, bf16[1536,128]{1,0:T(8,128)(2,1)S(1)}, u32[]{:S(2)}, u32[]{:S(2)}) collective-permute-start(bf16[1536,128]{1,0:T(8,128)(2,1)} %get-tuple-element.37), channel_id=1, source_target_pairs={{0,4},{8,9},{1,5},{9,10},{2,6},{10,11},{3,7},{11,8},{32,36},{40,41... | collective-permute-start | bytes 1179656 | tf_op jit(solution)/shard_map/ppermute | solution.py:46
  29.0 2.7 %collective-permute-start.7 = (f32[8,128]{1,0:T(8,128)}, f32[8,128]{1,0:T(8,128)S(1)}, u32[]{:S(2)}, u32[]{:S(2)}) collective-permute-start(f32[8,128]{1,0:T(8,128)} %get-tuple-element.36), channel_id=1, source_target_pairs={{0,16},{8,24},{1,17},{9,25},{2,18},{10,26},{3,19},{11,27},{32,48},... | collective-permute-start | bytes 12296 | tf_op jit(solution)/shard_map/ppermute | solution.py:46
  32.0 1.7 %collective-permute-start.12 = (bf16[3072,128]{1,0:T(8,128)(2,1)}, bf16[3072,128]{1,0:T(8,128)(2,1)S(1)}, u32[]{:S(2)}, u32[]{:S(2)}) collective-permute-start(bf16[3072,128]{1,0:T(8,128)(2,1)} %get-tuple-element.38), channel_id=1, source_target_pairs={{0,2},{8,24},{1,3},{9,25},{2,0},{10,26},{3,1},{11,27},{32,34},{40,... | collective-permute-start | bytes 2359304 | tf_op jit(solution)/shard_map/ppermute | solution.py:46
  34.5 3.3 %collective-permute-start.9 = (bf16[1536,128]{1,0:T(8,128)(2,1)}, bf16[1536,128]{1,0:T(8,128)(2,1)S(1)}, u32[]{:S(2)}, u32[]{:S(2)}) collective-permute-start(bf16[1536,128]{1,0:T(8,128)(2,1)} %get-tuple-element.37), channel_id=1, source_target_pairs={{0,16},{8,10},{1,17},{9,11},{2,18},{10,8},{3,19},{11,9},{32,48},{4... | collective-permute-start | bytes 1179656 | tf_op jit(solution)/shard_map/ppermute | solution.py:46
  42.3 5.4 %collective-permute-done.9 = bf16[1536,128]{1,0:T(8,128)(2,1)S(1)} collective-permute-done((bf16[1536,128]{1,0:T(8,128)(2,1)}, bf16[1536,128]{1,0:T(8,128)(2,1)S(1)}, u32[]{:S(2)}, u32[]{:S(2)}) %collective-permute-start.9) | collective-permute-done | bytes 393248 | tf_op jit(solution)/shard_map/ppermute | solution.py:46
  47.7 10.4 %collective-permute-done.10 = bf16[1536,128]{1,0:T(8,128)(2,1)S(1)} collective-permute-done((bf16[1536,128]{1,0:T(8,128)(2,1)}, bf16[1536,128]{1,0:T(8,128)(2,1)S(1)}, u32[]{:S(2)}, u32[]{:S(2)}) %collective-permute-start.10) | collective-permute-done | bytes 393248 | tf_op jit(solution)/shard_map/ppermute | solution.py:46
  58.3 3.4 %collective-permute-done.13 = bf16[3072,128]{1,0:T(8,128)(2,1)S(1)} collective-permute-done((bf16[3072,128]{1,0:T(8,128)(2,1)}, bf16[3072,128]{1,0:T(8,128)(2,1)S(1)}, u32[]{:S(2)}, u32[]{:S(2)}) %collective-permute-start.13) | collective-permute-done | bytes 786464 | tf_op jit(solution)/shard_map/ppermute | solution.py:46
  62.6 22.1 %shard_map.75 = (bf16[1632,128]{1,0:T(8,128)(2,1)}, bf16[1632,128]{1,0:T(8,128)(2,1)}, bf16[1632,128]{1,0:T(8,128)(2,1)}, bf16[1632,128]{1,0:T(8,128)(2,1)}) custom-call(s32[280]{0:T(512)} %pad_add_fusion.table_ref, bf16[3,8,64,128]{3,2,1,0:T(8,128)(2,1)} %bitcast.20, bf16[3,8,64,128]{3,2,1,0:T(8,128)(2,1)} %bitcast.21, bf16[3,8,64,128]{3,2,1,0:T(8,128)(2,1)} %bitcast.22, ...), custom_call_target="tpu_custom_call" | custom-call | tf_op jit(solution)/shard_map/pallas_call | solution.py:225
  84.7 2.2 %collective-permute-start.14 = (bf16[1632,128]{1,0:T(8,128)(2,1)}, bf16[1632,128]{1,0:T(8,128)(2,1)S(1)}, u32[]{:S(2)}, u32[]{:S(2)}) collective-permute-start(bf16[1632,128]{1,0:T(8,128)(2,1)} %get-tuple-element.40), channel_id=1, source_target_pairs={{0,20},{8,11},{1,21},{9,8},{2,22},{10,9},{3,23},{11,10},{32,52},{4... | collective-permute-start | bytes 1253384 | tf_op jit(solution)/shard_map/ppermute | solution.py:46
  86.9 1.3 %collective-permute-start.15 = (bf16[1632,128]{1,0:T(8,128)(2,1)}, bf16[1632,128]{1,0:T(8,128)(2,1)S(1)}, u32[]{:S(2)}, u32[]{:S(2)}) collective-permute-start(bf16[1632,128]{1,0:T(8,128)(2,1)} %get-tuple-element.41), channel_id=1, source_target_pairs={{0,16},{8,10},{1,17},{9,11},{2,18},{10,8},{3,19},{11,9},{32,48},{4... | collective-permute-start | bytes 1253384 | tf_op jit(solution)/shard_map/ppermute | solution.py:46
  88.9 7.8 %collective-permute-done.14.refs_1_ = bf16[1632,128]{1,0:T(8,128)(2,1)S(1)} collective-permute-done((bf16[1632,128]{1,0:T(8,128)(2,1)}, bf16[1632,128]{1,0:T(8,128)(2,1)S(1)}, u32[]{:S(2)}, u32[]{:S(2)}) %collective-permute-start.14) | collective-permute-done | bytes 417824 | tf_op jit(solution)/shard_map/ppermute | solution.py:46
  96.7 3.6 %collective-permute-done.16.refs_3_ = bf16[1632,128]{1,0:T(8,128)(2,1)S(1)} collective-permute-done((bf16[1632,128]{1,0:T(8,128)(2,1)}, bf16[1632,128]{1,0:T(8,128)(2,1)S(1)}, u32[]{:S(2)}, u32[]{:S(2)}) %collective-permute-start.16) | collective-permute-done | bytes 417824 | tf_op jit(solution)/shard_map/ppermute | solution.py:46
  101.0 2.9 %shard_map.76 = (bf16[64,384]{1,0:T(8,128)(2,1)}, bf16[64,384]{1,0:T(8,128)(2,1)}, bf16[64,384]{1,0:T(8,128)(2,1)}, bf16[64,384]{1,0:T(8,128)(2,1)}, bf16[64,384...) custom-call(s32[280]{0:T(512)} %pad_add_fusion.table_ref, ...), custom_call_target="tpu_custom_call" | custom-call | tf_op jit(solution)/shard_map/pallas_call | solution.py:351
  104.0 2.1 %collective-permute-start.17 = (bf16[64,384]{1,0:T(8,128)(2,1)}, bf16[64,384]{1,0:T(8,128)(2,1)S(1)}, u32[]{:S(2)}, u32[]{:S(2)}) collective-permute-start(bf16[64,384]{1,0:T(8,128)(2,1)} %get-tuple-element.44), channel_id=1, source_target_pairs={{0,8},{8,0},{1,9},{9,1},{2,10},{10,2},{3,11},{11,3},{32,40},{40,32... | collective-permute-start | bytes 147464 | tf_op jit(solution)/shard_map/ppermute | solution.py:46
  106.0 2.9 %collective-permute-start.18 = (bf16[64,384]{1,0:T(8,128)(2,1)}, bf16[64,384]{1,0:T(8,128)(2,1)S(1)}, u32[]{:S(2)}, u32[]{:S(2)}) collective-permute-start(bf16[64,384]{1,0:T(8,128)(2,1)} %get-tuple-element.45), channel_id=1, source_target_pairs={{0,96},{8,104},{1,97},{9,105},{2,98},{10,106},{3,99},{11,107},{32,... | collective-permute-start | bytes 147464 | tf_op jit(solution)/shard_map/ppermute | solution.py:46
  109.2 1.3 %collective-permute-start.20 = (bf16[64,384]{1,0:T(8,128)(2,1)}, bf16[64,384]{1,0:T(8,128)(2,1)S(1)}, u32[]{:S(2)}, u32[]{:S(2)}) collective-permute-start(bf16[64,384]{1,0:T(8,128)(2,1)} %get-tuple-element.47), channel_id=1, source_target_pairs={{0,64},{8,72},{1,65},{9,73},{2,66},{10,74},{3,67},{11,75},{32,96},... | collective-permute-start | bytes 147464 | tf_op jit(solution)/shard_map/ppermute | solution.py:46
  110.5 2.1 %collective-permute-start.21 = (bf16[64,384]{1,0:T(8,128)(2,1)}, bf16[64,384]{1,0:T(8,128)(2,1)S(1)}, u32[]{:S(2)}, u32[]{:S(2)}) collective-permute-start(bf16[64,384]{1,0:T(8,128)(2,1)} %get-tuple-element.48), channel_id=1, source_target_pairs={{0,72},{8,64},{1,73},{9,65},{2,74},{10,66},{3,75},{11,67},{32,104}... | collective-permute-start | bytes 147464 | tf_op jit(solution)/shard_map/ppermute | solution.py:46
  112.5 1.5 %collective-permute-start.22 = (bf16[64,384]{1,0:T(8,128)(2,1)}, bf16[64,384]{1,0:T(8,128)(2,1)S(1)}, u32[]{:S(2)}, u32[]{:S(2)}) collective-permute-start(bf16[64,384]{1,0:T(8,128)(2,1)} %get-tuple-element.49), channel_id=1, source_target_pairs={{0,32},{8,40},{1,33},{9,41},{2,34},{10,42},{3,35},{11,43},{32,64},... | collective-permute-start | bytes 147464 | tf_op jit(solution)/shard_map/ppermute | solution.py:46
  114.7 1.7 %collective-permute-done.21.refs_5_ = bf16[64,384]{1,0:T(8,128)(2,1)S(1)} collective-permute-done((bf16[64,384]{1,0:T(8,128)(2,1)}, bf16[64,384]{1,0:T(8,128)(2,1)S(1)}, u32[]{:S(2)}, u32[]{:S(2)}) %collective-permute-start.21) | collective-permute-done | bytes 49184 | tf_op jit(solution)/shard_map/ppermute | solution.py:46
  117.2 1.9 %collective-permute-done.23.refs_7_ = bf16[64,384]{1,0:T(8,128)(2,1)S(1)} collective-permute-done((bf16[64,384]{1,0:T(8,128)(2,1)}, bf16[64,384]{1,0:T(8,128)(2,1)S(1)}, u32[]{:S(2)}, u32[]{:S(2)}) %collective-permute-start.23) | collective-permute-done | bytes 49184 | tf_op jit(solution)/shard_map/ppermute | solution.py:46
  119.7 1.9 %shard_map.77 = bf16[64,3072]{1,0:T(8,128)(2,1)} custom-call(s32[8]{0:T(128)} %fusion.3.at_ref, s32[1]{0:T(128)S(6)} %copy.8.level_ref, f32[16,3072]{1,0:T(8,128)} %gates_ref.1, bf16[64,384]{1,0:T(8,128)(2,1)} %get-tuple-element.43.refs_0_, bf16[64,384]{1,0:T(8,128)(2,1)} %copy-done.16, bf16[64,384]{1,0:T(8,128)(2,1)} %copy-done.17, ...), custom_call_target="tpu_custom_call" | custom-call | tf_op jit(solution)/shard_map/pallas_call | solution.py:357
  (92 shorter events, 13.2 us)
Async XLA Ops:
  2.9 8.9 %collective-permute-start = (bf16[208,384]{1,0:T(8,128)(2,1)}, bf16[208,384]{1,0:T(8,128)(2,1)S(1)}, u32[]{:S(2)}, u32[]{:S(2)}) collective-permute-start(bf16[208,384]{1,0:T(8,128)(2,1)} %get-tuple-element.29), channel_id=1, source_target_pairs={{0,8},{8,0},{1,9},{9,1},{2,10},{10,2},{3,11},{11,3},{32,40},{40,32... | collective-permute-start | bytes 479240 | tf_op jit(solution)/shard_map/ppermute | solution.py:46
  4.3 9.0 %collective-permute-start.1 = (bf16[208,384]{1,0:T(8,128)(2,1)}, bf16[208,384]{1,0:T(8,128)(2,1)S(1)}, u32[]{:S(2)}, u32[]{:S(2)}) collective-permute-start(bf16[208,384]{1,0:T(8,128)(2,1)} %get-tuple-element.30), channel_id=1, source_target_pairs={{0,32},{8,40},{1,33},{9,41},{2,34},{10,42},{3,35},{11,43},{32,64},... | collective-permute-start | bytes 479240 | tf_op jit(solution)/shard_map/ppermute | solution.py:46
  5.7 9.4 %collective-permute-start.2 = (bf16[208,384]{1,0:T(8,128)(2,1)}, bf16[208,384]{1,0:T(8,128)(2,1)S(1)}, u32[]{:S(2)}, u32[]{:S(2)}) collective-permute-start(bf16[208,384]{1,0:T(8,128)(2,1)} %get-tuple-element.31), channel_id=1, source_target_pairs={{0,40},{8,32},{1,41},{9,33},{2,42},{10,34},{3,43},{11,35},{32,72},... | collective-permute-start | bytes 479240 | tf_op jit(solution)/shard_map/ppermute | solution.py:46
  7.2 12.3 %collective-permute-start.3 = (bf16[208,384]{1,0:T(8,128)(2,1)}, bf16[208,384]{1,0:T(8,128)(2,1)S(1)}, u32[]{:S(2)}, u32[]{:S(2)}) collective-permute-start(bf16[208,384]{1,0:T(8,128)(2,1)} %get-tuple-element.32), channel_id=1, source_target_pairs={{0,64},{8,72},{1,65},{9,73},{2,66},{10,74},{3,67},{11,75},{32,96},... | collective-permute-start | bytes 479240 | tf_op jit(solution)/shard_map/ppermute | solution.py:46
  8.4 14.8 %collective-permute-start.4 = (bf16[208,384]{1,0:T(8,128)(2,1)}, bf16[208,384]{1,0:T(8,128)(2,1)S(1)}, u32[]{:S(2)}, u32[]{:S(2)}) collective-permute-start(bf16[208,384]{1,0:T(8,128)(2,1)} %get-tuple-element.33), channel_id=1, source_target_pairs={{0,72},{8,64},{1,73},{9,65},{2,74},{10,66},{3,75},{11,67},{32,104}... | collective-permute-start | bytes 479240 | tf_op jit(solution)/shard_map/ppermute | solution.py:46
  11.8 12.3 %copy-start.9 = (bf16[208,384]{1,0:T(8,128)(2,1)}, bf16[208,384]{1,0:T(8,128)(2,1)S(1)}, u32[]{:S(2)}) copy-start(bf16[208,384]{1,0:T(8,128)(2,1)S(1)} %collective-permute-done.refs_1_) | copy-start | bytes 479236
  11.8 11.4 %collective-permute-start.5 = (bf16[208,384]{1,0:T(8,128)(2,1)}, bf16[208,384]{1,0:T(8,128)(2,1)S(1)}, u32[]{:S(2)}, u32[]{:S(2)}) collective-permute-start(bf16[208,384]{1,0:T(8,128)(2,1)} %get-tuple-element.34), channel_id=1, source_target_pairs={{0,96},{8,104},{1,97},{9,105},{2,98},{10,106},{3,99},{11,107},{32,... | collective-permute-start | bytes 479240 | tf_op jit(solution)/shard_map/ppermute | solution.py:46
  13.3 10.8 %copy-start.10 = (bf16[208,384]{1,0:T(8,128)(2,1)}, bf16[208,384]{1,0:T(8,128)(2,1)S(1)}, u32[]{:S(2)}) copy-start(bf16[208,384]{1,0:T(8,128)(2,1)S(1)} %collective-permute-done.1.refs_2_) | copy-start | bytes 479236
  13.3 10.8 %collective-permute-start.6 = (bf16[208,384]{1,0:T(8,128)(2,1)}, bf16[208,384]{1,0:T(8,128)(2,1)S(1)}, u32[]{:S(2)}, u32[]{:S(2)}) collective-permute-start(bf16[208,384]{1,0:T(8,128)(2,1)} %get-tuple-element.35), channel_id=1, source_target_pairs={{0,104},{8,96},{1,105},{9,97},{2,106},{10,98},{3,107},{11,99},{32,... | collective-permute-start | bytes 479240 | tf_op jit(solution)/shard_map/ppermute | solution.py:46
  15.2 8.9 %copy-start.11 = (bf16[208,384]{1,0:T(8,128)(2,1)}, bf16[208,384]{1,0:T(8,128)(2,1)S(1)}, u32[]{:S(2)}) copy-start(bf16[208,384]{1,0:T(8,128)(2,1)S(1)} %collective-permute-done.2.refs_3_) | copy-start | bytes 479236
  27.3 10.7 %collective-permute-start.8 = (bf16[1536,128]{1,0:T(8,128)(2,1)}, bf16[1536,128]{1,0:T(8,128)(2,1)S(1)}, u32[]{:S(2)}, u32[]{:S(2)}) collective-permute-start(bf16[1536,128]{1,0:T(8,128)(2,1)} %get-tuple-element.37), channel_id=1, source_target_pairs={{0,4},{8,9},{1,5},{9,10},{2,6},{10,11},{3,7},{11,8},{32,36},{40,41... | collective-permute-start | bytes 1179656 | tf_op jit(solution)/shard_map/ppermute | solution.py:46
  29.0 5.5 %collective-permute-start.7 = (f32[8,128]{1,0:T(8,128)}, f32[8,128]{1,0:T(8,128)S(1)}, u32[]{:S(2)}, u32[]{:S(2)}) collective-permute-start(f32[8,128]{1,0:T(8,128)} %get-tuple-element.36), channel_id=1, source_target_pairs={{0,16},{8,24},{1,17},{9,25},{2,18},{10,26},{3,19},{11,27},{32,48},... | collective-permute-start | bytes 12296 | tf_op jit(solution)/shard_map/ppermute | solution.py:46
  31.7 6.1 %copy-start.23 = (f32[8,128]{1,0:T(8,128)S(1)}, f32[8,128]{1,0:T(8,128)}, u32[]{:S(2)}) copy-start(f32[8,128]{1,0:T(8,128)} %get-tuple-element.36) | copy-start | bytes 12292
  31.7 26.4 %collective-permute-start.11 = (bf16[3072,128]{1,0:T(8,128)(2,1)}, bf16[3072,128]{1,0:T(8,128)(2,1)S(1)}, u32[]{:S(2)}, u32[]{:S(2)}) collective-permute-start(bf16[3072,128]{1,0:T(8,128)(2,1)} %get-tuple-element.38), channel_id=1, source_target_pairs={{0,1},{8,12},{1,2},{9,13},{2,3},{10,14},{3,0},{11,15},{32,33},{40,... | collective-permute-start | bytes 2359304 | tf_op jit(solution)/shard_map/ppermute | solution.py:46
  32.0 26.3 %collective-permute-start.12 = (bf16[3072,128]{1,0:T(8,128)(2,1)}, bf16[3072,128]{1,0:T(8,128)(2,1)S(1)}, u32[]{:S(2)}, u32[]{:S(2)}) collective-permute-start(bf16[3072,128]{1,0:T(8,128)(2,1)} %get-tuple-element.38), channel_id=1, source_target_pairs={{0,2},{8,24},{1,3},{9,25},{2,0},{10,26},{3,1},{11,27},{32,34},{40,... | collective-permute-start | bytes 2359304 | tf_op jit(solution)/shard_map/ppermute | solution.py:46
  33.8 28.0 %collective-permute-start.13 = (bf16[3072,128]{1,0:T(8,128)(2,1)}, bf16[3072,128]{1,0:T(8,128)(2,1)S(1)}, u32[]{:S(2)}, u32[]{:S(2)}) collective-permute-start(bf16[3072,128]{1,0:T(8,128)(2,1)} %get-tuple-element.38), channel_id=1, source_target_pairs={{0,3},{8,28},{1,0},{9,29},{2,1},{10,30},{3,2},{11,31},{32,35},{40,... | collective-permute-start | bytes 2359304 | tf_op jit(solution)/shard_map/ppermute | solution.py:46
  34.5 13.2 %collective-permute-start.9 = (bf16[1536,128]{1,0:T(8,128)(2,1)}, bf16[1536,128]{1,0:T(8,128)(2,1)S(1)}, u32[]{:S(2)}, u32[]{:S(2)}) collective-permute-start(bf16[1536,128]{1,0:T(8,128)(2,1)} %get-tuple-element.37), channel_id=1, source_target_pairs={{0,16},{8,10},{1,17},{9,11},{2,18},{10,8},{3,19},{11,9},{32,48},{4... | collective-permute-start | bytes 1179656 | tf_op jit(solution)/shard_map/ppermute | solution.py:46
  38.0 23.7 %copy-start.6 = (bf16[1536,128]{1,0:T(8,128)(2,1)}, bf16[1536,128]{1,0:T(8,128)(2,1)S(1)}, u32[]{:S(2)}) copy-start(bf16[1536,128]{1,0:T(8,128)(2,1)S(1)} %collective-permute-done.8) | copy-start | bytes 1179652
  38.0 20.1 %collective-permute-start.10 = (bf16[1536,128]{1,0:T(8,128)(2,1)}, bf16[1536,128]{1,0:T(8,128)(2,1)S(1)}, u32[]{:S(2)}, u32[]{:S(2)}) collective-permute-start(bf16[1536,128]{1,0:T(8,128)(2,1)} %get-tuple-element.37), channel_id=1, source_target_pairs={{0,20},{8,11},{1,21},{9,8},{2,22},{10,9},{3,23},{11,10},{32,52},{4... | collective-permute-start | bytes 1179656 | tf_op jit(solution)/shard_map/ppermute | solution.py:46
  47.7 14.1 %copy-start.7 = (bf16[1536,128]{1,0:T(8,128)(2,1)}, bf16[1536,128]{1,0:T(8,128)(2,1)S(1)}, u32[]{:S(2)}) copy-start(bf16[1536,128]{1,0:T(8,128)(2,1)S(1)} %collective-permute-done.9) | copy-start | bytes 1179652
  84.7 12.0 %collective-permute-start.14 = (bf16[1632,128]{1,0:T(8,128)(2,1)}, bf16[1632,128]{1,0:T(8,128)(2,1)S(1)}, u32[]{:S(2)}, u32[]{:S(2)}) collective-permute-start(bf16[1632,128]{1,0:T(8,128)(2,1)} %get-tuple-element.40), channel_id=1, source_target_pairs={{0,20},{8,11},{1,21},{9,8},{2,22},{10,9},{3,23},{11,10},{32,52},{4... | collective-permute-start | bytes 1253384 | tf_op jit(solution)/shard_map/ppermute | solution.py:46
  86.9 9.8 %collective-permute-start.15 = (bf16[1632,128]{1,0:T(8,128)(2,1)}, bf16[1632,128]{1,0:T(8,128)(2,1)S(1)}, u32[]{:S(2)}, u32[]{:S(2)}) collective-permute-start(bf16[1632,128]{1,0:T(8,128)(2,1)} %get-tuple-element.41), channel_id=1, source_target_pairs={{0,16},{8,10},{1,17},{9,11},{2,18},{10,8},{3,19},{11,9},{32,48},{4... | collective-permute-start | bytes 1253384 | tf_op jit(solution)/shard_map/ppermute | solution.py:46
  88.2 12.1 %collective-permute-start.16 = (bf16[1632,128]{1,0:T(8,128)(2,1)}, bf16[1632,128]{1,0:T(8,128)(2,1)S(1)}, u32[]{:S(2)}, u32[]{:S(2)}) collective-permute-start(bf16[1632,128]{1,0:T(8,128)(2,1)} %get-tuple-element.42), channel_id=1, source_target_pairs={{0,4},{8,9},{1,5},{9,10},{2,6},{10,11},{3,7},{11,8},{32,36},{40,41... | collective-permute-start | bytes 1253384 | tf_op jit(solution)/shard_map/ppermute | solution.py:46
  104.0 8.6 %collective-permute-start.17 = (bf16[64,384]{1,0:T(8,128)(2,1)}, bf16[64,384]{1,0:T(8,128)(2,1)S(1)}, u32[]{:S(2)}, u32[]{:S(2)}) collective-permute-start(bf16[64,384]{1,0:T(8,128)(2,1)} %get-tuple-element.44), channel_id=1, source_target_pairs={{0,8},{8,0},{1,9},{9,1},{2,10},{10,2},{3,11},{11,3},{32,40},{40,32... | collective-permute-start | bytes 147464 | tf_op jit(solution)/shard_map/ppermute | solution.py:46
  106.0 7.9 %collective-permute-start.18 = (bf16[64,384]{1,0:T(8,128)(2,1)}, bf16[64,384]{1,0:T(8,128)(2,1)S(1)}, u32[]{:S(2)}, u32[]{:S(2)}) collective-permute-start(bf16[64,384]{1,0:T(8,128)(2,1)} %get-tuple-element.45), channel_id=1, source_target_pairs={{0,96},{8,104},{1,97},{9,105},{2,98},{10,106},{3,99},{11,107},{32,... | collective-permute-start | bytes 147464 | tf_op jit(solution)/shard_map/ppermute | solution.py:46
  109.0 5.7 %collective-permute-start.19 = (bf16[64,384]{1,0:T(8,128)(2,1)}, bf16[64,384]{1,0:T(8,128)(2,1)S(1)}, u32[]{:S(2)}, u32[]{:S(2)}) collective-permute-start(bf16[64,384]{1,0:T(8,128)(2,1)} %get-tuple-element.46), channel_id=1, source_target_pairs={{0,104},{8,96},{1,105},{9,97},{2,106},{10,98},{3,107},{11,99},{32,... | collective-permute-start | bytes 147464 | tf_op jit(solution)/shard_map/ppermute | solution.py:46
  109.2 5.5 %collective-permute-start.20 = (bf16[64,384]{1,0:T(8,128)(2,1)}, bf16[64,384]{1,0:T(8,128)(2,1)S(1)}, u32[]{:S(2)}, u32[]{:S(2)}) collective-permute-start(bf16[64,384]{1,0:T(8,128)(2,1)} %get-tuple-element.47), channel_id=1, source_target_pairs={{0,64},{8,72},{1,65},{9,73},{2,66},{10,74},{3,67},{11,75},{32,96},... | collective-permute-start | bytes 147464 | tf_op jit(solution)/shard_map/ppermute | solution.py:46
  110.5 6.0 %collective-permute-start.21 = (bf16[64,384]{1,0:T(8,128)(2,1)}, bf16[64,384]{1,0:T(8,128)(2,1)S(1)}, u32[]{:S(2)}, u32[]{:S(2)}) collective-permute-start(bf16[64,384]{1,0:T(8,128)(2,1)} %get-tuple-element.48), channel_id=1, source_target_pairs={{0,72},{8,64},{1,73},{9,65},{2,74},{10,66},{3,75},{11,67},{32,104}... | collective-permute-start | bytes 147464 | tf_op jit(solution)/shard_map/ppermute | solution.py:46
  112.5 6.6 %copy-start.16 = (bf16[64,384]{1,0:T(8,128)(2,1)}, bf16[64,384]{1,0:T(8,128)(2,1)S(1)}, u32[]{:S(2)}) copy-start(bf16[64,384]{1,0:T(8,128)(2,1)S(1)} %collective-permute-done.17.refs_1_) | copy-start | bytes 147460
  112.5 4.7 %collective-permute-start.22 = (bf16[64,384]{1,0:T(8,128)(2,1)}, bf16[64,384]{1,0:T(8,128)(2,1)S(1)}, u32[]{:S(2)}, u32[]{:S(2)}) collective-permute-start(bf16[64,384]{1,0:T(8,128)(2,1)} %get-tuple-element.49), channel_id=1, source_target_pairs={{0,32},{8,40},{1,33},{9,41},{2,34},{10,42},{3,35},{11,43},{32,64},... | collective-permute-start | bytes 147464 | tf_op jit(solution)/shard_map/ppermute | solution.py:46
  114.0 5.1 %copy-start.17 = (bf16[64,384]{1,0:T(8,128)(2,1)}, bf16[64,384]{1,0:T(8,128)(2,1)S(1)}, u32[]{:S(2)}) copy-start(bf16[64,384]{1,0:T(8,128)(2,1)S(1)} %collective-permute-done.18.refs_2_) | copy-start | bytes 147460
  114.0 5.1 %collective-permute-start.23 = (bf16[64,384]{1,0:T(8,128)(2,1)}, bf16[64,384]{1,0:T(8,128)(2,1)S(1)}, u32[]{:S(2)}, u32[]{:S(2)}) collective-permute-start(bf16[64,384]{1,0:T(8,128)(2,1)} %get-tuple-element.50), channel_id=1, source_target_pairs={{0,40},{8,32},{1,41},{9,33},{2,42},{10,34},{3,43},{11,35},{32,72},... | collective-permute-start | bytes 147464 | tf_op jit(solution)/shard_map/ppermute | solution.py:46
  (20 other events, 43.1 us)

commit v3 on v2

--- a/solution.py
+++ b/solution.py
@@ -107,26 +107,27 @@
     q_place = [table_ref[limits + TILES + d] for d in range(RING)]
     k_place = [table_ref[limits + TILES + RING + d] for d in range(RING)]
     copies = []
-    for h in range(count):
-        for d in range(RING):
-            for n, (source, target, place) in enumerate(
-                (
+    for n in range(3):
+        for h in range(count):
+            for d in range(RING):
+                source, target, place = (
+                    (kv_refs[d].at[h, 1], v_all, k_place[d]),
+                    (kv_refs[d].at[h, 0], k_all, k_place[d]),
                     (q_refs[d].at[h], q_all, q_place[d]),
-                    (kv_refs[d].at[h, 0], k_all, k_place[d]),
-                    (kv_refs[d].at[h, 1], v_all, k_place[d]),
-                )
-            ):
+                )[n]
                 copy = pltpu.make_async_copy(
-                    source, target.at[h, :, place], sems.at[(h * RING + d) * 3 + n]
+                    source, target.at[h, :, place], sems.at[len(copies)]
                 )
                 copy.start()
                 copies.append(copy)
-    for copy in copies:
+    for copy in copies[: count * RING]:
         copy.wait()
     for h in range(count):
         for i in range(TILES):
             rows = slice(i * TILE, (i + 1) * TILE)
             v_turned[h, :, rows] = rows_of(v_all, h, i).T
+    for copy in copies[count * RING :]:
+        copy.wait()
 
     chains = [(t, h) for t in range(together) for h in range(count)]
 
@@ -319,7 +320,8 @@
     base = (y - tile // 4) % 4 * 4 + (core ^ tile // 2 % 2)
     wide_slots, near_slots = base + 2 * (tile % 2), base + 2 * half
     near_mask = jnp.repeat(spread[-1], 2, axis=0)
-    far_mask = jnp.repeat(moved(spread[-1], dx=2), 2, axis=0)
+    other_mask = moved(spread[-1], dx=2)
+    far_mask = jnp.repeat(other_mask, 2, axis=0)
     wide_mask = jnp.where((tile % 2 == half)[:, None], near_mask, far_mask)
     first = core == 0
     ring = jnp.arange(RING, dtype=jnp.int32)

time: 122 us -> 122 us (level)
  no operation moved by 1% of the time
where the time goes in v3:
time: 122 us; the launch traced here: 121 us
  waiting for transfers between devices  44.5 us (36%)
  starting transfers between devices  35.7 us (29%)
  Pallas kernels  31.7 us (26%)
  local copies, waits for them, and re-layouts  4.21 us (3%)
  other arithmetic  3.95 us (3%)
  between operations  1.52 us (1%)
    ppermute x24, waiting for transfers between devices, moved(): return lax.ppermute(array, BOTH, pairs)  44.5 us
    ppermute x24, starting transfers between devices, moved(): return lax.ppermute(array, BOTH, pairs)  35.7 us
    pallas_call x1, Pallas kernels, attend(): call(functools.partial(attend_kernel, count), [shape(count * (SET + META)...  21.8 us
    unnamed x56, local copies, waits for them, and re-layouts  4.12 us
    pallas_call x1, Pallas kernels, local(): call(combine_kernel, [shape(ROWS, WIDTH)] * GROUP, [SMEM] + [VMEM] * len(...  2.93 us
    pallas_call x1, Pallas kernels, local(): call(spread_kernel, shapes + [shape(GROUP, HEAD_DIM, jnp.float32)], [VMEM...  2.59 us
  transfers between devices with their start and end apart: 24, of which 13 were waited for; matrix products, arithmetic and copies ran while one was open for 3% of the time, Pallas kernels for 0%

profile of v3, /device:TPU:1, one launch (start us, length us, event | category | flops | bytes accessed | tf_op | source)
XLA Modules:
  0.0 121.4 jit_solution(15177924026056486380)
XLA Ops:
  0.5 2.4 %shard_map.73 = (bf16[208,384]{1,0:T(8,128)(2,1)}, bf16[208,384]{1,0:T(8,128)(2,1)}, bf16[208,384]{1,0:T(8,128)(2,1)}, bf16[208,384]{1,0:T(8,128)(2,1)}, bf16[20...) custom-call(s32[8]{0:T(128)} %fusion.3.at_ref, ...), custom_call_target="tpu_custom_call" | custom-call | tf_op jit(solution)/shard_map/pallas_call | solution.py:303
  2.9 1.4 %collective-permute-start = (bf16[208,384]{1,0:T(8,128)(2,1)}, bf16[208,384]{1,0:T(8,128)(2,1)S(1)}, u32[]{:S(2)}, u32[]{:S(2)}) collective-permute-start(bf16[208,384]{1,0:T(8,128)(2,1)} %get-tuple-element.29), channel_id=1, source_target_pairs={{0,8},{8,0},{1,9},{9,1},{2,10},{10,2},{3,11},{11,3},{32,40},{40,32... | collective-permute-start | bytes 479240 | tf_op jit(solution)/shard_map/ppermute | solution.py:46
  4.3 1.4 %collective-permute-start.1 = (bf16[208,384]{1,0:T(8,128)(2,1)}, bf16[208,384]{1,0:T(8,128)(2,1)S(1)}, u32[]{:S(2)}, u32[]{:S(2)}) collective-permute-start(bf16[208,384]{1,0:T(8,128)(2,1)} %get-tuple-element.30), channel_id=1, source_target_pairs={{0,32},{8,40},{1,33},{9,41},{2,34},{10,42},{3,35},{11,43},{32,64},... | collective-permute-start | bytes 479240 | tf_op jit(solution)/shard_map/ppermute | solution.py:46
  5.7 1.5 %collective-permute-start.2 = (bf16[208,384]{1,0:T(8,128)(2,1)}, bf16[208,384]{1,0:T(8,128)(2,1)S(1)}, u32[]{:S(2)}, u32[]{:S(2)}) collective-permute-start(bf16[208,384]{1,0:T(8,128)(2,1)} %get-tuple-element.31), channel_id=1, source_target_pairs={{0,40},{8,32},{1,41},{9,33},{2,42},{10,34},{3,43},{11,35},{32,72},... | collective-permute-start | bytes 479240 | tf_op jit(solution)/shard_map/ppermute | solution.py:46
  7.2 1.2 collective-permute-start.3
  8.4 2.2 %collective-permute-start.4 = (bf16[208,384]{1,0:T(8,128)(2,1)}, bf16[208,384]{1,0:T(8,128)(2,1)S(1)}, u32[]{:S(2)}, u32[]{:S(2)}) collective-permute-start(bf16[208,384]{1,0:T(8,128)(2,1)} %get-tuple-element.33), channel_id=1, source_target_pairs={{0,72},{8,64},{1,73},{9,65},{2,74},{10,66},{3,75},{11,67},{32,104}... | collective-permute-start | bytes 479240 | tf_op jit(solution)/shard_map/ppermute | solution.py:46
  11.8 1.4 %collective-permute-start.5 = (bf16[208,384]{1,0:T(8,128)(2,1)}, bf16[208,384]{1,0:T(8,128)(2,1)S(1)}, u32[]{:S(2)}, u32[]{:S(2)}) collective-permute-start(bf16[208,384]{1,0:T(8,128)(2,1)} %get-tuple-element.34), channel_id=1, source_target_pairs={{0,96},{8,104},{1,97},{9,105},{2,98},{10,106},{3,99},{11,107},{32,... | collective-permute-start | bytes 479240 | tf_op jit(solution)/shard_map/ppermute | solution.py:46
  13.3 1.0 collective-permute-start.6
  15.2 4.4 %collective-permute-done.3.refs_4_ = bf16[208,384]{1,0:T(8,128)(2,1)S(1)} collective-permute-done((bf16[208,384]{1,0:T(8,128)(2,1)}, bf16[208,384]{1,0:T(8,128)(2,1)S(1)}, u32[]{:S(2)}, u32[]{:S(2)}) %collective-permute-start.3) | collective-permute-done | bytes 159776 | tf_op jit(solution)/shard_map/ppermute | solution.py:46
  19.5 3.6 %collective-permute-done.4.refs_5_ = bf16[208,384]{1,0:T(8,128)(2,1)S(1)} collective-permute-done((bf16[208,384]{1,0:T(8,128)(2,1)}, bf16[208,384]{1,0:T(8,128)(2,1)S(1)}, u32[]{:S(2)}, u32[]{:S(2)}) %collective-permute-start.4) | collective-permute-done | bytes 159776 | tf_op jit(solution)/shard_map/ppermute | solution.py:46
  24.7 2.6 %shard_map.74 = (bf16[1536,128]{1,0:T(8,128)(2,1)}, bf16[3072,128]{1,0:T(8,128)(2,1)}, f32[8,128]{1,0:T(8,128)}) custom-call(bf16[208,384]{1,0:T(8,128)(2,1)} %get-tuple-element.28.refs_0_, bf16[208,384]{1,0:T(8,128)(2,1)} %copy-done.9, bf16[208,384]{1,0:T(8,128)(2,1)} %copy-done.10, bf16[208,384]{1,0:T(8,128)(2,1)} %copy-done.11, ...), custom_call_target="tpu_custom_call" | custom-call | tf_op jit(solution)/shard_map/pallas_call | solution.py:315
  27.3 1.6 %collective-permute-start.8 = (bf16[1536,128]{1,0:T(8,128)(2,1)}, bf16[1536,128]{1,0:T(8,128)(2,1)S(1)}, u32[]{:S(2)}, u32[]{:S(2)}) collective-permute-start(bf16[1536,128]{1,0:T(8,128)(2,1)} %get-tuple-element.37), channel_id=1, source_target_pairs={{0,4},{8,9},{1,5},{9,10},{2,6},{10,11},{3,7},{11,8},{32,36},{40,41... | collective-permute-start | bytes 1179656 | tf_op jit(solution)/shard_map/ppermute | solution.py:46
  29.0 2.7 %collective-permute-start.7 = (f32[8,128]{1,0:T(8,128)}, f32[8,128]{1,0:T(8,128)S(1)}, u32[]{:S(2)}, u32[]{:S(2)}) collective-permute-start(f32[8,128]{1,0:T(8,128)} %get-tuple-element.36), channel_id=1, source_target_pairs={{0,16},{8,24},{1,17},{9,25},{2,18},{10,26},{3,19},{11,27},{32,48},... | collective-permute-start | bytes 12296 | tf_op jit(solution)/shard_map/ppermute | solution.py:46
  32.0 1.7 %collective-permute-start.12 = (bf16[3072,128]{1,0:T(8,128)(2,1)}, bf16[3072,128]{1,0:T(8,128)(2,1)S(1)}, u32[]{:S(2)}, u32[]{:S(2)}) collective-permute-start(bf16[3072,128]{1,0:T(8,128)(2,1)} %get-tuple-element.38), channel_id=1, source_target_pairs={{0,2},{8,24},{1,3},{9,25},{2,0},{10,26},{3,1},{11,27},{32,34},{40,... | collective-permute-start | bytes 2359304 | tf_op jit(solution)/shard_map/ppermute | solution.py:46
  34.5 3.3 %collective-permute-start.9 = (bf16[1536,128]{1,0:T(8,128)(2,1)}, bf16[1536,128]{1,0:T(8,128)(2,1)S(1)}, u32[]{:S(2)}, u32[]{:S(2)}) collective-permute-start(bf16[1536,128]{1,0:T(8,128)(2,1)} %get-tuple-element.37), channel_id=1, source_target_pairs={{0,16},{8,10},{1,17},{9,11},{2,18},{10,8},{3,19},{11,9},{32,48},{4... | collective-permute-start | bytes 1179656 | tf_op jit(solution)/shard_map/ppermute | solution.py:46
  42.3 5.4 %collective-permute-done.9 = bf16[1536,128]{1,0:T(8,128)(2,1)S(1)} collective-permute-done((bf16[1536,128]{1,0:T(8,128)(2,1)}, bf16[1536,128]{1,0:T(8,128)(2,1)S(1)}, u32[]{:S(2)}, u32[]{:S(2)}) %collective-permute-start.9) | collective-permute-done | bytes 393248 | tf_op jit(solution)/shard_map/ppermute | solution.py:46
  47.7 10.4 %collective-permute-done.10 = bf16[1536,128]{1,0:T(8,128)(2,1)S(1)} collective-permute-done((bf16[1536,128]{1,0:T(8,128)(2,1)}, bf16[1536,128]{1,0:T(8,128)(2,1)S(1)}, u32[]{:S(2)}, u32[]{:S(2)}) %collective-permute-start.10) | collective-permute-done | bytes 393248 | tf_op jit(solution)/shard_map/ppermute | solution.py:46
  58.3 3.4 %collective-permute-done.13 = bf16[3072,128]{1,0:T(8,128)(2,1)S(1)} collective-permute-done((bf16[3072,128]{1,0:T(8,128)(2,1)}, bf16[3072,128]{1,0:T(8,128)(2,1)S(1)}, u32[]{:S(2)}, u32[]{:S(2)}) %collective-permute-start.13) | collective-permute-done | bytes 786464 | tf_op jit(solution)/shard_map/ppermute | solution.py:46
  62.6 21.8 %shard_map.75 = (bf16[1632,128]{1,0:T(8,128)(2,1)}, bf16[1632,128]{1,0:T(8,128)(2,1)}, bf16[1632,128]{1,0:T(8,128)(2,1)}, bf16[1632,128]{1,0:T(8,128)(2,1)}) custom-call(s32[280]{0:T(512)} %pad_add_fusion.table_ref, bf16[3,8,64,128]{3,2,1,0:T(8,128)(2,1)} %bitcast.20, bf16[3,8,64,128]{3,2,1,0:T(8,128)(2,1)} %bitcast.21, bf16[3,8,64,128]{3,2,1,0:T(8,128)(2,1)} %bitcast.22, ...), custom_call_target="tpu_custom_call" | custom-call | tf_op jit(solution)/shard_map/pallas_call | solution.py:226
  84.5 2.2 %collective-permute-start.14 = (bf16[1632,128]{1,0:T(8,128)(2,1)}, bf16[1632,128]{1,0:T(8,128)(2,1)S(1)}, u32[]{:S(2)}, u32[]{:S(2)}) collective-permute-start(bf16[1632,128]{1,0:T(8,128)(2,1)} %get-tuple-element.40), channel_id=1, source_target_pairs={{0,20},{8,11},{1,21},{9,8},{2,22},{10,9},{3,23},{11,10},{32,52},{4... | collective-permute-start | bytes 1253384 | tf_op jit(solution)/shard_map/ppermute | solution.py:46
  86.7 1.3 %collective-permute-start.15 = (bf16[1632,128]{1,0:T(8,128)(2,1)}, bf16[1632,128]{1,0:T(8,128)(2,1)S(1)}, u32[]{:S(2)}, u32[]{:S(2)}) collective-permute-start(bf16[1632,128]{1,0:T(8,128)(2,1)} %get-tuple-element.41), channel_id=1, source_target_pairs={{0,16},{8,10},{1,17},{9,11},{2,18},{10,8},{3,19},{11,9},{32,48},{4... | collective-permute-start | bytes 1253384 | tf_op jit(solution)/shard_map/ppermute | solution.py:46
  88.7 7.8 %collective-permute-done.14.refs_1_ = bf16[1632,128]{1,0:T(8,128)(2,1)S(1)} collective-permute-done((bf16[1632,128]{1,0:T(8,128)(2,1)}, bf16[1632,128]{1,0:T(8,128)(2,1)S(1)}, u32[]{:S(2)}, u32[]{:S(2)}) %collective-permute-start.14) | collective-permute-done | bytes 417824 | tf_op jit(solution)/shard_map/ppermute | solution.py:46
  96.5 3.6 %collective-permute-done.16.refs_3_ = bf16[1632,128]{1,0:T(8,128)(2,1)S(1)} collective-permute-done((bf16[1632,128]{1,0:T(8,128)(2,1)}, bf16[1632,128]{1,0:T(8,128)(2,1)S(1)}, u32[]{:S(2)}, u32[]{:S(2)}) %collective-permute-start.16) | collective-permute-done | bytes 417824 | tf_op jit(solution)/shard_map/ppermute | solution.py:46
  100.8 2.9 %shard_map.76 = (bf16[64,384]{1,0:T(8,128)(2,1)}, bf16[64,384]{1,0:T(8,128)(2,1)}, bf16[64,384]{1,0:T(8,128)(2,1)}, bf16[64,384]{1,0:T(8,128)(2,1)}, bf16[64,384...) custom-call(s32[280]{0:T(512)} %pad_add_fusion.table_ref, ...), custom_call_target="tpu_custom_call" | custom-call | tf_op jit(solution)/shard_map/pallas_call | solution.py:353
  103.7 2.1 %collective-permute-start.17 = (bf16[64,384]{1,0:T(8,128)(2,1)}, bf16[64,384]{1,0:T(8,128)(2,1)S(1)}, u32[]{:S(2)}, u32[]{:S(2)}) collective-permute-start(bf16[64,384]{1,0:T(8,128)(2,1)} %get-tuple-element.44), channel_id=1, source_target_pairs={{0,8},{8,0},{1,9},{9,1},{2,10},{10,2},{3,11},{11,3},{32,40},{40,32... | collective-permute-start | bytes 147464 | tf_op jit(solution)/shard_map/ppermute | solution.py:46
  105.8 2.9 %collective-permute-start.18 = (bf16[64,384]{1,0:T(8,128)(2,1)}, bf16[64,384]{1,0:T(8,128)(2,1)S(1)}, u32[]{:S(2)}, u32[]{:S(2)}) collective-permute-start(bf16[64,384]{1,0:T(8,128)(2,1)} %get-tuple-element.45), channel_id=1, source_target_pairs={{0,96},{8,104},{1,97},{9,105},{2,98},{10,106},{3,99},{11,107},{32,... | collective-permute-start | bytes 147464 | tf_op jit(solution)/shard_map/ppermute | solution.py:46
  108.9 1.3 %collective-permute-start.20 = (bf16[64,384]{1,0:T(8,128)(2,1)}, bf16[64,384]{1,0:T(8,128)(2,1)S(1)}, u32[]{:S(2)}, u32[]{:S(2)}) collective-permute-start(bf16[64,384]{1,0:T(8,128)(2,1)} %get-tuple-element.47), channel_id=1, source_target_pairs={{0,64},{8,72},{1,65},{9,73},{2,66},{10,74},{3,67},{11,75},{32,96},... | collective-permute-start | bytes 147464 | tf_op jit(solution)/shard_map/ppermute | solution.py:46
  110.2 2.1 %collective-permute-start.21 = (bf16[64,384]{1,0:T(8,128)(2,1)}, bf16[64,384]{1,0:T(8,128)(2,1)S(1)}, u32[]{:S(2)}, u32[]{:S(2)}) collective-permute-start(bf16[64,384]{1,0:T(8,128)(2,1)} %get-tuple-element.48), channel_id=1, source_target_pairs={{0,72},{8,64},{1,73},{9,65},{2,74},{10,66},{3,75},{11,67},{32,104}... | collective-permute-start | bytes 147464 | tf_op jit(solution)/shard_map/ppermute | solution.py:46
  112.3 1.5 %collective-permute-start.22 = (bf16[64,384]{1,0:T(8,128)(2,1)}, bf16[64,384]{1,0:T(8,128)(2,1)S(1)}, u32[]{:S(2)}, u32[]{:S(2)}) collective-permute-start(bf16[64,384]{1,0:T(8,128)(2,1)} %get-tuple-element.49), channel_id=1, source_target_pairs={{0,32},{8,40},{1,33},{9,41},{2,34},{10,42},{3,35},{11,43},{32,64},... | collective-permute-start | bytes 147464 | tf_op jit(solution)/shard_map/ppermute | solution.py:46
  114.5 1.7 %collective-permute-done.21.refs_5_ = bf16[64,384]{1,0:T(8,128)(2,1)S(1)} collective-permute-done((bf16[64,384]{1,0:T(8,128)(2,1)}, bf16[64,384]{1,0:T(8,128)(2,1)S(1)}, u32[]{:S(2)}, u32[]{:S(2)}) %collective-permute-start.21) | collective-permute-done | bytes 49184 | tf_op jit(solution)/shard_map/ppermute | solution.py:46
  117.0 1.9 %collective-permute-done.23.refs_7_ = bf16[64,384]{1,0:T(8,128)(2,1)S(1)} collective-permute-done((bf16[64,384]{1,0:T(8,128)(2,1)}, bf16[64,384]{1,0:T(8,128)(2,1)S(1)}, u32[]{:S(2)}, u32[]{:S(2)}) %collective-permute-start.23) | collective-permute-done | bytes 49184 | tf_op jit(solution)/shard_map/ppermute | solution.py:46
  119.5 1.9 %shard_map.77 = bf16[64,3072]{1,0:T(8,128)(2,1)} custom-call(s32[8]{0:T(128)} %fusion.3.at_ref, s32[1]{0:T(128)S(6)} %copy.8.level_ref, f32[16,3072]{1,0:T(8,128)} %gates_ref.1, bf16[64,384]{1,0:T(8,128)(2,1)} %get-tuple-element.43.refs_0_, bf16[64,384]{1,0:T(8,128)(2,1)} %copy-done.16, bf16[64,384]{1,0:T(8,128)(2,1)} %copy-done.17, ...), custom_call_target="tpu_custom_call" | custom-call | tf_op jit(solution)/shard_map/pallas_call | solution.py:359
  (92 shorter events, 13.2 us)
Async XLA Ops:
  2.9 8.9 %collective-permute-start = (bf16[208,384]{1,0:T(8,128)(2,1)}, bf16[208,384]{1,0:T(8,128)(2,1)S(1)}, u32[]{:S(2)}, u32[]{:S(2)}) collective-permute-start(bf16[208,384]{1,0:T(8,128)(2,1)} %get-tuple-element.29), channel_id=1, source_target_pairs={{0,8},{8,0},{1,9},{9,1},{2,10},{10,2},{3,11},{11,3},{32,40},{40,32... | collective-permute-start | bytes 479240 | tf_op jit(solution)/shard_map/ppermute | solution.py:46
  4.3 9.0 %collective-permute-start.1 = (bf16[208,384]{1,0:T(8,128)(2,1)}, bf16[208,384]{1,0:T(8,128)(2,1)S(1)}, u32[]{:S(2)}, u32[]{:S(2)}) collective-permute-start(bf16[208,384]{1,0:T(8,128)(2,1)} %get-tuple-element.30), channel_id=1, source_target_pairs={{0,32},{8,40},{1,33},{9,41},{2,34},{10,42},{3,35},{11,43},{32,64},... | collective-permute-start | bytes 479240 | tf_op jit(solution)/shard_map/ppermute | solution.py:46
  5.7 9.4 %collective-permute-start.2 = (bf16[208,384]{1,0:T(8,128)(2,1)}, bf16[208,384]{1,0:T(8,128)(2,1)S(1)}, u32[]{:S(2)}, u32[]{:S(2)}) collective-permute-start(bf16[208,384]{1,0:T(8,128)(2,1)} %get-tuple-element.31), channel_id=1, source_target_pairs={{0,40},{8,32},{1,41},{9,33},{2,42},{10,34},{3,43},{11,35},{32,72},... | collective-permute-start | bytes 479240 | tf_op jit(solution)/shard_map/ppermute | solution.py:46
  7.2 12.3 %collective-permute-start.3 = (bf16[208,384]{1,0:T(8,128)(2,1)}, bf16[208,384]{1,0:T(8,128)(2,1)S(1)}, u32[]{:S(2)}, u32[]{:S(2)}) collective-permute-start(bf16[208,384]{1,0:T(8,128)(2,1)} %get-tuple-element.32), channel_id=1, source_target_pairs={{0,64},{8,72},{1,65},{9,73},{2,66},{10,74},{3,67},{11,75},{32,96},... | collective-permute-start | bytes 479240 | tf_op jit(solution)/shard_map/ppermute | solution.py:46
  8.4 14.8 %collective-permute-start.4 = (bf16[208,384]{1,0:T(8,128)(2,1)}, bf16[208,384]{1,0:T(8,128)(2,1)S(1)}, u32[]{:S(2)}, u32[]{:S(2)}) collective-permute-start(bf16[208,384]{1,0:T(8,128)(2,1)} %get-tuple-element.33), channel_id=1, source_target_pairs={{0,72},{8,64},{1,73},{9,65},{2,74},{10,66},{3,75},{11,67},{32,104}... | collective-permute-start | bytes 479240 | tf_op jit(solution)/shard_map/ppermute | solution.py:46
  11.8 12.3 %copy-start.9 = (bf16[208,384]{1,0:T(8,128)(2,1)}, bf16[208,384]{1,0:T(8,128)(2,1)S(1)}, u32[]{:S(2)}) copy-start(bf16[208,384]{1,0:T(8,128)(2,1)S(1)} %collective-permute-done.refs_1_) | copy-start | bytes 479236
  11.8 11.4 %collective-permute-start.5 = (bf16[208,384]{1,0:T(8,128)(2,1)}, bf16[208,384]{1,0:T(8,128)(2,1)S(1)}, u32[]{:S(2)}, u32[]{:S(2)}) collective-permute-start(bf16[208,384]{1,0:T(8,128)(2,1)} %get-tuple-element.34), channel_id=1, source_target_pairs={{0,96},{8,104},{1,97},{9,105},{2,98},{10,106},{3,99},{11,107},{32,... | collective-permute-start | bytes 479240 | tf_op jit(solution)/shard_map/ppermute | solution.py:46
  13.3 10.8 %copy-start.10 = (bf16[208,384]{1,0:T(8,128)(2,1)}, bf16[208,384]{1,0:T(8,128)(2,1)S(1)}, u32[]{:S(2)}) copy-start(bf16[208,384]{1,0:T(8,128)(2,1)S(1)} %collective-permute-done.1.refs_2_) | copy-start | bytes 479236
  13.3 10.8 %collective-permute-start.6 = (bf16[208,384]{1,0:T(8,128)(2,1)}, bf16[208,384]{1,0:T(8,128)(2,1)S(1)}, u32[]{:S(2)}, u32[]{:S(2)}) collective-permute-start(bf16[208,384]{1,0:T(8,128)(2,1)} %get-tuple-element.35), channel_id=1, source_target_pairs={{0,104},{8,96},{1,105},{9,97},{2,106},{10,98},{3,107},{11,99},{32,... | collective-permute-start | bytes 479240 | tf_op jit(solution)/shard_map/ppermute | solution.py:46
  15.2 8.9 %copy-start.11 = (bf16[208,384]{1,0:T(8,128)(2,1)}, bf16[208,384]{1,0:T(8,128)(2,1)S(1)}, u32[]{:S(2)}) copy-start(bf16[208,384]{1,0:T(8,128)(2,1)S(1)} %collective-permute-done.2.refs_3_) | copy-start | bytes 479236
  27.3 10.7 %collective-permute-start.8 = (bf16[1536,128]{1,0:T(8,128)(2,1)}, bf16[1536,128]{1,0:T(8,128)(2,1)S(1)}, u32[]{:S(2)}, u32[]{:S(2)}) collective-permute-start(bf16[1536,128]{1,0:T(8,128)(2,1)} %get-tuple-element.37), channel_id=1, source_target_pairs={{0,4},{8,9},{1,5},{9,10},{2,6},{10,11},{3,7},{11,8},{32,36},{40,41... | collective-permute-start | bytes 1179656 | tf_op jit(solution)/shard_map/ppermute | solution.py:46
  29.0 5.5 %collective-permute-start.7 = (f32[8,128]{1,0:T(8,128)}, f32[8,128]{1,0:T(8,128)S(1)}, u32[]{:S(2)}, u32[]{:S(2)}) collective-permute-start(f32[8,128]{1,0:T(8,128)} %get-tuple-element.36), channel_id=1, source_target_pairs={{0,16},{8,24},{1,17},{9,25},{2,18},{10,26},{3,19},{11,27},{32,48},... | collective-permute-start | bytes 12296 | tf_op jit(solution)/shard_map/ppermute | solution.py:46
  31.7 6.1 %copy-start.23 = (f32[8,128]{1,0:T(8,128)S(1)}, f32[8,128]{1,0:T(8,128)}, u32[]{:S(2)}) copy-start(f32[8,128]{1,0:T(8,128)} %get-tuple-element.36) | copy-start | bytes 12292
  31.7 26.4 %collective-permute-start.11 = (bf16[3072,128]{1,0:T(8,128)(2,1)}, bf16[3072,128]{1,0:T(8,128)(2,1)S(1)}, u32[]{:S(2)}, u32[]{:S(2)}) collective-permute-start(bf16[3072,128]{1,0:T(8,128)(2,1)} %get-tuple-element.38), channel_id=1, source_target_pairs={{0,1},{8,12},{1,2},{9,13},{2,3},{10,14},{3,0},{11,15},{32,33},{40,... | collective-permute-start | bytes 2359304 | tf_op jit(solution)/shard_map/ppermute | solution.py:46
  32.0 26.3 %collective-permute-start.12 = (bf16[3072,128]{1,0:T(8,128)(2,1)}, bf16[3072,128]{1,0:T(8,128)(2,1)S(1)}, u32[]{:S(2)}, u32[]{:S(2)}) collective-permute-start(bf16[3072,128]{1,0:T(8,128)(2,1)} %get-tuple-element.38), channel_id=1, source_target_pairs={{0,2},{8,24},{1,3},{9,25},{2,0},{10,26},{3,1},{11,27},{32,34},{40,... | collective-permute-start | bytes 2359304 | tf_op jit(solution)/shard_map/ppermute | solution.py:46
  33.8 28.0 %collective-permute-start.13 = (bf16[3072,128]{1,0:T(8,128)(2,1)}, bf16[3072,128]{1,0:T(8,128)(2,1)S(1)}, u32[]{:S(2)}, u32[]{:S(2)}) collective-permute-start(bf16[3072,128]{1,0:T(8,128)(2,1)} %get-tuple-element.38), channel_id=1, source_target_pairs={{0,3},{8,28},{1,0},{9,29},{2,1},{10,30},{3,2},{11,31},{32,35},{40,... | collective-permute-start | bytes 2359304 | tf_op jit(solution)/shard_map/ppermute | solution.py:46
  34.5 13.2 %collective-permute-start.9 = (bf16[1536,128]{1,0:T(8,128)(2,1)}, bf16[1536,128]{1,0:T(8,128)(2,1)S(1)}, u32[]{:S(2)}, u32[]{:S(2)}) collective-permute-start(bf16[1536,128]{1,0:T(8,128)(2,1)} %get-tuple-element.37), channel_id=1, source_target_pairs={{0,16},{8,10},{1,17},{9,11},{2,18},{10,8},{3,19},{11,9},{32,48},{4... | collective-permute-start | bytes 1179656 | tf_op jit(solution)/shard_map/ppermute | solution.py:46
  38.0 23.7 %copy-start.6 = (bf16[1536,128]{1,0:T(8,128)(2,1)}, bf16[1536,128]{1,0:T(8,128)(2,1)S(1)}, u32[]{:S(2)}) copy-start(bf16[1536,128]{1,0:T(8,128)(2,1)S(1)} %collective-permute-done.8) | copy-start | bytes 1179652
  38.0 20.1 %collective-permute-start.10 = (bf16[1536,128]{1,0:T(8,128)(2,1)}, bf16[1536,128]{1,0:T(8,128)(2,1)S(1)}, u32[]{:S(2)}, u32[]{:S(2)}) collective-permute-start(bf16[1536,128]{1,0:T(8,128)(2,1)} %get-tuple-element.37), channel_id=1, source_target_pairs={{0,20},{8,11},{1,21},{9,8},{2,22},{10,9},{3,23},{11,10},{32,52},{4... | collective-permute-start | bytes 1179656 | tf_op jit(solution)/shard_map/ppermute | solution.py:46
  47.7 14.1 %copy-start.7 = (bf16[1536,128]{1,0:T(8,128)(2,1)}, bf16[1536,128]{1,0:T(8,128)(2,1)S(1)}, u32[]{:S(2)}) copy-start(bf16[1536,128]{1,0:T(8,128)(2,1)S(1)} %collective-permute-done.9) | copy-start | bytes 1179652
  84.5 12.0 %collective-permute-start.14 = (bf16[1632,128]{1,0:T(8,128)(2,1)}, bf16[1632,128]{1,0:T(8,128)(2,1)S(1)}, u32[]{:S(2)}, u32[]{:S(2)}) collective-permute-start(bf16[1632,128]{1,0:T(8,128)(2,1)} %get-tuple-element.40), channel_id=1, source_target_pairs={{0,20},{8,11},{1,21},{9,8},{2,22},{10,9},{3,23},{11,10},{32,52},{4... | collective-permute-start | bytes 1253384 | tf_op jit(solution)/shard_map/ppermute | solution.py:46
  86.7 9.8 %collective-permute-start.15 = (bf16[1632,128]{1,0:T(8,128)(2,1)}, bf16[1632,128]{1,0:T(8,128)(2,1)S(1)}, u32[]{:S(2)}, u32[]{:S(2)}) collective-permute-start(bf16[1632,128]{1,0:T(8,128)(2,1)} %get-tuple-element.41), channel_id=1, source_target_pairs={{0,16},{8,10},{1,17},{9,11},{2,18},{10,8},{3,19},{11,9},{32,48},{4... | collective-permute-start | bytes 1253384 | tf_op jit(solution)/shard_map/ppermute | solution.py:46
  88.0 12.1 %collective-permute-start.16 = (bf16[1632,128]{1,0:T(8,128)(2,1)}, bf16[1632,128]{1,0:T(8,128)(2,1)S(1)}, u32[]{:S(2)}, u32[]{:S(2)}) collective-permute-start(bf16[1632,128]{1,0:T(8,128)(2,1)} %get-tuple-element.42), channel_id=1, source_target_pairs={{0,4},{8,9},{1,5},{9,10},{2,6},{10,11},{3,7},{11,8},{32,36},{40,41... | collective-permute-start | bytes 1253384 | tf_op jit(solution)/shard_map/ppermute | solution.py:46
  103.7 8.6 %collective-permute-start.17 = (bf16[64,384]{1,0:T(8,128)(2,1)}, bf16[64,384]{1,0:T(8,128)(2,1)S(1)}, u32[]{:S(2)}, u32[]{:S(2)}) collective-permute-start(bf16[64,384]{1,0:T(8,128)(2,1)} %get-tuple-element.44), channel_id=1, source_target_pairs={{0,8},{8,0},{1,9},{9,1},{2,10},{10,2},{3,11},{11,3},{32,40},{40,32... | collective-permute-start | bytes 147464 | tf_op jit(solution)/shard_map/ppermute | solution.py:46
  105.8 7.9 %collective-permute-start.18 = (bf16[64,384]{1,0:T(8,128)(2,1)}, bf16[64,384]{1,0:T(8,128)(2,1)S(1)}, u32[]{:S(2)}, u32[]{:S(2)}) collective-permute-start(bf16[64,384]{1,0:T(8,128)(2,1)} %get-tuple-element.45), channel_id=1, source_target_pairs={{0,96},{8,104},{1,97},{9,105},{2,98},{10,106},{3,99},{11,107},{32,... | collective-permute-start | bytes 147464 | tf_op jit(solution)/shard_map/ppermute | solution.py:46
  108.8 5.7 %collective-permute-start.19 = (bf16[64,384]{1,0:T(8,128)(2,1)}, bf16[64,384]{1,0:T(8,128)(2,1)S(1)}, u32[]{:S(2)}, u32[]{:S(2)}) collective-permute-start(bf16[64,384]{1,0:T(8,128)(2,1)} %get-tuple-element.46), channel_id=1, source_target_pairs={{0,104},{8,96},{1,105},{9,97},{2,106},{10,98},{3,107},{11,99},{32,... | collective-permute-start | bytes 147464 | tf_op jit(solution)/shard_map/ppermute | solution.py:46
  108.9 5.6 %collective-permute-start.20 = (bf16[64,384]{1,0:T(8,128)(2,1)}, bf16[64,384]{1,0:T(8,128)(2,1)S(1)}, u32[]{:S(2)}, u32[]{:S(2)}) collective-permute-start(bf16[64,384]{1,0:T(8,128)(2,1)} %get-tuple-element.47), channel_id=1, source_target_pairs={{0,64},{8,72},{1,65},{9,73},{2,66},{10,74},{3,67},{11,75},{32,96},... | collective-permute-start | bytes 147464 | tf_op jit(solution)/shard_map/ppermute | solution.py:46
  110.2 6.0 %collective-permute-start.21 = (bf16[64,384]{1,0:T(8,128)(2,1)}, bf16[64,384]{1,0:T(8,128)(2,1)S(1)}, u32[]{:S(2)}, u32[]{:S(2)}) collective-permute-start(bf16[64,384]{1,0:T(8,128)(2,1)} %get-tuple-element.48), channel_id=1, source_target_pairs={{0,72},{8,64},{1,73},{9,65},{2,74},{10,66},{3,75},{11,67},{32,104}... | collective-permute-start | bytes 147464 | tf_op jit(solution)/shard_map/ppermute | solution.py:46
  112.3 6.6 %copy-start.16 = (bf16[64,384]{1,0:T(8,128)(2,1)}, bf16[64,384]{1,0:T(8,128)(2,1)S(1)}, u32[]{:S(2)}) copy-start(bf16[64,384]{1,0:T(8,128)(2,1)S(1)} %collective-permute-done.17.refs_1_) | copy-start | bytes 147460
  112.3 4.7 %collective-permute-start.22 = (bf16[64,384]{1,0:T(8,128)(2,1)}, bf16[64,384]{1,0:T(8,128)(2,1)S(1)}, u32[]{:S(2)}, u32[]{:S(2)}) collective-permute-start(bf16[64,384]{1,0:T(8,128)(2,1)} %get-tuple-element.49), channel_id=1, source_target_pairs={{0,32},{8,40},{1,33},{9,41},{2,34},{10,42},{3,35},{11,43},{32,64},... | collective-permute-start | bytes 147464 | tf_op jit(solution)/shard_map/ppermute | solution.py:46
  113.8 5.1 %copy-start.17 = (bf16[64,384]{1,0:T(8,128)(2,1)}, bf16[64,384]{1,0:T(8,128)(2,1)S(1)}, u32[]{:S(2)}) copy-start(bf16[64,384]{1,0:T(8,128)(2,1)S(1)} %collective-permute-done.18.refs_2_) | copy-start | bytes 147460
  113.8 5.1 %collective-permute-start.23 = (bf16[64,384]{1,0:T(8,128)(2,1)}, bf16[64,384]{1,0:T(8,128)(2,1)S(1)}, u32[]{:S(2)}, u32[]{:S(2)}) collective-permute-start(bf16[64,384]{1,0:T(8,128)(2,1)} %get-tuple-element.50), channel_id=1, source_target_pairs={{0,40},{8,32},{1,41},{9,33},{2,42},{10,34},{3,43},{11,35},{32,72},... | collective-permute-start | bytes 147464 | tf_op jit(solution)/shard_map/ppermute | solution.py:46
  (20 other events, 43.1 us)

commit v4 on v2

--- a/solution.py
+++ b/solution.py
@@ -97,7 +97,7 @@
     together = together_in(count)
     q_refs, kv_refs = refs[:RING], refs[RING : 2 * RING]
     out_refs = refs[2 * RING : 3 * RING]
-    q_all, k_all, v_all, o_all, v_turned, score_ref, lse_ref, sems = refs[3 * RING :]
+    q_all, k_all, v_all, o_all, v_turned, score_ref, lse_ref = refs[3 * RING :]
     factor = jnp.float32(HEAD_DIM ** (-0.5) * LOG2E)
 
     def rows_of(ref, h, i):
@@ -106,23 +106,11 @@
     limits = TILES * TILES
     q_place = [table_ref[limits + TILES + d] for d in range(RING)]
     k_place = [table_ref[limits + TILES + RING + d] for d in range(RING)]
-    copies = []
     for h in range(count):
         for d in range(RING):
-            for n, (source, target, place) in enumerate(
-                (
-                    (q_refs[d].at[h], q_all, q_place[d]),
-                    (kv_refs[d].at[h, 0], k_all, k_place[d]),
-                    (kv_refs[d].at[h, 1], v_all, k_place[d]),
-                )
-            ):
-                copy = pltpu.make_async_copy(
-                    source, target.at[h, :, place], sems.at[(h * RING + d) * 3 + n]
-                )
-                copy.start()
-                copies.append(copy)
-    for copy in copies:
-        copy.wait()
+            q_all[h, :, q_place[d]] = q_refs[d][h]
+            k_all[h, :, k_place[d]] = kv_refs[d][h, 0]
+            v_all[h, :, k_place[d]] = kv_refs[d][h, 1]
     for h in range(count):
         for i in range(TILES):
             rows = slice(i * TILE, (i + 1) * TILE)
@@ -225,14 +213,13 @@
     return call(
         functools.partial(attend_kernel, count),
         [shape(count * (SET + META), HEAD_DIM)] * RING,
-        [SMEM] + [pl.BlockSpec(memory_space=pl.ANY)] * (2 * RING),
+        [SMEM] + [VMEM] * (2 * RING),
         [pieces] * 3
         + [
             pltpu.VMEM((count, RING * SET, HEAD_DIM), jnp.bfloat16),
             pltpu.VMEM((count, HEAD_DIM, RING * SET), jnp.bfloat16),
             pltpu.VMEM((count * together_in(count), STEP * TILE, TILE), jnp.float32),
             pltpu.VMEM((count, 2, GROUP, HEAD_DIM), jnp.float32),
-            pltpu.SemaphoreType.DMA((count * RING * 3,)),
         ],
     )(table, *q, *kv)
 

time: 122 us -> 121 us (level)
  no operation moved by 1% of the time
where the time goes in v4:
time: 121 us
  waiting for transfers between devices  44.5 us (37%)
  starting transfers between devices  35.6 us (29%)
  Pallas kernels  31.1 us (26%)
  local copies, waits for them, and re-layouts  4.21 us (3%)
  other arithmetic  3.95 us (3%)
  between operations  1.51 us (1%)
    ppermute x24, waiting for transfers between devices, moved(): return lax.ppermute(array, BOTH, pairs)  44.5 us
    ppermute x24, starting transfers between devices, moved(): return lax.ppermute(array, BOTH, pairs)  35.6 us
    pallas_call x1, Pallas kernels, attend(): call(functools.partial(attend_kernel, count), [shape(count * (SET + META)...  21.3 us
    unnamed x56, local copies, waits for them, and re-layouts  4.12 us
    pallas_call x1, Pallas kernels, local(): call(combine_kernel, [shape(ROWS, WIDTH)] * GROUP, [SMEM] + [VMEM] * len(...  2.93 us
    pallas_call x1, Pallas kernels, local(): call(spread_kernel, shapes + [shape(GROUP, HEAD_DIM, jnp.float32)], [VMEM...  2.59 us
  transfers between devices with their start and end apart: 24, of which 13 were waited for; matrix products, arithmetic and copies ran while one was open for 3% of the time, Pallas kernels for 0%

profile of v4, /device:TPU:1, one launch (start us, length us, event | category | flops | bytes accessed | tf_op | source)
XLA Modules:
  0.0 120.8 jit_solution(6186098843665833866)
XLA Ops:
  0.5 2.4 %shard_map.73 = (bf16[208,384]{1,0:T(8,128)(2,1)}, bf16[208,384]{1,0:T(8,128)(2,1)}, bf16[208,384]{1,0:T(8,128)(2,1)}, bf16[208,384]{1,0:T(8,128)(2,1)}, bf16[20...) custom-call(s32[8]{0:T(128)} %fusion.3.at_ref, ...), custom_call_target="tpu_custom_call" | custom-call | tf_op jit(solution)/shard_map/pallas_call | solution.py:289
  2.9 1.4 %collective-permute-start = (bf16[208,384]{1,0:T(8,128)(2,1)}, bf16[208,384]{1,0:T(8,128)(2,1)S(1)}, u32[]{:S(2)}, u32[]{:S(2)}) collective-permute-start(bf16[208,384]{1,0:T(8,128)(2,1)} %get-tuple-element.29), channel_id=1, source_target_pairs={{0,8},{8,0},{1,9},{9,1},{2,10},{10,2},{3,11},{11,3},{32,40},{40,32... | collective-permute-start | bytes 479240 | tf_op jit(solution)/shard_map/ppermute | solution.py:46
  4.3 1.4 %collective-permute-start.1 = (bf16[208,384]{1,0:T(8,128)(2,1)}, bf16[208,384]{1,0:T(8,128)(2,1)S(1)}, u32[]{:S(2)}, u32[]{:S(2)}) collective-permute-start(bf16[208,384]{1,0:T(8,128)(2,1)} %get-tuple-element.30), channel_id=1, source_target_pairs={{0,32},{8,40},{1,33},{9,41},{2,34},{10,42},{3,35},{11,43},{32,64},... | collective-permute-start | bytes 479240 | tf_op jit(solution)/shard_map/ppermute | solution.py:46
  5.7 1.5 %collective-permute-start.2 = (bf16[208,384]{1,0:T(8,128)(2,1)}, bf16[208,384]{1,0:T(8,128)(2,1)S(1)}, u32[]{:S(2)}, u32[]{:S(2)}) collective-permute-start(bf16[208,384]{1,0:T(8,128)(2,1)} %get-tuple-element.31), channel_id=1, source_target_pairs={{0,40},{8,32},{1,41},{9,33},{2,42},{10,34},{3,43},{11,35},{32,72},... | collective-permute-start | bytes 479240 | tf_op jit(solution)/shard_map/ppermute | solution.py:46
  7.2 1.2 collective-permute-start.3
  8.4 2.2 %collective-permute-start.4 = (bf16[208,384]{1,0:T(8,128)(2,1)}, bf16[208,384]{1,0:T(8,128)(2,1)S(1)}, u32[]{:S(2)}, u32[]{:S(2)}) collective-permute-start(bf16[208,384]{1,0:T(8,128)(2,1)} %get-tuple-element.33), channel_id=1, source_target_pairs={{0,72},{8,64},{1,73},{9,65},{2,74},{10,66},{3,75},{11,67},{32,104}... | collective-permute-start | bytes 479240 | tf_op jit(solution)/shard_map/ppermute | solution.py:46
  11.8 1.4 %collective-permute-start.5 = (bf16[208,384]{1,0:T(8,128)(2,1)}, bf16[208,384]{1,0:T(8,128)(2,1)S(1)}, u32[]{:S(2)}, u32[]{:S(2)}) collective-permute-start(bf16[208,384]{1,0:T(8,128)(2,1)} %get-tuple-element.34), channel_id=1, source_target_pairs={{0,96},{8,104},{1,97},{9,105},{2,98},{10,106},{3,99},{11,107},{32,... | collective-permute-start | bytes 479240 | tf_op jit(solution)/shard_map/ppermute | solution.py:46
  13.3 1.0 collective-permute-start.6
  15.2 4.4 %collective-permute-done.3.refs_4_ = bf16[208,384]{1,0:T(8,128)(2,1)S(1)} collective-permute-done((bf16[208,384]{1,0:T(8,128)(2,1)}, bf16[208,384]{1,0:T(8,128)(2,1)S(1)}, u32[]{:S(2)}, u32[]{:S(2)}) %collective-permute-start.3) | collective-permute-done | bytes 159776 | tf_op jit(solution)/shard_map/ppermute | solution.py:46
  19.5 3.6 %collective-permute-done.4.refs_5_ = bf16[208,384]{1,0:T(8,128)(2,1)S(1)} collective-permute-done((bf16[208,384]{1,0:T(8,128)(2,1)}, bf16[208,384]{1,0:T(8,128)(2,1)S(1)}, u32[]{:S(2)}, u32[]{:S(2)}) %collective-permute-start.4) | collective-permute-done | bytes 159776 | tf_op jit(solution)/shard_map/ppermute | solution.py:46
  24.7 2.6 %shard_map.74 = (bf16[1536,128]{1,0:T(8,128)(2,1)}, bf16[3072,128]{1,0:T(8,128)(2,1)}, f32[8,128]{1,0:T(8,128)}) custom-call(bf16[208,384]{1,0:T(8,128)(2,1)} %get-tuple-element.28.refs_0_, bf16[208,384]{1,0:T(8,128)(2,1)} %copy-done.9, bf16[208,384]{1,0:T(8,128)(2,1)} %copy-done.10, bf16[208,384]{1,0:T(8,128)(2,1)} %copy-done.11, ...), custom_call_target="tpu_custom_call" | custom-call | tf_op jit(solution)/shard_map/pallas_call | solution.py:301
  27.3 1.6 %collective-permute-start.8 = (bf16[1536,128]{1,0:T(8,128)(2,1)}, bf16[1536,128]{1,0:T(8,128)(2,1)S(1)}, u32[]{:S(2)}, u32[]{:S(2)}) collective-permute-start(bf16[1536,128]{1,0:T(8,128)(2,1)} %get-tuple-element.37), channel_id=1, source_target_pairs={{0,4},{8,9},{1,5},{9,10},{2,6},{10,11},{3,7},{11,8},{32,36},{40,41... | collective-permute-start | bytes 1179656 | tf_op jit(solution)/shard_map/ppermute | solution.py:46
  29.0 2.7 %collective-permute-start.7 = (f32[8,128]{1,0:T(8,128)}, f32[8,128]{1,0:T(8,128)S(1)}, u32[]{:S(2)}, u32[]{:S(2)}) collective-permute-start(f32[8,128]{1,0:T(8,128)} %get-tuple-element.36), channel_id=1, source_target_pairs={{0,16},{8,24},{1,17},{9,25},{2,18},{10,26},{3,19},{11,27},{32,48},... | collective-permute-start | bytes 12296 | tf_op jit(solution)/shard_map/ppermute | solution.py:46
  32.0 1.7 %collective-permute-start.12 = (bf16[3072,128]{1,0:T(8,128)(2,1)}, bf16[3072,128]{1,0:T(8,128)(2,1)S(1)}, u32[]{:S(2)}, u32[]{:S(2)}) collective-permute-start(bf16[3072,128]{1,0:T(8,128)(2,1)} %get-tuple-element.38), channel_id=1, source_target_pairs={{0,2},{8,24},{1,3},{9,25},{2,0},{10,26},{3,1},{11,27},{32,34},{40,... | collective-permute-start | bytes 2359304 | tf_op jit(solution)/shard_map/ppermute | solution.py:46
  34.5 3.3 %collective-permute-start.9 = (bf16[1536,128]{1,0:T(8,128)(2,1)}, bf16[1536,128]{1,0:T(8,128)(2,1)S(1)}, u32[]{:S(2)}, u32[]{:S(2)}) collective-permute-start(bf16[1536,128]{1,0:T(8,128)(2,1)} %get-tuple-element.37), channel_id=1, source_target_pairs={{0,16},{8,10},{1,17},{9,11},{2,18},{10,8},{3,19},{11,9},{32,48},{4... | collective-permute-start | bytes 1179656 | tf_op jit(solution)/shard_map/ppermute | solution.py:46
  42.3 5.4 %collective-permute-done.9 = bf16[1536,128]{1,0:T(8,128)(2,1)S(1)} collective-permute-done((bf16[1536,128]{1,0:T(8,128)(2,1)}, bf16[1536,128]{1,0:T(8,128)(2,1)S(1)}, u32[]{:S(2)}, u32[]{:S(2)}) %collective-permute-start.9) | collective-permute-done | bytes 393248 | tf_op jit(solution)/shard_map/ppermute | solution.py:46
  47.7 10.4 %collective-permute-done.10 = bf16[1536,128]{1,0:T(8,128)(2,1)S(1)} collective-permute-done((bf16[1536,128]{1,0:T(8,128)(2,1)}, bf16[1536,128]{1,0:T(8,128)(2,1)S(1)}, u32[]{:S(2)}, u32[]{:S(2)}) %collective-permute-start.10) | collective-permute-done | bytes 393248 | tf_op jit(solution)/shard_map/ppermute | solution.py:46
  58.3 3.4 %collective-permute-done.13 = bf16[3072,128]{1,0:T(8,128)(2,1)S(1)} collective-permute-done((bf16[3072,128]{1,0:T(8,128)(2,1)}, bf16[3072,128]{1,0:T(8,128)(2,1)S(1)}, u32[]{:S(2)}, u32[]{:S(2)}) %collective-permute-start.13) | collective-permute-done | bytes 786464 | tf_op jit(solution)/shard_map/ppermute | solution.py:46
  62.6 21.3 %shard_map.75 = (bf16[1632,128]{1,0:T(8,128)(2,1)}, bf16[1632,128]{1,0:T(8,128)(2,1)}, bf16[1632,128]{1,0:T(8,128)(2,1)}, bf16[1632,128]{1,0:T(8,128)(2,1)}) custom-call(s32[280]{0:T(512)} %pad_add_fusion.table_ref, bf16[3,8,64,128]{3,2,1,0:T(8,128)(2,1)} %bitcast.20, bf16[3,8,64,128]{3,2,1,0:T(8,128)(2,1)} %bitcast.21, bf16[3,8,64,128]{3,2,1,0:T(8,128)(2,1)} %bitcast.22, ...), custom_call_target="tpu_custom_call" | custom-call | tf_op jit(solution)/shard_map/pallas_call | solution.py:213
  83.9 2.1 %collective-permute-start.14 = (bf16[1632,128]{1,0:T(8,128)(2,1)}, bf16[1632,128]{1,0:T(8,128)(2,1)S(1)}, u32[]{:S(2)}, u32[]{:S(2)}) collective-permute-start(bf16[1632,128]{1,0:T(8,128)(2,1)} %get-tuple-element.40), channel_id=1, source_target_pairs={{0,20},{8,11},{1,21},{9,8},{2,22},{10,9},{3,23},{11,10},{32,52},{4... | collective-permute-start | bytes 1253384 | tf_op jit(solution)/shard_map/ppermute | solution.py:46
  86.0 1.3 %collective-permute-start.15 = (bf16[1632,128]{1,0:T(8,128)(2,1)}, bf16[1632,128]{1,0:T(8,128)(2,1)S(1)}, u32[]{:S(2)}, u32[]{:S(2)}) collective-permute-start(bf16[1632,128]{1,0:T(8,128)(2,1)} %get-tuple-element.41), channel_id=1, source_target_pairs={{0,16},{8,10},{1,17},{9,11},{2,18},{10,8},{3,19},{11,9},{32,48},{4... | collective-permute-start | bytes 1253384 | tf_op jit(solution)/shard_map/ppermute | solution.py:46
  88.1 7.8 %collective-permute-done.14.refs_1_ = bf16[1632,128]{1,0:T(8,128)(2,1)S(1)} collective-permute-done((bf16[1632,128]{1,0:T(8,128)(2,1)}, bf16[1632,128]{1,0:T(8,128)(2,1)S(1)}, u32[]{:S(2)}, u32[]{:S(2)}) %collective-permute-start.14) | collective-permute-done | bytes 417824 | tf_op jit(solution)/shard_map/ppermute | solution.py:46
  95.9 3.6 %collective-permute-done.16.refs_3_ = bf16[1632,128]{1,0:T(8,128)(2,1)S(1)} collective-permute-done((bf16[1632,128]{1,0:T(8,128)(2,1)}, bf16[1632,128]{1,0:T(8,128)(2,1)S(1)}, u32[]{:S(2)}, u32[]{:S(2)}) %collective-permute-start.16) | collective-permute-done | bytes 417824 | tf_op jit(solution)/shard_map/ppermute | solution.py:46
  100.2 2.9 %shard_map.76 = (bf16[64,384]{1,0:T(8,128)(2,1)}, bf16[64,384]{1,0:T(8,128)(2,1)}, bf16[64,384]{1,0:T(8,128)(2,1)}, bf16[64,384]{1,0:T(8,128)(2,1)}, bf16[64,384...) custom-call(s32[280]{0:T(512)} %pad_add_fusion.table_ref, ...), custom_call_target="tpu_custom_call" | custom-call | tf_op jit(solution)/shard_map/pallas_call | solution.py:338
  103.1 2.1 %collective-permute-start.17 = (bf16[64,384]{1,0:T(8,128)(2,1)}, bf16[64,384]{1,0:T(8,128)(2,1)S(1)}, u32[]{:S(2)}, u32[]{:S(2)}) collective-permute-start(bf16[64,384]{1,0:T(8,128)(2,1)} %get-tuple-element.44), channel_id=1, source_target_pairs={{0,8},{8,0},{1,9},{9,1},{2,10},{10,2},{3,11},{11,3},{32,40},{40,32... | collective-permute-start | bytes 147464 | tf_op jit(solution)/shard_map/ppermute | solution.py:46
  105.2 2.9 %collective-permute-start.18 = (bf16[64,384]{1,0:T(8,128)(2,1)}, bf16[64,384]{1,0:T(8,128)(2,1)S(1)}, u32[]{:S(2)}, u32[]{:S(2)}) collective-permute-start(bf16[64,384]{1,0:T(8,128)(2,1)} %get-tuple-element.45), channel_id=1, source_target_pairs={{0,96},{8,104},{1,97},{9,105},{2,98},{10,106},{3,99},{11,107},{32,... | collective-permute-start | bytes 147464 | tf_op jit(solution)/shard_map/ppermute | solution.py:46
  108.3 1.3 %collective-permute-start.20 = (bf16[64,384]{1,0:T(8,128)(2,1)}, bf16[64,384]{1,0:T(8,128)(2,1)S(1)}, u32[]{:S(2)}, u32[]{:S(2)}) collective-permute-start(bf16[64,384]{1,0:T(8,128)(2,1)} %get-tuple-element.47), channel_id=1, source_target_pairs={{0,64},{8,72},{1,65},{9,73},{2,66},{10,74},{3,67},{11,75},{32,96},... | collective-permute-start | bytes 147464 | tf_op jit(solution)/shard_map/ppermute | solution.py:46
  109.6 2.1 %collective-permute-start.21 = (bf16[64,384]{1,0:T(8,128)(2,1)}, bf16[64,384]{1,0:T(8,128)(2,1)S(1)}, u32[]{:S(2)}, u32[]{:S(2)}) collective-permute-start(bf16[64,384]{1,0:T(8,128)(2,1)} %get-tuple-element.48), channel_id=1, source_target_pairs={{0,72},{8,64},{1,73},{9,65},{2,74},{10,66},{3,75},{11,67},{32,104}... | collective-permute-start | bytes 147464 | tf_op jit(solution)/shard_map/ppermute | solution.py:46
  111.7 1.5 %collective-permute-start.22 = (bf16[64,384]{1,0:T(8,128)(2,1)}, bf16[64,384]{1,0:T(8,128)(2,1)S(1)}, u32[]{:S(2)}, u32[]{:S(2)}) collective-permute-start(bf16[64,384]{1,0:T(8,128)(2,1)} %get-tuple-element.49), channel_id=1, source_target_pairs={{0,32},{8,40},{1,33},{9,41},{2,34},{10,42},{3,35},{11,43},{32,64},... | collective-permute-start | bytes 147464 | tf_op jit(solution)/shard_map/ppermute | solution.py:46
  113.9 1.7 %collective-permute-done.21.refs_5_ = bf16[64,384]{1,0:T(8,128)(2,1)S(1)} collective-permute-done((bf16[64,384]{1,0:T(8,128)(2,1)}, bf16[64,384]{1,0:T(8,128)(2,1)S(1)}, u32[]{:S(2)}, u32[]{:S(2)}) %collective-permute-start.21) | collective-permute-done | bytes 49184 | tf_op jit(solution)/shard_map/ppermute | solution.py:46
  116.4 1.9 %collective-permute-done.23.refs_7_ = bf16[64,384]{1,0:T(8,128)(2,1)S(1)} collective-permute-done((bf16[64,384]{1,0:T(8,128)(2,1)}, bf16[64,384]{1,0:T(8,128)(2,1)S(1)}, u32[]{:S(2)}, u32[]{:S(2)}) %collective-permute-start.23) | collective-permute-done | bytes 49184 | tf_op jit(solution)/shard_map/ppermute | solution.py:46
  118.9 1.9 %shard_map.77 = bf16[64,3072]{1,0:T(8,128)(2,1)} custom-call(s32[8]{0:T(128)} %fusion.3.at_ref, s32[1]{0:T(128)S(6)} %copy.8.level_ref, f32[16,3072]{1,0:T(8,128)} %gates_ref.1, bf16[64,384]{1,0:T(8,128)(2,1)} %get-tuple-element.43.refs_0_, bf16[64,384]{1,0:T(8,128)(2,1)} %copy-done.16, bf16[64,384]{1,0:T(8,128)(2,1)} %copy-done.17, ...), custom_call_target="tpu_custom_call" | custom-call | tf_op jit(solution)/shard_map/pallas_call | solution.py:344
  (92 shorter events, 13.2 us)
Async XLA Ops:
  2.9 8.9 %collective-permute-start = (bf16[208,384]{1,0:T(8,128)(2,1)}, bf16[208,384]{1,0:T(8,128)(2,1)S(1)}, u32[]{:S(2)}, u32[]{:S(2)}) collective-permute-start(bf16[208,384]{1,0:T(8,128)(2,1)} %get-tuple-element.29), channel_id=1, source_target_pairs={{0,8},{8,0},{1,9},{9,1},{2,10},{10,2},{3,11},{11,3},{32,40},{40,32... | collective-permute-start | bytes 479240 | tf_op jit(solution)/shard_map/ppermute | solution.py:46
  4.3 9.0 %collective-permute-start.1 = (bf16[208,384]{1,0:T(8,128)(2,1)}, bf16[208,384]{1,0:T(8,128)(2,1)S(1)}, u32[]{:S(2)}, u32[]{:S(2)}) collective-permute-start(bf16[208,384]{1,0:T(8,128)(2,1)} %get-tuple-element.30), channel_id=1, source_target_pairs={{0,32},{8,40},{1,33},{9,41},{2,34},{10,42},{3,35},{11,43},{32,64},... | collective-permute-start | bytes 479240 | tf_op jit(solution)/shard_map/ppermute | solution.py:46
  5.7 9.4 %collective-permute-start.2 = (bf16[208,384]{1,0:T(8,128)(2,1)}, bf16[208,384]{1,0:T(8,128)(2,1)S(1)}, u32[]{:S(2)}, u32[]{:S(2)}) collective-permute-start(bf16[208,384]{1,0:T(8,128)(2,1)} %get-tuple-element.31), channel_id=1, source_target_pairs={{0,40},{8,32},{1,41},{9,33},{2,42},{10,34},{3,43},{11,35},{32,72},... | collective-permute-start | bytes 479240 | tf_op jit(solution)/shard_map/ppermute | solution.py:46
  7.2 12.3 %collective-permute-start.3 = (bf16[208,384]{1,0:T(8,128)(2,1)}, bf16[208,384]{1,0:T(8,128)(2,1)S(1)}, u32[]{:S(2)}, u32[]{:S(2)}) collective-permute-start(bf16[208,384]{1,0:T(8,128)(2,1)} %get-tuple-element.32), channel_id=1, source_target_pairs={{0,64},{8,72},{1,65},{9,73},{2,66},{10,74},{3,67},{11,75},{32,96},... | collective-permute-start | bytes 479240 | tf_op jit(solution)/shard_map/ppermute | solution.py:46
  8.4 14.8 %collective-permute-start.4 = (bf16[208,384]{1,0:T(8,128)(2,1)}, bf16[208,384]{1,0:T(8,128)(2,1)S(1)}, u32[]{:S(2)}, u32[]{:S(2)}) collective-permute-start(bf16[208,384]{1,0:T(8,128)(2,1)} %get-tuple-element.33), channel_id=1, source_target_pairs={{0,72},{8,64},{1,73},{9,65},{2,74},{10,66},{3,75},{11,67},{32,104}... | collective-permute-start | bytes 479240 | tf_op jit(solution)/shard_map/ppermute | solution.py:46
  11.8 12.3 %copy-start.9 = (bf16[208,384]{1,0:T(8,128)(2,1)}, bf16[208,384]{1,0:T(8,128)(2,1)S(1)}, u32[]{:S(2)}) copy-start(bf16[208,384]{1,0:T(8,128)(2,1)S(1)} %collective-permute-done.refs_1_) | copy-start | bytes 479236
  11.8 11.4 %collective-permute-start.5 = (bf16[208,384]{1,0:T(8,128)(2,1)}, bf16[208,384]{1,0:T(8,128)(2,1)S(1)}, u32[]{:S(2)}, u32[]{:S(2)}) collective-permute-start(bf16[208,384]{1,0:T(8,128)(2,1)} %get-tuple-element.34), channel_id=1, source_target_pairs={{0,96},{8,104},{1,97},{9,105},{2,98},{10,106},{3,99},{11,107},{32,... | collective-permute-start | bytes 479240 | tf_op jit(solution)/shard_map/ppermute | solution.py:46
  13.3 10.8 %copy-start.10 = (bf16[208,384]{1,0:T(8,128)(2,1)}, bf16[208,384]{1,0:T(8,128)(2,1)S(1)}, u32[]{:S(2)}) copy-start(bf16[208,384]{1,0:T(8,128)(2,1)S(1)} %collective-permute-done.1.refs_2_) | copy-start | bytes 479236
  13.3 10.8 %collective-permute-start.6 = (bf16[208,384]{1,0:T(8,128)(2,1)}, bf16[208,384]{1,0:T(8,128)(2,1)S(1)}, u32[]{:S(2)}, u32[]{:S(2)}) collective-permute-start(bf16[208,384]{1,0:T(8,128)(2,1)} %get-tuple-element.35), channel_id=1, source_target_pairs={{0,104},{8,96},{1,105},{9,97},{2,106},{10,98},{3,107},{11,99},{32,... | collective-permute-start | bytes 479240 | tf_op jit(solution)/shard_map/ppermute | solution.py:46
  15.2 8.9 %copy-start.11 = (bf16[208,384]{1,0:T(8,128)(2,1)}, bf16[208,384]{1,0:T(8,128)(2,1)S(1)}, u32[]{:S(2)}) copy-start(bf16[208,384]{1,0:T(8,128)(2,1)S(1)} %collective-permute-done.2.refs_3_) | copy-start | bytes 479236
  27.3 10.7 %collective-permute-start.8 = (bf16[1536,128]{1,0:T(8,128)(2,1)}, bf16[1536,128]{1,0:T(8,128)(2,1)S(1)}, u32[]{:S(2)}, u32[]{:S(2)}) collective-permute-start(bf16[1536,128]{1,0:T(8,128)(2,1)} %get-tuple-element.37), channel_id=1, source_target_pairs={{0,4},{8,9},{1,5},{9,10},{2,6},{10,11},{3,7},{11,8},{32,36},{40,41... | collective-permute-start | bytes 1179656 | tf_op jit(solution)/shard_map/ppermute | solution.py:46
  29.0 5.5 %collective-permute-start.7 = (f32[8,128]{1,0:T(8,128)}, f32[8,128]{1,0:T(8,128)S(1)}, u32[]{:S(2)}, u32[]{:S(2)}) collective-permute-start(f32[8,128]{1,0:T(8,128)} %get-tuple-element.36), channel_id=1, source_target_pairs={{0,16},{8,24},{1,17},{9,25},{2,18},{10,26},{3,19},{11,27},{32,48},... | collective-permute-start | bytes 12296 | tf_op jit(solution)/shard_map/ppermute | solution.py:46
  31.7 6.1 %copy-start.23 = (f32[8,128]{1,0:T(8,128)S(1)}, f32[8,128]{1,0:T(8,128)}, u32[]{:S(2)}) copy-start(f32[8,128]{1,0:T(8,128)} %get-tuple-element.36) | copy-start | bytes 12292
  31.7 26.4 %collective-permute-start.11 = (bf16[3072,128]{1,0:T(8,128)(2,1)}, bf16[3072,128]{1,0:T(8,128)(2,1)S(1)}, u32[]{:S(2)}, u32[]{:S(2)}) collective-permute-start(bf16[3072,128]{1,0:T(8,128)(2,1)} %get-tuple-element.38), channel_id=1, source_target_pairs={{0,1},{8,12},{1,2},{9,13},{2,3},{10,14},{3,0},{11,15},{32,33},{40,... | collective-permute-start | bytes 2359304 | tf_op jit(solution)/shard_map/ppermute | solution.py:46
  32.0 26.3 %collective-permute-start.12 = (bf16[3072,128]{1,0:T(8,128)(2,1)}, bf16[3072,128]{1,0:T(8,128)(2,1)S(1)}, u32[]{:S(2)}, u32[]{:S(2)}) collective-permute-start(bf16[3072,128]{1,0:T(8,128)(2,1)} %get-tuple-element.38), channel_id=1, source_target_pairs={{0,2},{8,24},{1,3},{9,25},{2,0},{10,26},{3,1},{11,27},{32,34},{40,... | collective-permute-start | bytes 2359304 | tf_op jit(solution)/shard_map/ppermute | solution.py:46
  33.8 28.0 %collective-permute-start.13 = (bf16[3072,128]{1,0:T(8,128)(2,1)}, bf16[3072,128]{1,0:T(8,128)(2,1)S(1)}, u32[]{:S(2)}, u32[]{:S(2)}) collective-permute-start(bf16[3072,128]{1,0:T(8,128)(2,1)} %get-tuple-element.38), channel_id=1, source_target_pairs={{0,3},{8,28},{1,0},{9,29},{2,1},{10,30},{3,2},{11,31},{32,35},{40,... | collective-permute-start | bytes 2359304 | tf_op jit(solution)/shard_map/ppermute | solution.py:46
  34.5 13.2 %collective-permute-start.9 = (bf16[1536,128]{1,0:T(8,128)(2,1)}, bf16[1536,128]{1,0:T(8,128)(2,1)S(1)}, u32[]{:S(2)}, u32[]{:S(2)}) collective-permute-start(bf16[1536,128]{1,0:T(8,128)(2,1)} %get-tuple-element.37), channel_id=1, source_target_pairs={{0,16},{8,10},{1,17},{9,11},{2,18},{10,8},{3,19},{11,9},{32,48},{4... | collective-permute-start | bytes 1179656 | tf_op jit(solution)/shard_map/ppermute | solution.py:46
  38.0 23.7 %copy-start.6 = (bf16[1536,128]{1,0:T(8,128)(2,1)}, bf16[1536,128]{1,0:T(8,128)(2,1)S(1)}, u32[]{:S(2)}) copy-start(bf16[1536,128]{1,0:T(8,128)(2,1)S(1)} %collective-permute-done.8) | copy-start | bytes 1179652
  38.0 20.1 %collective-permute-start.10 = (bf16[1536,128]{1,0:T(8,128)(2,1)}, bf16[1536,128]{1,0:T(8,128)(2,1)S(1)}, u32[]{:S(2)}, u32[]{:S(2)}) collective-permute-start(bf16[1536,128]{1,0:T(8,128)(2,1)} %get-tuple-element.37), channel_id=1, source_target_pairs={{0,20},{8,11},{1,21},{9,8},{2,22},{10,9},{3,23},{11,10},{32,52},{4... | collective-permute-start | bytes 1179656 | tf_op jit(solution)/shard_map/ppermute | solution.py:46
  47.7 14.1 %copy-start.7 = (bf16[1536,128]{1,0:T(8,128)(2,1)}, bf16[1536,128]{1,0:T(8,128)(2,1)S(1)}, u32[]{:S(2)}) copy-start(bf16[1536,128]{1,0:T(8,128)(2,1)S(1)} %collective-permute-done.9) | copy-start | bytes 1179652
  83.9 11.9 %collective-permute-start.14 = (bf16[1632,128]{1,0:T(8,128)(2,1)}, bf16[1632,128]{1,0:T(8,128)(2,1)S(1)}, u32[]{:S(2)}, u32[]{:S(2)}) collective-permute-start(bf16[1632,128]{1,0:T(8,128)(2,1)} %get-tuple-element.40), channel_id=1, source_target_pairs={{0,20},{8,11},{1,21},{9,8},{2,22},{10,9},{3,23},{11,10},{32,52},{4... | collective-permute-start | bytes 1253384 | tf_op jit(solution)/shard_map/ppermute | solution.py:46
  86.0 9.8 %collective-permute-start.15 = (bf16[1632,128]{1,0:T(8,128)(2,1)}, bf16[1632,128]{1,0:T(8,128)(2,1)S(1)}, u32[]{:S(2)}, u32[]{:S(2)}) collective-permute-start(bf16[1632,128]{1,0:T(8,128)(2,1)} %get-tuple-element.41), channel_id=1, source_target_pairs={{0,16},{8,10},{1,17},{9,11},{2,18},{10,8},{3,19},{11,9},{32,48},{4... | collective-permute-start | bytes 1253384 | tf_op jit(solution)/shard_map/ppermute | solution.py:46
  87.3 12.1 %collective-permute-start.16 = (bf16[1632,128]{1,0:T(8,128)(2,1)}, bf16[1632,128]{1,0:T(8,128)(2,1)S(1)}, u32[]{:S(2)}, u32[]{:S(2)}) collective-permute-start(bf16[1632,128]{1,0:T(8,128)(2,1)} %get-tuple-element.42), channel_id=1, source_target_pairs={{0,4},{8,9},{1,5},{9,10},{2,6},{10,11},{3,7},{11,8},{32,36},{40,41... | collective-permute-start | bytes 1253384 | tf_op jit(solution)/shard_map/ppermute | solution.py:46
  103.1 8.6 %collective-permute-start.17 = (bf16[64,384]{1,0:T(8,128)(2,1)}, bf16[64,384]{1,0:T(8,128)(2,1)S(1)}, u32[]{:S(2)}, u32[]{:S(2)}) collective-permute-start(bf16[64,384]{1,0:T(8,128)(2,1)} %get-tuple-element.44), channel_id=1, source_target_pairs={{0,8},{8,0},{1,9},{9,1},{2,10},{10,2},{3,11},{11,3},{32,40},{40,32... | collective-permute-start | bytes 147464 | tf_op jit(solution)/shard_map/ppermute | solution.py:46
  105.2 7.9 %collective-permute-start.18 = (bf16[64,384]{1,0:T(8,128)(2,1)}, bf16[64,384]{1,0:T(8,128)(2,1)S(1)}, u32[]{:S(2)}, u32[]{:S(2)}) collective-permute-start(bf16[64,384]{1,0:T(8,128)(2,1)} %get-tuple-element.45), channel_id=1, source_target_pairs={{0,96},{8,104},{1,97},{9,105},{2,98},{10,106},{3,99},{11,107},{32,... | collective-permute-start | bytes 147464 | tf_op jit(solution)/shard_map/ppermute | solution.py:46
  108.1 5.7 %collective-permute-start.19 = (bf16[64,384]{1,0:T(8,128)(2,1)}, bf16[64,384]{1,0:T(8,128)(2,1)S(1)}, u32[]{:S(2)}, u32[]{:S(2)}) collective-permute-start(bf16[64,384]{1,0:T(8,128)(2,1)} %get-tuple-element.46), channel_id=1, source_target_pairs={{0,104},{8,96},{1,105},{9,97},{2,106},{10,98},{3,107},{11,99},{32,... | collective-permute-start | bytes 147464 | tf_op jit(solution)/shard_map/ppermute | solution.py:46
  108.3 5.6 %collective-permute-start.20 = (bf16[64,384]{1,0:T(8,128)(2,1)}, bf16[64,384]{1,0:T(8,128)(2,1)S(1)}, u32[]{:S(2)}, u32[]{:S(2)}) collective-permute-start(bf16[64,384]{1,0:T(8,128)(2,1)} %get-tuple-element.47), channel_id=1, source_target_pairs={{0,64},{8,72},{1,65},{9,73},{2,66},{10,74},{3,67},{11,75},{32,96},... | collective-permute-start | bytes 147464 | tf_op jit(solution)/shard_map/ppermute | solution.py:46
  109.6 6.0 %collective-permute-start.21 = (bf16[64,384]{1,0:T(8,128)(2,1)}, bf16[64,384]{1,0:T(8,128)(2,1)S(1)}, u32[]{:S(2)}, u32[]{:S(2)}) collective-permute-start(bf16[64,384]{1,0:T(8,128)(2,1)} %get-tuple-element.48), channel_id=1, source_target_pairs={{0,72},{8,64},{1,73},{9,65},{2,74},{10,66},{3,75},{11,67},{32,104}... | collective-permute-start | bytes 147464 | tf_op jit(solution)/shard_map/ppermute | solution.py:46
  111.7 6.6 %copy-start.16 = (bf16[64,384]{1,0:T(8,128)(2,1)}, bf16[64,384]{1,0:T(8,128)(2,1)S(1)}, u32[]{:S(2)}) copy-start(bf16[64,384]{1,0:T(8,128)(2,1)S(1)} %collective-permute-done.17.refs_1_) | copy-start | bytes 147460
  111.7 4.7 %collective-permute-start.22 = (bf16[64,384]{1,0:T(8,128)(2,1)}, bf16[64,384]{1,0:T(8,128)(2,1)S(1)}, u32[]{:S(2)}, u32[]{:S(2)}) collective-permute-start(bf16[64,384]{1,0:T(8,128)(2,1)} %get-tuple-element.49), channel_id=1, source_target_pairs={{0,32},{8,40},{1,33},{9,41},{2,34},{10,42},{3,35},{11,43},{32,64},... | collective-permute-start | bytes 147464 | tf_op jit(solution)/shard_map/ppermute | solution.py:46
  113.1 5.1 %copy-start.17 = (bf16[64,384]{1,0:T(8,128)(2,1)}, bf16[64,384]{1,0:T(8,128)(2,1)S(1)}, u32[]{:S(2)}) copy-start(bf16[64,384]{1,0:T(8,128)(2,1)S(1)} %collective-permute-done.18.refs_2_) | copy-start | bytes 147460
  113.1 5.1 %collective-permute-start.23 = (bf16[64,384]{1,0:T(8,128)(2,1)}, bf16[64,384]{1,0:T(8,128)(2,1)S(1)}, u32[]{:S(2)}, u32[]{:S(2)}) collective-permute-start(bf16[64,384]{1,0:T(8,128)(2,1)} %get-tuple-element.50), channel_id=1, source_target_pairs={{0,40},{8,32},{1,41},{9,33},{2,42},{10,34},{3,43},{11,35},{32,72},... | collective-permute-start | bytes 147464 | tf_op jit(solution)/shard_map/ppermute | solution.py:46
  (20 other events, 43.1 us)
